TPU v7x, 256 devices: a whole 4x4x8 slice. The times are simulated.
256 devices in a mesh: rows: 16 (over z_lo, y, core), tm: 16 (over x, z_hi).
Axes of the slice: x: 4, y: 4, z: 8 (z_hi: 4, z_lo: 2; z = z_hi * 2 + z_lo), core: 2. Of those that a mesh axis runs over, the one named last changes fastest.
Arguments:
- residual: float32 [64, 1024, 512], P('tm', 'rows'), may hold values from -45 to 45
- cycle_weight: float32 [64, 1024, 512], P('tm', 'rows'), may hold values from -0.75 to 0.75
- cycle_offsets: int32 [64, 2], replicated, may hold values from -6 to 6, as said below
Outputs:
- new_weight: float32 [64, 1024, 512], P('tm', 'rows')
- error: float32 [64, 1024, 512], P('tm', 'rows')
Inputs may be any that keep to these rules, and one draw needn't show every extreme that they name: `cycle_offsets`: each row is a distinct (row, column) offset; together the rows are the 64 pixels (dy, dx) with 17 <= dy*dy + dx*dx <= 36, in an order drawn from the seed.
All inputs are finite; a program needn't handle non-finite values.
Results may differ from a plain program's by a relative error of at most 0.0003.
Values sent between devices are 32-bit elements; how exact they have to be, the bound alone decides.
A program may use at most 64 MiB of HBM per device.

v0:
```python
import jax
import jax.numpy as jnp
import numpy as np
from jax import lax
from jax.sharding import PartitionSpec as P


def with_halo(cells, sides, width):
    for axis, dim in sides:
        count = lax.axis_size(axis)
        ends = count - 1
        head = lax.slice_in_dim(cells, 0, width, axis=dim)
        tail = lax.slice_in_dim(cells, cells.shape[dim] - width, cells.shape[dim], axis=dim)
        cells = jnp.concatenate(
            [
                lax.ppermute(tail, axis, [(i, (i + 1) % count) for i in range(ends)]),
                cells,
                lax.ppermute(head, axis, [((i + 1) % count, i) for i in range(ends)]),
            ],
            axis=dim,
        )
    return cells


def cycle_points():
    points = []
    for row_off in range(-6, 7):
        for col_off in range(-6, 7):
            radius = row_off * row_off + col_off * col_off
            if radius >= 17 and radius <= 36:
                points.append((row_off, col_off))
    return points


def matching(cycle_offsets, points):
    table_rows = jnp.asarray(np.array([p[0] for p in points], dtype=np.int32))
    table_cols = jnp.asarray(np.array([p[1] for p in points], dtype=np.int32))
    same = (table_rows[:, None] == cycle_offsets[None, :, 0]) & (
        table_cols[:, None] == cycle_offsets[None, :, 1]
    )
    return same.astype(jnp.float32)


def reorder(selector, weights):
    return jnp.einsum("jk,kyx->jyx", selector, weights, precision=lax.Precision.HIGHEST)


def window_of(padded, point, height, width):
    return padded[:, 6 + point[0] : 6 + point[0] + height, 6 + point[1] : 6 + point[1] + width]


def cycle_passes(padded, centre, ordered_weight, points, height, width):
    background = jnp.zeros(centre.shape, jnp.float32)
    for index, point in enumerate(points):
        background = background + ordered_weight[index][None] * window_of(
            padded, point, height, width
        )
    error_part = centre - background
    grads = jnp.stack(
        [jnp.sum(error_part * window_of(padded, point, height, width), axis=0) for point in points]
    )
    squares = jnp.sum(padded * padded, axis=0)
    energy_sum = jnp.zeros((height, width), jnp.float32)
    for point in points:
        energy_sum = (
            energy_sum
            + squares[6 + point[0] : 6 + point[0] + height, 6 + point[1] : 6 + point[1] + width]
        )
    return (error_part, grads, energy_sum)


def on_device(residual, cycle_weight, cycle_offsets):
    frames_dev, rows_dev, cols = residual.shape
    cycle = cycle_offsets.shape[0]
    tm_count = lax.axis_size("tm")
    frames_all = frames_dev * tm_count
    points = cycle_points()
    selector = matching(cycle_offsets, points)
    extended = with_halo(residual, (("rows", 1),), 6)
    padded = jnp.pad(extended, ((0, 0), (0, 0), (6, 6)))
    columns = selector
    ordered_weight = reorder(columns, lax.all_gather(cycle_weight, "tm", axis=0, tiled=True))
    error, ordered_grad, local_energy = cycle_passes(
        padded, residual, ordered_weight, points, rows_dev, cols
    )
    columns = selector
    gradient = lax.psum_scatter(
        jnp.einsum("jk,jyx->kyx", columns, ordered_grad, precision=lax.Precision.HIGHEST),
        "tm",
        scatter_dimension=0,
        tiled=True,
    )
    energy = lax.psum(local_energy, "tm") / (cycle * frames_all) + 1e-06
    new_weight = cycle_weight + gradient / (frames_all * energy)[None]
    return (new_weight, error)


def solution(mesh):
    in_specs = (P("tm", "rows", None), P("tm", "rows", None), P())
    out_specs = (P("tm", "rows", None), P("tm", "rows", None))
    return jax.shard_map(
        on_device, mesh=mesh, in_specs=in_specs, out_specs=out_specs, check_vma=False
    )
```

profile of v0, /device:TPU:1, one launch (start us, length us, event | category | flops | bytes accessed | tf_op | source)
XLA Modules:
  0.0 429.3 jit_solution(9261241765014633690)
XLA Ops:
  8.0 0.9 fusion.19
  8.9 4.6 %collective-permute-start = (f32[4,6,512]{2,1,0:T(8,128)S(1)}, f32[4,6,512]{2,1,0:T(8,128)S(1)}, u32[]{:S(2)}, u32[]{:S(2)}) collective-permute-start(f32[4,6,512]{2,1,0:T(8,128)S(1)} %get-tuple-element.143), channel_id=1, source_target_pairs={{0,16},{16,32},{32,48},{48,64},{64,80},{80,96},{96,112},{112,128},... | collective-permute-start | bytes 147464 | tf_op jit(solution)/shard_map/ppermute | solution.py:16
  13.4 1.9 collective-permute-start.1
  15.4 0.8 slice_bitcast_fusion.1
  16.1 1.1 constant_dynamic-update-slice_fusion.1
  17.2 1.8 collective-permute-done.1
  19.0 1.4 multiply_reduce_fusion
  20.4 2.8 slice_add_fusion
  23.8 93.9 %all-gather.2.cloned.1.call-done = f32[64,64,512]{2,1,0:T(8,128)} async-done(((f32[4,64,512]{2,1,0:T(8,128)}), f32[64,64,512]{2,1,0:T(8,128)}) %all-gather.2.cloned.1.call-update) | async-done | bytes 8388624 | tf_op jit(solution)/shard_map/all_gather | solution.py:82
  117.7 13.4 %fusion = f32[64,64,512]{2,0,1:T(8,128)S(1)} fusion(f32[64,64,512]{2,1,0:T(8,128)} %all-gather.2.cloned.1.call-done, s32[64]{0:T(128)S(1)} %copy-done.4, s32[64]{0:T(128)S(1)} %copy-done.3, s32[64]{0:T(128)S(1)} %get-tuple-element.146, s32[64]{0:T(128)S(1)} %get-tuple-element.145), kind=kOutput, calls=%fused_computation | convolution fusion | flops 1610625024 | bytes 16778240 | tf_op jit(solution)/shard_map/jk,kyx->jyx/dot_general | solution.py:45
  131.2 2.0 fusion.17
  133.1 2.3 fusion.15
  135.4 2.4 fusion.16
  139.5 9.4 %multiply_reduce_fusion.2 = (f32[64,512]{1,0:T(8,128)S(1)}, f32[64,512]{1,0:T(8,128)S(1)}, f32[64,512]{1,0:T(8,128)S(1)}, f32[64,512]{1,0:T(8,128)S(1)}, f32[64,...) fusion(f32[4,76,524]{2,1,0:T(8,128)S(1)} %get-tuple-element.142, ...), kind=kLoop, calls=%fused_computation.14 | loop fusion | flops 21168128 | bytes 44351488 | tf_op jit(solution)/shard_map/reduce_sum | solution.py:60
  149.0 2.5 multiply_reduce_fusion.39
  151.5 2.4 multiply_reduce_fusion.21
  155.0 0.7 stack.214
  158.6 0.7 stack.219
  159.4 0.7 stack.220
  165.3 0.7 stack.228
  168.3 0.7 stack.232
  169.0 0.7 stack.233
  173.4 0.9 multiply_reduce_fusion.1
  179.4 0.8 stack.248
  183.8 1.0 stack.255
  186.3 28.8 %stack.259 = f32[64,64,512]{2,0,1:T(8,128)} concatenate(f32[1,64,512]{2,0,1:T(1,128)S(1)} %stack.195, f32[1,64,512]{2,0,1:T(1,128)S(1)} %stack.196, f32[1,64,512]{2,0,1:T(1,128)S(1)} %stack.197, f32[1,64,512]{2,0,1:T(1,128)S(1)} %stack.198, f32[1,64,512]{2,0,1:T(1,128)S(1)} %stack.199, f32[1,64,512]{2,0,1:T(1,128)S(1)} %stack.200, f32[1,64,512]{2,0,1:T(1,128)S(1)} %stack.201, ...), dimensions={0} | concatenate | bytes 16777216 | tf_op jit(solution)/shard_map/stack | solution.py:59
  215.0 8.1 %fusion.5 = f32[64,64,512]{2,0,1:T(8,128)S(1)} fusion(f32[64,64,512]{2,0,1:T(8,128)} %stack.259, s32[64]{0:T(128)S(1)} %copy-done.4, s32[64]{0:T(128)S(1)} %copy-done.3, s32[64]{0:T(128)S(1)} %get-tuple-element.146, s32[64]{0:T(128)S(1)} %get-tuple-element.145), kind=kOutput, calls=%fused_computation.207 | convolution fusion | flops 1610625024 | bytes 16778240 | tf_op jit(solution)/shard_map/jk,jyx->kyx/dot_general | solution.py:88
  223.2 8.1 %copy.13 = f32[64,64,512]{2,1,0:T(8,128)} copy(f32[64,64,512]{2,0,1:T(8,128)S(1)} %fusion.5) | data formatting | bytes 16777216 | tf_op jit(solution)/shard_map/jk,jyx->kyx/dot_general | solution.py:88
  231.3 57.9 %all-reduce.3.cloned.1.call-done = f32[64,512]{1,0:T(8,128)} async-done(((f32[64,512]{1,0:T(8,128)}), f32[64,512]{1,0:T(8,128)}) %all-reduce.3.cloned.1.call-update) | async-done | bytes 131088 | tf_op jit(solution)/shard_map/psum | solution.py:93
  289.2 0.9 add_multiply_fusion
  290.1 130.5 %reduce-scatter.2.cloned.1.call-done = f32[4,64,512]{2,1,0:T(8,128)} async-done(((f32[64,64,512]{2,1,0:T(8,128)}), f32[4,64,512]{2,1,0:T(8,128)}) %reduce-scatter.2.cloned.1.call-update) | async-done | bytes 524304 | tf_op jit(solution)/shard_map/reduce_scatter | solution.py:87
  420.6 1.9 divide_add_fusion
  (107 shorter events, 27.9 us)
Async XLA Ops:
  7.2 110.6 %copy-start.3 = (s32[64]{0:T(128)S(1)}, s32[64]{0:T(128)}, u32[]{:S(2)}) copy-start(s32[64]{0:T(128)} %constant.15.clone) | copy-start | bytes 772
  7.2 110.6 %copy-start.4 = (s32[64]{0:T(128)S(1)}, s32[64]{0:T(128)}, u32[]{:S(2)}) copy-start(s32[64]{0:T(128)} %constant.16.clone) | copy-start | bytes 772
  7.2 110.5 %all-gather.2.cloned.1.call-start = ((), (), s32[]{:S(2)}) async-start(), calls=%async_computation.1 | async-start | bytes 8912896 | tf_op jit(solution)/shard_map/all_gather | solution.py:82
  7.9 281.3 %all-reduce.3.cloned.1.call-start = ((), (), s32[]{:S(2)}) async-start(), calls=%async_computation.3 | async-start | bytes 262144 | tf_op jit(solution)/shard_map/psum | solution.py:93
  8.9 8.4 %collective-permute-start = (f32[4,6,512]{2,1,0:T(8,128)S(1)}, f32[4,6,512]{2,1,0:T(8,128)S(1)}, u32[]{:S(2)}, u32[]{:S(2)}) collective-permute-start(f32[4,6,512]{2,1,0:T(8,128)S(1)} %get-tuple-element.143), channel_id=1, source_target_pairs={{0,16},{16,32},{32,48},{48,64},{64,80},{80,96},{96,112},{112,128},... | collective-permute-start | bytes 147464 | tf_op jit(solution)/shard_map/ppermute | solution.py:16
  13.4 5.6 %collective-permute-start.1 = (f32[4,6,512]{2,1,0:T(8,128)S(1)}, f32[4,6,512]{2,1,0:T(8,128)S(1)}, u32[]{:S(2)}, u32[]{:S(2)}) collective-permute-start(f32[4,6,512]{2,1,0:T(8,128)S(1)} %get-tuple-element.144), channel_id=1, source_target_pairs={{16,0},{32,16},{48,32},{64,48},{80,64},{96,80},{112,96},{128,112},... | collective-permute-start | bytes 147464 | tf_op jit(solution)/shard_map/ppermute | solution.py:18
  23.3 397.3 %reduce-scatter.2.cloned.1.call-start = ((), (), s32[]{:S(2)}) async-start(), calls=%async_computation.2 | async-start | bytes 8912896 | tf_op jit(solution)/shard_map/reduce_scatter | solution.py:87
  138.5 1.0 copy-start
  149.0 24.5 %copy-start.1 = (f32[4,64,512]{2,1,0:T(8,128)}, f32[4,64,512]{2,1,0:T(8,128)S(1)}, u32[]{:S(2)}) copy-start(f32[4,64,512]{2,1,0:T(8,128)S(1)} %get-tuple-element.76) | copy-start | bytes 1572868
  231.3 189.4 %copy-start.2 = (f32[4,64,512]{2,1,0:T(8,128)S(1)}, f32[4,64,512]{2,1,0:T(8,128)}, u32[]{:S(2)}) copy-start(f32[4,64,512]{2,1,0:T(8,128)} %param.6) | copy-start | bytes 1572868
Sparse Core Ops, SparseCore 0:
  10.4 107.2 all-gather.1
  120.3 168.8 all-reduce.2
  292.9 127.6 reduce-scatter.1
where the time goes:
time: 434 us; the launch traced here: 429 us
  waiting for transfers between devices  285 us (66%)
  local copies, waits for them, and re-layouts  79 us (18%)
  other arithmetic  22.3 us (5%)
  matrix products  21.6 us (5%)
  between operations  14.6 us (3%)
  starting transfers between devices  7.09 us (2%)
    reduce_scatter x1, waiting for transfers between devices, on_device(): lax.psum_scatter(jnp.einsum('jk,jyx->kyx', columns, ordered_grad, precisi...  130 us
    all_gather x1, waiting for transfers between devices, on_device(): lax.all_gather(cycle_weight, 'tm', axis=0, tiled=True)  93.9 us
    another operation x65, local copies, waits for them, and re-layouts, cycle_passes(): jnp.stack([jnp.sum(error_part * window_of(padded, point, height, width),...  60.1 us
    psum x1, waiting for transfers between devices, on_device(): energy = lax.psum(local_energy, 'tm') / (cycle * frames_all) + 1e-06  57.9 us
    reduce_sum x4, other arithmetic, cycle_passes(): jnp.sum(error_part * window_of(padded, point, height, width), axis=0)  15.2 us
    dot_general x1, matrix products, reorder(): jnp.einsum('jk,kyx->jyx', selector, weights, precision=lax.Precision.HIGH...  13.4 us
  transfers between devices with their start and end apart: 5, of which 4 were waited for; matrix products, arithmetic and copies ran while one was open for 28% of the time, Pallas kernels for 0%

commit v1 on v0

v1 whole, which is shorter than its diff:
```python
import jax
import jax.numpy as jnp
import numpy as np
from jax import lax
from jax.sharding import PartitionSpec as P

HALO = 6


def with_halo(cells, sides, width):
    for axis, dim in sides:
        count = lax.axis_size(axis)
        ends = count - 1
        head = lax.slice_in_dim(cells, 0, width, axis=dim)
        tail = lax.slice_in_dim(cells, cells.shape[dim] - width, cells.shape[dim], axis=dim)
        cells = jnp.concatenate(
            [
                lax.ppermute(tail, axis, [(i, (i + 1) % count) for i in range(ends)]),
                cells,
                lax.ppermute(head, axis, [((i + 1) % count, i) for i in range(ends)]),
            ],
            axis=dim,
        )
    return cells


def cycle_points():
    points = []
    for row_off in range(-6, 7):
        for col_off in range(-6, 7):
            radius = row_off * row_off + col_off * col_off
            if radius >= 17 and radius <= 36:
                points.append((row_off, col_off))
    return points


def matching(cycle_offsets, points):
    table_rows = jnp.asarray(np.array([p[0] for p in points], dtype=np.int32))
    table_cols = jnp.asarray(np.array([p[1] for p in points], dtype=np.int32))
    same = (table_rows[:, None] == cycle_offsets[None, :, 0]) & (
        table_cols[:, None] == cycle_offsets[None, :, 1]
    )
    return same.astype(jnp.int32)


def tile_split(count, rows, cols):
    b = 1
    while b * 2 <= count and cols // (b * 2) >= 128 and count % (b * 2) == 0:
        b *= 2
    a = count // b
    return a, b


def tile_compute(rt, wt, order, place, points, h, w, frames_all, cycle):
    ordered_weight = jnp.take(wt, order, axis=0)
    background = jnp.zeros((rt.shape[0], h, w), jnp.float32)
    for index, (dy, dx) in enumerate(points):
        window = rt[:, HALO + dy : HALO + dy + h, HALO + dx : HALO + dx + w]
        background = background + ordered_weight[index][None] * window
    error = rt[:, HALO : HALO + h, HALO : HALO + w] - background
    grads = jnp.stack(
        [
            jnp.sum(error * rt[:, HALO + dy : HALO + dy + h, HALO + dx : HALO + dx + w], axis=0)
            for dy, dx in points
        ]
    )
    squares = jnp.sum(rt * rt, axis=0)
    energy_sum = jnp.zeros((h, w), jnp.float32)
    for dy, dx in points:
        energy_sum = energy_sum + squares[HALO + dy : HALO + dy + h, HALO + dx : HALO + dx + w]
    gradient = jnp.take(grads, place, axis=0)
    energy = energy_sum / (cycle * frames_all) + 1e-06
    new_weight = wt + gradient / (frames_all * energy)[None]
    return error, new_weight


def on_device(residual, cycle_weight, cycle_offsets):
    frames_dev, rows_dev, cols = residual.shape
    k_dev = cycle_weight.shape[0]
    cycle = cycle_offsets.shape[0]
    n = lax.axis_size("tm")
    frames_all = frames_dev * n
    points = cycle_points()
    same = matching(cycle_offsets, points)
    ks = jnp.arange(cycle, dtype=jnp.int32)
    order = jnp.sum(same * ks[None, :], axis=1)
    place = jnp.sum(same * ks[:, None], axis=0)

    a, b = tile_split(n, rows_dev, cols)
    h, w = rows_dev // a, cols // b

    extended = with_halo(residual, (("rows", 1),), HALO)
    padded = jnp.pad(extended, ((0, 0), (0, 0), (HALO, HALO)))
    res_tiles = jnp.stack(
        [
            padded[:, i * h : i * h + h + 2 * HALO, j * w : j * w + w + 2 * HALO]
            for i in range(a)
            for j in range(b)
        ]
    )
    rt = lax.all_to_all(res_tiles, "tm", 0, 0, tiled=True)
    rt = rt.reshape(frames_all, h + 2 * HALO, w + 2 * HALO)

    w_tiles = cycle_weight.reshape(k_dev, a, h, b, w).transpose(1, 3, 0, 2, 4)
    w_tiles = w_tiles.reshape(n, k_dev, h, w)
    wt = lax.all_to_all(w_tiles, "tm", 0, 0, tiled=True).reshape(cycle, h, w)

    error_t, new_t = tile_compute(rt, wt, order, place, points, h, w, frames_all, cycle)

    def back(x, lead):
        x = lax.all_to_all(x.reshape(n, lead, h, w), "tm", 0, 0, tiled=True)
        x = x.reshape(a, b, lead, h, w).transpose(2, 0, 3, 1, 4)
        return x.reshape(lead, rows_dev, cols)

    return back(new_t, k_dev), back(error_t, frames_dev)


def solution(mesh):
    in_specs = (P("tm", "rows", None), P("tm", "rows", None), P())
    out_specs = (P("tm", "rows", None), P("tm", "rows", None))
    return jax.shard_map(
        on_device, mesh=mesh, in_specs=in_specs, out_specs=out_specs, check_vma=False
    )
```

time: 434 us -> 161 us (0.37)
  waiting for transfers between devices: 285 us -> 80.5 us
  local copies, waits for them, and re-layouts: 79 us -> 25.5 us
  starting transfers between devices: 7.09 us -> 31.6 us
  matrix products: 21.6 us -> 0 us
  between operations: 14.6 us -> 1.47 us
    reduce_scatter x1 -> x0, waiting for transfers between devices: 130 us -> none  [on_device(): lax.psum_scatter(jnp.einsum('jk,jyx->kyx', columns, ordered_grad, precisi...]
    all_gather x1 -> x0, waiting for transfers between devices: 93.9 us -> none  [on_device(): lax.all_gather(cycle_weight, 'tm', axis=0, tiled=True)]
    all_to_all x0 -> x4, waiting for transfers between devices: none -> 80.5 us  [the longest x1 47.4 us: on_device(): rt = lax.all_to_all(res_tiles, 'tm', 0, 0, tiled=True)]
    another operation x65 -> x2, local copies, waits for them, and re-layouts: 60.1 us -> 0.66 us  [the longest x1 0.66 us: on_device(): jnp.stack([padded[:, i * h:i * h + h + 2 * HALO, j * w:j * w + w + 2 * HA...]
    psum x1 -> x0, waiting for transfers between devices: 57.9 us -> none  [on_device(): energy = lax.psum(local_energy, 'tm') / (cycle * frames_all) + 1e-06]
    all_to_all x0 -> x4, starting transfers between devices: none -> 25.1 us  [the longest x1 10.7 us: on_device(): wt = lax.all_to_all(w_tiles, 'tm', 0, 0, tiled=True).reshape(cycle, h, w)]
    dot_general x2 -> x0, matrix products: 21.6 us -> none  [the longest x1 13.4 us: reorder(): jnp.einsum('jk,kyx->jyx', selector, weights, precision=lax.Precision.HIGH...]
    unnamed x43 -> x93, local copies, waits for them, and re-layouts: 1.89 us -> 14 us
  transfers between devices with their start and end apart: 5 -> 6, of which waited for: 4 -> 4; matrix products, arithmetic and copies ran while one was open for 28% -> 11% of each run, Pallas kernels for 0% -> 0%
where the time goes in v1:
time: 161 us; the launch traced here: 160 us
  waiting for transfers between devices  80.5 us (50%)
  starting transfers between devices  31.6 us (20%)
  local copies, waits for them, and re-layouts  25.5 us (16%)
  other arithmetic  21.1 us (13%)
    all_to_all x1, waiting for transfers between devices, on_device(): rt = lax.all_to_all(res_tiles, 'tm', 0, 0, tiled=True)  47.4 us
    all_to_all x2, waiting for transfers between devices, back(): x = lax.all_to_all(x.reshape(n, lead, h, w), 'tm', 0, 0, tiled=True)  30.4 us
    reduce_sum x4, other arithmetic, tile_compute(): jnp.sum(error * rt[:, HALO + dy:HALO + dy + h, HALO + dx:HALO + dx + w],...  18.7 us
    unnamed x93, local copies, waits for them, and re-layouts  14 us
    all_to_all x1, starting transfers between devices, on_device(): wt = lax.all_to_all(w_tiles, 'tm', 0, 0, tiled=True).reshape(cycle, h, w)  10.7 us
    all_to_all x2, starting transfers between devices, back(): x = lax.all_to_all(x.reshape(n, lead, h, w), 'tm', 0, 0, tiled=True)  7.98 us
    all_to_all x1, starting transfers between devices, on_device(): rt = lax.all_to_all(res_tiles, 'tm', 0, 0, tiled=True)  6.35 us
    ppermute x1, starting transfers between devices, with_halo(): lax.ppermute(tail, axis, [(i, (i + 1) % count) for i in range(ends)])  4.58 us
  transfers between devices with their start and end apart: 6, of which 4 were waited for; matrix products, arithmetic and copies ran while one was open for 11% of the time, Pallas kernels for 0%

profile of v1, /device:TPU:1, one launch (start us, length us, event | category | flops | bytes accessed | tf_op | source)
XLA Modules:
  0.0 160.1 jit_solution(8437036179205812696)
XLA Ops:
  0.6 1.4 copy.37
  2.1 4.6 %collective-permute-start = (f32[4,6,512]{2,0,1:T(4,128)S(1)}, f32[4,6,512]{2,0,1:T(4,128)S(1)}, u32[]{:S(2)}, u32[]{:S(2)}) collective-permute-start(f32[4,6,512]{2,0,1:T(4,128)S(1)} %get-tuple-element.136), channel_id=1, source_target_pairs={{0,16},{16,32},{32,48},{48,64},{64,80},{80,96},{96,112},{112,128},... | collective-permute-start | bytes 147464 | tf_op jit(solution)/shard_map/ppermute | solution.py:18
  6.7 1.9 %collective-permute-start.1 = (f32[4,6,512]{2,0,1:T(4,128)S(1)}, f32[4,6,512]{2,0,1:T(4,128)S(1)}, u32[]{:S(2)}, u32[]{:S(2)}) collective-permute-start(f32[4,6,512]{2,0,1:T(4,128)S(1)} %get-tuple-element.137), channel_id=1, source_target_pairs={{16,0},{32,16},{48,32},{64,48},{80,64},{96,80},{112,96},{128,112},... | collective-permute-start | bytes 147464 | tf_op jit(solution)/shard_map/ppermute | solution.py:20
  8.6 1.2 reshape.44
  9.8 0.9 copy.36
  10.7 10.7 %all-to-all-start = ((f32[16,4,16,128]{3,2,1,0:T(8,128)}), f32[16,4,16,128]{3,2,1,0:T(8,128)S(1)}, u32[]{:S(2)}, u32[]{:S(2)}) async-start(f32[16,4,16,128]{3,2,1,0:T(8,128)} %bitcast.1), calls=%async_computation | async-start | bytes 1048576 | tf_op jit(solution)/shard_map/all_to_all | solution.py:106
  23.2 0.8 constant_dynamic-update-slice_fusion.18
  24.0 0.8 constant_dynamic-update-slice_fusion.17
  26.1 0.8 constant_dynamic-update-slice_fusion.14
  26.9 0.8 constant_dynamic-update-slice_fusion.13
  28.9 0.8 constant_dynamic-update-slice_fusion.10
  29.7 0.8 constant_dynamic-update-slice_fusion.9
  31.8 0.8 constant_dynamic-update-slice_fusion.6
  32.6 0.8 constant_dynamic-update-slice_fusion.5
  34.0 2.7 %all-to-all-done = f32[16,4,16,128]{3,2,1,0:T(8,128)S(1)} async-done(((f32[16,4,16,128]{3,2,1,0:T(8,128)}), f32[16,4,16,128]{3,2,1,0:T(8,128)S(1)}, u32[]{:S(2)}, u32[]{:S(2)}) %all-to-all-start) | async-done | bytes 524320 | tf_op jit(solution)/shard_map/all_to_all | solution.py:106
  36.7 6.3 %all-to-all-start.1 = ((f32[16,4,28,140]{3,1,2,0:T(4,128)}), f32[16,4,28,140]{3,1,2,0:T(4,128)S(1)}, u32[]{:S(2)}, u32[]{:S(2)}) async-start(f32[16,4,28,140]{3,1,2,0:T(4,128)} %constant_dynamic-update-slice_fusion.4), calls=%async_computation.1 | async-start | bytes 3670016 | tf_op jit(solution)/shard_map/all_to_all | solution.py:101
  44.0 47.4 %all-to-all-done.1 = f32[16,4,28,140]{3,1,2,0:T(4,128)S(1)} async-done(((f32[16,4,28,140]{3,1,2,0:T(4,128)}), f32[16,4,28,140]{3,1,2,0:T(4,128)S(1)}, u32[]{:S(2)}, u32[]{:S(2)}) %all-to-all-start.1) | async-done | bytes 1003552 | tf_op jit(solution)/shard_map/all_to_all | solution.py:101
  91.4 1.3 copy-done
  92.6 1.7 %copy.46 = f32[16,4,28,140]{3,1,0,2:T(4,128)} copy(f32[16,4,28,140]{3,1,2,0:T(4,128)S(1)} %all-to-all-done.1) | data formatting | bytes 2007040 | tf_op jit(solution)/shard_map/all_to_all | solution.py:101
  94.4 1.9 %reshape.47 = f32[64,28,140]{2,0,1:T(8,128)S(1)} reshape(f32[16,4,28,140]{3,1,0,2:T(4,128)} %copy.46) | data formatting | bytes 2007040 | tf_op jit(solution)/shard_map/reshape | solution.py:102
  96.3 10.7 %multiply_reduce_fusion.1 = (f32[16,128]{1,0:T(8,128)S(1)}, f32[16,128]{1,0:T(8,128)S(1)}, f32[16,128]{1,0:T(8,128)S(1)}, f32[16,128]{1,0:T(8,128)S(1)}, f32[16,...) fusion(f32[64,28,140]{2,0,1:T(8,128)S(1)} %reshape.47, ...), kind=kLoop, calls=%fused_computation.11 | loop fusion | flops 21458944 | bytes 35274752 | tf_op jit(solution)/shard_map/reduce_sum | solution.py:63
  107.0 2.8 %multiply_reduce_fusion.19 = (f32[16,128]{1,0:T(8,128)S(1)}, f32[16,128]{1,0:T(8,128)S(1)}, f32[16,128]{1,0:T(8,128)S(1)}, f32[16,128]{1,0:T(8,128)S(1)}, f32[16...) fusion(f32[64,16,128]{2,0,1:T(8,128)S(1)} %get-tuple-element.69, ...), kind=kLoop, calls=%fused_computation.29 | loop fusion | flops 4681728 | bytes 10108928 | tf_op jit(solution)/shard_map/reduce_sum | solution.py:63
  109.9 3.4 %multiply_reduce_fusion.37 = (f32[16,128]{1,0:T(8,128)S(1)}, f32[16,128]{1,0:T(8,128)S(1)}, f32[16,128]{1,0:T(8,128)S(1)}, f32[16,128]{1,0:T(8,128)S(1)}, f32[16...) fusion(f32[64,16,128]{2,0,1:T(8,128)S(1)} %get-tuple-element.69, ...), kind=kLoop, calls=%fused_computation.47 | loop fusion | flops 4681728 | bytes 10108928 | tf_op jit(solution)/shard_map/reduce_sum | solution.py:63
  113.3 1.7 %multiply_reduce_fusion.55 = (f32[16,128]{1,0:T(8,128)S(1)}, f32[16,128]{1,0:T(8,128)S(1)}, f32[16,128]{1,0:T(8,128)S(1)}, f32[16,128]{1,0:T(8,128)S(1)}, f32[16...) fusion(f32[64,16,128]{2,0,1:T(8,128)S(1)} %get-tuple-element.69, ...), kind=kLoop, calls=%fused_computation.65 | loop fusion | flops 2600960 | bytes 5849088 | tf_op jit(solution)/shard_map/reduce_sum | solution.py:63
  117.0 0.9 fusion.1
  117.9 3.6 %all-to-all-start.2 = ((f32[16,4,16,128]{3,2,1,0:T(8,128)}), f32[16,4,16,128]{3,2,1,0:T(8,128)S(1)}, u32[]{:S(2)}, u32[]{:S(2)}) async-start(f32[16,4,16,128]{3,2,1,0:T(8,128)} %bitcast.149), calls=%async_computation.2 | async-start | bytes 1048576 | tf_op jit(solution)/shard_map/all_to_all | solution.py:111
  121.5 1.1 copy.48
  122.6 15.8 %all-to-all-done.2 = f32[16,4,16,128]{3,2,1,0:T(8,128)S(1)} async-done(((f32[16,4,16,128]{3,2,1,0:T(8,128)}), f32[16,4,16,128]{3,2,1,0:T(8,128)S(1)}, u32[]{:S(2)}, u32[]{:S(2)}) %all-to-all-start.2) | async-done | bytes 524320 | tf_op jit(solution)/shard_map/all_to_all | solution.py:111
  138.4 4.4 %all-to-all-start.3 = ((f32[16,4,16,128]{3,2,1,0:T(8,128)}), f32[16,4,16,128]{3,2,1,0:T(8,128)S(1)}, u32[]{:S(2)}, u32[]{:S(2)}) async-start(f32[16,4,16,128]{3,2,1,0:T(8,128)} %copy.48), calls=%async_computation.3 | async-start | bytes 1048576 | tf_op jit(solution)/shard_map/all_to_all | solution.py:111
  143.1 1.0 reshape.50
  144.1 14.6 %all-to-all-done.3 = f32[16,4,16,128]{3,2,1,0:T(8,128)S(1)} async-done(((f32[16,4,16,128]{3,2,1,0:T(8,128)}), f32[16,4,16,128]{3,2,1,0:T(8,128)S(1)}, u32[]{:S(2)}, u32[]{:S(2)}) %all-to-all-start.3) | async-done | bytes 524320 | tf_op jit(solution)/shard_map/all_to_all | solution.py:111
  159.1 1.0 reshape.53
  (109 shorter events, 9.4 us)
Async XLA Ops:
  2.0 19.4 %copy-start.3 = (s32[64,2]{0,1:T(2,128)S(1)}, s32[64,2]{0,1:T(2,128)}, u32[]{:S(2)}) copy-start(s32[64,2]{0,1:T(2,128)} %param.9) | copy-start | bytes 1540
  2.0 19.4 %copy-start.4 = (s32[64]{0:T(128)S(1)}, s32[64]{0:T(128)}, u32[]{:S(2)}) copy-start(s32[64]{0:T(128)} %constant.28.clone) | copy-start | bytes 772
  2.0 19.4 %copy-start.5 = (s32[64]{0:T(128)S(1)}, s32[64]{0:T(128)}, u32[]{:S(2)}) copy-start(s32[64]{0:T(128)} %constant.29.clone) | copy-start | bytes 772
  2.1 19.6 %collective-permute-start = (f32[4,6,512]{2,0,1:T(4,128)S(1)}, f32[4,6,512]{2,0,1:T(4,128)S(1)}, u32[]{:S(2)}, u32[]{:S(2)}) collective-permute-start(f32[4,6,512]{2,0,1:T(4,128)S(1)} %get-tuple-element.136), channel_id=1, source_target_pairs={{0,16},{16,32},{32,48},{48,64},{64,80},{80,96},{96,112},{112,128},... | collective-permute-start | bytes 147464 | tf_op jit(solution)/shard_map/ppermute | solution.py:18
  6.7 15.0 %collective-permute-start.1 = (f32[4,6,512]{2,0,1:T(4,128)S(1)}, f32[4,6,512]{2,0,1:T(4,128)S(1)}, u32[]{:S(2)}, u32[]{:S(2)}) collective-permute-start(f32[4,6,512]{2,0,1:T(4,128)S(1)} %get-tuple-element.137), channel_id=1, source_target_pairs={{16,0},{32,16},{48,32},{64,48},{80,64},{96,80},{112,96},{128,112},... | collective-permute-start | bytes 147464 | tf_op jit(solution)/shard_map/ppermute | solution.py:20
  9.8 13.0 %copy-start.2 = (f32[4,64,512]{2,1,0:T(8,128)S(1)}, f32[4,64,512]{2,1,0:T(8,128)}, u32[]{:S(2)}) copy-start(f32[4,64,512]{2,1,0:T(8,128)} %param.7) | copy-start | bytes 1572868
  10.7 26.0 %all-to-all-start = ((f32[16,4,16,128]{3,2,1,0:T(8,128)}), f32[16,4,16,128]{3,2,1,0:T(8,128)S(1)}, u32[]{:S(2)}, u32[]{:S(2)}) async-start(f32[16,4,16,128]{3,2,1,0:T(8,128)} %bitcast.1), calls=%async_computation | async-start | bytes 1048576 | tf_op jit(solution)/shard_map/all_to_all | solution.py:106
  36.7 54.7 %all-to-all-start.1 = ((f32[16,4,28,140]{3,1,2,0:T(4,128)}), f32[16,4,28,140]{3,1,2,0:T(4,128)S(1)}, u32[]{:S(2)}, u32[]{:S(2)}) async-start(f32[16,4,28,140]{3,1,2,0:T(4,128)} %constant_dynamic-update-slice_fusion.4), calls=%async_computation.1 | async-start | bytes 3670016 | tf_op jit(solution)/shard_map/all_to_all | solution.py:101
  91.4 1.3 copy-start
  113.3 1.7 %copy-start.1 = (f32[16,4,28,140]{3,1,2,0:T(4,128)S(1)}, f32[16,4,28,140]{3,1,2,0:T(4,128)}, u32[]{:S(2)}) copy-start(f32[16,4,28,140]{3,1,2,0:T(4,128)} %copy-done) | copy-start | bytes 3010564
  117.9 20.4 %all-to-all-start.2 = ((f32[16,4,16,128]{3,2,1,0:T(8,128)}), f32[16,4,16,128]{3,2,1,0:T(8,128)S(1)}, u32[]{:S(2)}, u32[]{:S(2)}) async-start(f32[16,4,16,128]{3,2,1,0:T(8,128)} %bitcast.149), calls=%async_computation.2 | async-start | bytes 1048576 | tf_op jit(solution)/shard_map/all_to_all | solution.py:111
  138.4 20.4 %all-to-all-start.3 = ((f32[16,4,16,128]{3,2,1,0:T(8,128)}), f32[16,4,16,128]{3,2,1,0:T(8,128)S(1)}, u32[]{:S(2)}, u32[]{:S(2)}) async-start(f32[16,4,16,128]{3,2,1,0:T(8,128)} %copy.48), calls=%async_computation.3 | async-start | bytes 1048576 | tf_op jit(solution)/shard_map/all_to_all | solution.py:111

commit v2 on v1

--- a/solution.py
+++ b/solution.py
@@ -91,28 +91,39 @@
 
     extended = with_halo(residual, (("rows", 1),), HALO)
     padded = jnp.pad(extended, ((0, 0), (0, 0), (HALO, HALO)))
+    hh, ww = h + 2 * HALO, w + 2 * HALO
     res_tiles = jnp.stack(
         [
-            padded[:, i * h : i * h + h + 2 * HALO, j * w : j * w + w + 2 * HALO]
+            padded[:, i * h : i * h + hh, j * w : j * w + ww]
             for i in range(a)
             for j in range(b)
         ]
     )
-    rt = lax.all_to_all(res_tiles, "tm", 0, 0, tiled=True)
-    rt = rt.reshape(frames_all, h + 2 * HALO, w + 2 * HALO)
-
     w_tiles = cycle_weight.reshape(k_dev, a, h, b, w).transpose(1, 3, 0, 2, 4)
-    w_tiles = w_tiles.reshape(n, k_dev, h, w)
-    wt = lax.all_to_all(w_tiles, "tm", 0, 0, tiled=True).reshape(cycle, h, w)
+    res_len = frames_dev * hh * ww
+    w_len = k_dev * h * w
+    chunk = -(-(res_len + w_len) // 1024) * 1024
+    send = jnp.concatenate(
+        [
+            res_tiles.reshape(n, res_len),
+            w_tiles.reshape(n, w_len),
+            jnp.zeros((n, chunk - res_len - w_len), jnp.float32),
+        ],
+        axis=1,
+    ).reshape(n, chunk // 128, 128)
+    got = lax.all_to_all(send, "tm", 0, 0, tiled=True).reshape(n, chunk)
+    rt = got[:, :res_len].reshape(frames_all, hh, ww)
+    wt = got[:, res_len : res_len + w_len].reshape(cycle, h, w)
 
     error_t, new_t = tile_compute(rt, wt, order, place, points, h, w, frames_all, cycle)
 
-    def back(x, lead):
-        x = lax.all_to_all(x.reshape(n, lead, h, w), "tm", 0, 0, tiled=True)
-        x = x.reshape(a, b, lead, h, w).transpose(2, 0, 3, 1, 4)
-        return x.reshape(lead, rows_dev, cols)
-
-    return back(new_t, k_dev), back(error_t, frames_dev)
+    out = jnp.concatenate(
+        [new_t.reshape(n, k_dev, h, w), error_t.reshape(n, frames_dev, h, w)], axis=1
+    )
+    out = lax.all_to_all(out, "tm", 0, 0, tiled=True)
+    out = out.reshape(a, b, k_dev + frames_dev, h, w).transpose(2, 0, 3, 1, 4)
+    out = out.reshape(k_dev + frames_dev, rows_dev, cols)
+    return out[:k_dev], out[k_dev:]
 
 
 def solution(mesh):

time: 161 us -> 135 us (0.84)
  the two profiles are of different devices: /device:TPU:1 before, /device:TPU:40 now
where the time goes in v2:
time: 135 us; the launch traced here: 134 us
  waiting for transfers between devices  41.3 us (31%)
  blocking collectives  32.3 us (24%)
  local copies, waits for them, and re-layouts  23.7 us (18%)
  other arithmetic  19.4 us (14%)
  starting transfers between devices  15.8 us (12%)
  between operations  1.7 us (1%)
    all_to_all x1, waiting for transfers between devices, on_device(): got = lax.all_to_all(send, 'tm', 0, 0, tiled=True).reshape(n, chunk)  41.3 us
    all_to_all x1, blocking collectives, on_device(): out = lax.all_to_all(out, 'tm', 0, 0, tiled=True)  32.3 us
    reduce_sum x4, other arithmetic, tile_compute(): jnp.sum(error * rt[:, HALO + dy:HALO + dy + h, HALO + dx:HALO + dx + w],...  16.7 us
    all_to_all x1, starting transfers between devices, on_device(): got = lax.all_to_all(send, 'tm', 0, 0, tiled=True).reshape(n, chunk)  10.3 us
    another operation x17, local copies, waits for them, and re-layouts, on_device(): jnp.stack([padded[:, i * h:i * h + hh, j * w:j * w + ww] for i in range(a...  7.68 us
    unnamed x104, local copies, waits for them, and re-layouts  4.24 us
    ppermute x1, starting transfers between devices, with_halo(): lax.ppermute(head, axis, [((i + 1) % count, i) for i in range(ends)])  3.64 us
    slice x5, local copies, waits for them, and re-layouts, on_device(): return (out[:k_dev], out[k_dev:])  2.78 us
  transfers between devices with their start and end apart: 3, of which 1 were waited for; matrix products, arithmetic and copies ran while one was open for 3% of the time, Pallas kernels for 0%

profile of v2, /device:TPU:40, one launch (start us, length us, event | category | flops | bytes accessed | tf_op | source)
XLA Modules:
  0.0 134.3 jit_solution(218210855446813105)
XLA Ops:
  0.6 0.9 fusion.9
  1.5 1.9 %collective-permute-start = (f32[4,6,512]{2,1,0:T(8,128)S(1)}, f32[4,6,512]{2,1,0:T(8,128)S(1)}, u32[]{:S(2)}, u32[]{:S(2)}) collective-permute-start(f32[4,6,512]{2,1,0:T(8,128)S(1)} %get-tuple-element.154), channel_id=1, source_target_pairs={{0,16},{16,32},{32,48},{48,64},{64,80},{80,96},{96,112},{112,128},... | collective-permute-start | bytes 147464 | tf_op jit(solution)/shard_map/ppermute | solution.py:18
  3.4 3.6 %collective-permute-start.1 = (f32[4,6,512]{2,1,0:T(8,128)S(1)}, f32[4,6,512]{2,1,0:T(8,128)S(1)}, u32[]{:S(2)}, u32[]{:S(2)}) collective-permute-start(f32[4,6,512]{2,1,0:T(8,128)S(1)} %get-tuple-element.155), channel_id=1, source_target_pairs={{16,0},{32,16},{48,32},{64,48},{80,64},{96,80},{112,96},{128,112},... | collective-permute-start | bytes 147464 | tf_op jit(solution)/shard_map/ppermute | solution.py:20
  7.1 1.1 constant_dynamic-update-slice_fusion.1
  8.2 1.3 reshape.77
  10.2 0.3 select_maximum_fusion
  12.1 0.3 fusion.8
  13.5 4.9 %stack.262 = f32[16,15680]{1,0:T(8,128)S(1)} concatenate(f32[1,15680]{1,0:T(1,128)S(1)} %stack.246, f32[1,15680]{1,0:T(1,128)S(1)} %stack.247, f32[1,15680]{1,0:T(1,128)S(1)} %stack.248, f32[1,15680]{1,0:T(1,128)S(1)} %stack.249, f32[1,15680]{1,0:T(1,128)S(1)} %stack.250, f32[1,15680]{1,0:T(1,128)S(1)} %stack.251, f32[1,15680]{1,0:T(1,128)S(1)} %stack.252, ...), dimensions={0} | concatenate | bytes 2007040 | tf_op jit(solution)/shard_map/stack | solution.py:95
  18.4 0.6 concatenate.21
  19.0 1.5 %copy.14 = f32[2,8,192,128]{3,2,1,0:T(8,128)} copy(f32[2,8,192,128]{3,1,2,0:T(8,128)S(1)} %bitcast.278) | data formatting | bytes 3145728
  20.4 10.3 %all-to-all-start = ((f32[16,192,128]{2,1,0:T(8,128)}), f32[16,192,128]{2,1,0:T(8,128)S(1)}, u32[]{:S(2)}, u32[]{:S(2)}) async-start(f32[16,192,128]{2,1,0:T(8,128)} %bitcast.138), calls=%async_computation | async-start | bytes 3145728 | tf_op jit(solution)/shard_map/all_to_all | solution.py:114
  30.9 0.6 pad_clamp_fusion
  31.5 0.6 compare_and_fusion.1
  32.1 41.3 %all-to-all-done = f32[16,192,128]{2,1,0:T(8,128)S(1)} async-done(((f32[16,192,128]{2,1,0:T(8,128)}), f32[16,192,128]{2,1,0:T(8,128)S(1)}, u32[]{:S(2)}, u32[]{:S(2)}) %all-to-all-start) | async-done | bytes 1572896 | tf_op jit(solution)/shard_map/all_to_all | solution.py:114
  73.4 0.9 copy.18
  74.6 1.0 slice.971
  75.7 0.6 gather_fusion
  76.5 0.7 slice_bitcast_fusion.63
  77.2 2.5 %reshape.82 = f32[64,28,140]{2,1,0:T(8,128)S(1)} reshape(f32[16,15680]{1,0:T(8,128)} %slice.971) | data formatting | bytes 2007040 | tf_op jit(solution)/shard_map/reshape | solution.py:115
  79.8 0.2 multiply_reduce_fusion
  80.1 0.3 copy-done.1
  80.6 10.1 %multiply_reduce_fusion.1 = (f32[16,128]{1,0:T(8,128)S(1)}, f32[16,128]{1,0:T(8,128)S(1)}, f32[16,128]{1,0:T(8,128)S(1)}, f32[16,128]{1,0:T(8,128)S(1)}, f32[16,...) fusion(f32[64,28,140]{2,1,0:T(8,128)S(1)} %reshape.82, ...), kind=kLoop, calls=%fused_computation.14 | loop fusion | flops 21458944 | bytes 35274752 | tf_op jit(solution)/shard_map/reduce_sum | solution.py:63
  90.7 1.4 %multiply_reduce_fusion.55 = (f32[16,128]{1,0:T(8,128)S(1)}, f32[16,128]{1,0:T(8,128)S(1)}, f32[16,128]{1,0:T(8,128)S(1)}, f32[16,128]{1,0:T(8,128)S(1)}, f32[16...) fusion(f32[64,16,128]{2,1,0:T(8,128)S(1)} %get-tuple-element.69, ...), kind=kLoop, calls=%fused_computation.68 | loop fusion | flops 2600960 | bytes 5849088 | tf_op jit(solution)/shard_map/reduce_sum | solution.py:63
  92.1 2.6 %multiply_reduce_fusion.37 = (f32[16,128]{1,0:T(8,128)S(1)}, f32[16,128]{1,0:T(8,128)S(1)}, f32[16,128]{1,0:T(8,128)S(1)}, f32[16,128]{1,0:T(8,128)S(1)}, f32[16...) fusion(f32[64,16,128]{2,1,0:T(8,128)S(1)} %get-tuple-element.69, ...), kind=kLoop, calls=%fused_computation.50 | loop fusion | flops 4681728 | bytes 10108928 | tf_op jit(solution)/shard_map/reduce_sum | solution.py:63
  94.8 2.5 %multiply_reduce_fusion.19 = (f32[16,128]{1,0:T(8,128)S(1)}, f32[16,128]{1,0:T(8,128)S(1)}, f32[16,128]{1,0:T(8,128)S(1)}, f32[16,128]{1,0:T(8,128)S(1)}, f32[16...) fusion(f32[64,16,128]{2,1,0:T(8,128)S(1)} %get-tuple-element.69, ...), kind=kLoop, calls=%fused_computation.32 | loop fusion | flops 4681728 | bytes 10108928 | tf_op jit(solution)/shard_map/reduce_sum | solution.py:63
  97.3 0.2 fusion.4
  98.2 0.8 gather_fusion.1
  99.2 32.3 %all_to_all.10 = f32[16,8,16,128]{3,2,1,0:T(8,128)S(1)} all-to-all(f32[16,8,16,128]{3,2,1,0:T(8,128)S(1)} %pad_maximum_fusion), channel_id=1, replica_groups=mesh['rows'=16,'tm'=16] {'tm'}, dimensions={0} | all-to-all | bytes 2097152 | tf_op jit(solution)/shard_map/all_to_all | solution.py:123
  131.6 0.3 copy.13
  131.9 1.0 slice.955
  132.9 0.3 copy.12
  133.3 1.0 slice.953
  (138 shorter events, 4.7 us)
Async XLA Ops:
  1.5 8.7 %collective-permute-start = (f32[4,6,512]{2,1,0:T(8,128)S(1)}, f32[4,6,512]{2,1,0:T(8,128)S(1)}, u32[]{:S(2)}, u32[]{:S(2)}) collective-permute-start(f32[4,6,512]{2,1,0:T(8,128)S(1)} %get-tuple-element.154), channel_id=1, source_target_pairs={{0,16},{16,32},{32,48},{48,64},{64,80},{80,96},{96,112},{112,128},... | collective-permute-start | bytes 147464 | tf_op jit(solution)/shard_map/ppermute | solution.py:18
  3.4 6.2 %collective-permute-start.1 = (f32[4,6,512]{2,1,0:T(8,128)S(1)}, f32[4,6,512]{2,1,0:T(8,128)S(1)}, u32[]{:S(2)}, u32[]{:S(2)}) collective-permute-start(f32[4,6,512]{2,1,0:T(8,128)S(1)} %get-tuple-element.155), channel_id=1, source_target_pairs={{16,0},{32,16},{48,32},{64,48},{80,64},{96,80},{112,96},{128,112},... | collective-permute-start | bytes 147464 | tf_op jit(solution)/shard_map/ppermute | solution.py:20
  8.2 2.0 %copy-start = (f32[4,64,512]{2,1,0:T(8,128)S(1)}, f32[4,64,512]{2,1,0:T(8,128)}, u32[]{:S(2)}) copy-start(f32[4,64,512]{2,1,0:T(8,128)} %param.7) | copy-start | bytes 1572868
  20.4 10.3 %copy-start.16 = (s32[64,2]{0,1:T(2,128)S(1)}, s32[64,2]{0,1:T(2,128)}, u32[]{:S(2)}) copy-start(s32[64,2]{0,1:T(2,128)} %param.9) | copy-start | bytes 1540
  20.4 10.3 %copy-start.17 = (s32[64]{0:T(128)S(1)}, s32[64]{0:T(128)}, u32[]{:S(2)}) copy-start(s32[64]{0:T(128)} %constant.30.clone) | copy-start | bytes 772
  20.4 10.3 %copy-start.18 = (s32[64]{0:T(128)S(1)}, s32[64]{0:T(128)}, u32[]{:S(2)}) copy-start(s32[64]{0:T(128)} %constant.29.clone) | copy-start | bytes 772
  20.4 53.0 %all-to-all-start = ((f32[16,192,128]{2,1,0:T(8,128)}), f32[16,192,128]{2,1,0:T(8,128)S(1)}, u32[]{:S(2)}, u32[]{:S(2)}) async-start(f32[16,192,128]{2,1,0:T(8,128)} %bitcast.138), calls=%async_computation | async-start | bytes 3145728 | tf_op jit(solution)/shard_map/all_to_all | solution.py:114
  79.7 0.7 copy-start.1
  79.7 0.7 copy-start.2
  79.7 0.7 copy-start.3
  79.7 0.7 copy-start.4
  79.7 0.7 copy-start.5
  79.7 0.7 copy-start.6
  79.8 0.7 copy-start.7
  79.8 0.7 copy-start.8
  79.8 0.7 copy-start.9
  79.8 0.8 copy-start.10
  79.8 0.8 copy-start.11
  79.8 0.8 copy-start.12
  79.8 0.8 copy-start.13
  79.8 0.8 copy-start.14
  97.3 1.7 %copy-start.15 = (pred[64]{0:T(512)(128)(4,1)S(1)}, pred[64]{0:T(512)(128)(4,1)}, u32[]{:S(2)}) copy-start(pred[64]{0:T(512)(128)(4,1)} %get-tuple-element.160) | copy-start | bytes 196

commit v3 on v1

--- a/solution.py
+++ b/solution.py
@@ -3,6 +3,7 @@
 import numpy as np
 from jax import lax
 from jax.sharding import PartitionSpec as P
+
 
 HALO = 6
 
@@ -43,7 +44,7 @@
     return same.astype(jnp.int32)
 
 
-def tile_split(count, rows, cols):
+def tile_split(count, cols):
     b = 1
     while b * 2 <= count and cols // (b * 2) >= 128 and count % (b * 2) == 0:
         b *= 2
@@ -51,8 +52,7 @@
     return a, b
 
 
-def tile_compute(rt, wt, order, place, points, h, w, frames_all, cycle):
-    ordered_weight = jnp.take(wt, order, axis=0)
+def tile_partial(rt, ordered_weight, points, h, w):
     background = jnp.zeros((rt.shape[0], h, w), jnp.float32)
     for index, (dy, dx) in enumerate(points):
         window = rt[:, HALO + dy : HALO + dy + h, HALO + dx : HALO + dx + w]
@@ -65,16 +65,18 @@
         ]
     )
     squares = jnp.sum(rt * rt, axis=0)
-    energy_sum = jnp.zeros((h, w), jnp.float32)
-    for dy, dx in points:
-        energy_sum = energy_sum + squares[HALO + dy : HALO + dy + h, HALO + dx : HALO + dx + w]
-    gradient = jnp.take(grads, place, axis=0)
-    energy = energy_sum / (cycle * frames_all) + 1e-06
-    new_weight = wt + gradient / (frames_all * energy)[None]
-    return error, new_weight
+    return error, grads, squares
 
 
-def on_device(residual, cycle_weight, cycle_offsets):
+def pack(parts, n):
+    flat = [p.reshape(n, -1) for p in parts]
+    used = sum(f.shape[1] for f in flat)
+    chunk = -(-used // 1024) * 1024
+    flat.append(jnp.zeros((n, chunk - used), jnp.float32))
+    return jnp.concatenate(flat, axis=1).reshape(n, chunk // 128, 128)
+
+
+def on_device_body(residual, cycle_weight, cycle_offsets):
     frames_dev, rows_dev, cols = residual.shape
     k_dev = cycle_weight.shape[0]
     cycle = cycle_offsets.shape[0]
@@ -86,38 +88,63 @@
     order = jnp.sum(same * ks[None, :], axis=1)
     place = jnp.sum(same * ks[:, None], axis=0)
 
-    a, b = tile_split(n, rows_dev, cols)
+    a, b = tile_split(n, cols)
     h, w = rows_dev // a, cols // b
 
     extended = with_halo(residual, (("rows", 1),), HALO)
     padded = jnp.pad(extended, ((0, 0), (0, 0), (HALO, HALO)))
+    hh, ww = h + 2 * HALO, w + 2 * HALO
     res_tiles = jnp.stack(
         [
-            padded[:, i * h : i * h + h + 2 * HALO, j * w : j * w + w + 2 * HALO]
+            padded[:, i * h : i * h + hh, j * w : j * w + ww]
             for i in range(a)
             for j in range(b)
         ]
     )
-    rt = lax.all_to_all(res_tiles, "tm", 0, 0, tiled=True)
-    rt = rt.reshape(frames_all, h + 2 * HALO, w + 2 * HALO)
+    w_tiles = cycle_weight.reshape(k_dev, a, h, b, w).transpose(1, 3, 0, 2, 4)
+    half = frames_dev // 2
+    res_len = half * hh * ww
+    w_len = k_dev * h * w
 
-    w_tiles = cycle_weight.reshape(k_dev, a, h, b, w).transpose(1, 3, 0, 2, 4)
-    w_tiles = w_tiles.reshape(n, k_dev, h, w)
-    wt = lax.all_to_all(w_tiles, "tm", 0, 0, tiled=True).reshape(cycle, h, w)
+    got_a = lax.all_to_all(pack([w_tiles, res_tiles[:, :half]], n), "tm", 0, 0, tiled=True)
+    got_a = got_a.reshape(n, -1)
+    wt = got_a[:, :w_len].reshape(cycle, h, w)
+    rt_a = got_a[:, w_len : w_len + res_len].reshape(n * half, hh, ww)
+    got_b = lax.all_to_all(pack([res_tiles[:, half:]], n), "tm", 0, 0, tiled=True)
+    rt_b = got_b.reshape(n, -1)[:, :res_len].reshape(n * half, hh, ww)
 
-    error_t, new_t = tile_compute(rt, wt, order, place, points, h, w, frames_all, cycle)
+    ordered_weight = jnp.take(wt, order, axis=0)
+    error_a, grads_a, squares_a = tile_partial(rt_a, ordered_weight, points, h, w)
+    back_a = lax.all_to_all(error_a.reshape(n, half, h, w), "tm", 0, 0, tiled=True)
+    error_b, grads_b, squares_b = tile_partial(rt_b, ordered_weight, points, h, w)
 
-    def back(x, lead):
-        x = lax.all_to_all(x.reshape(n, lead, h, w), "tm", 0, 0, tiled=True)
+    squares = squares_a + squares_b
+    energy_sum = jnp.zeros((h, w), jnp.float32)
+    for dy, dx in points:
+        energy_sum = energy_sum + squares[HALO + dy : HALO + dy + h, HALO + dx : HALO + dx + w]
+    gradient = jnp.take(grads_a + grads_b, place, axis=0)
+    energy = energy_sum / (cycle * frames_all) + 1e-06
+    new_t = wt + gradient / (frames_all * energy)[None]
+
+    out = jnp.concatenate(
+        [new_t.reshape(n, k_dev, h, w), error_b.reshape(n, frames_dev - half, h, w)], axis=1
+    )
+    back_b = lax.all_to_all(out, "tm", 0, 0, tiled=True)
+
+    def untile(x, lead):
         x = x.reshape(a, b, lead, h, w).transpose(2, 0, 3, 1, 4)
         return x.reshape(lead, rows_dev, cols)
 
-    return back(new_t, k_dev), back(error_t, frames_dev)
+    new_weight = untile(back_b[:, :k_dev], k_dev)
+    error = jnp.concatenate(
+        [untile(back_a, half), untile(back_b[:, k_dev:], frames_dev - half)], axis=0
+    )
+    return new_weight, error
 
 
 def solution(mesh):
     in_specs = (P("tm", "rows", None), P("tm", "rows", None), P())
     out_specs = (P("tm", "rows", None), P("tm", "rows", None))
     return jax.shard_map(
-        on_device, mesh=mesh, in_specs=in_specs, out_specs=out_specs, check_vma=False
+        on_device_body, mesh=mesh, in_specs=in_specs, out_specs=out_specs, check_vma=False
     )

time: 161 us -> 169 us (1.050)
  the two profiles are of different devices: /device:TPU:1 before, /device:TPU:8 now
where the time goes in v3:
time: 169 us; the launch traced here: 166 us
  waiting for transfers between devices  65.2 us (39%)
  starting transfers between devices  36.5 us (22%)
  local copies, waits for them, and re-layouts  31 us (18%)
  other arithmetic  30.2 us (18%)
  between operations  3.61 us (2%)
    reduce_sum x8, other arithmetic, tile_partial(): jnp.sum(error * rt[:, HALO + dy:HALO + dy + h, HALO + dx:HALO + dx + w],...  24.8 us
    all_to_all x1, waiting for transfers between devices, on_device_body(): back_b = lax.all_to_all(out, 'tm', 0, 0, tiled=True)  24.5 us
    all_to_all x1, waiting for transfers between devices, on_device_body(): lax.all_to_all(pack([w_tiles, res_tiles[:, :half]], n), 'tm', 0, 0, tiled...  23.5 us
    unnamed x393, local copies, waits for them, and re-layouts  22.8 us
    all_to_all x1, waiting for transfers between devices, on_device_body(): lax.all_to_all(pack([res_tiles[:, half:]], n), 'tm', 0, 0, tiled=True)  16.4 us
    all_to_all x1, starting transfers between devices, on_device_body(): lax.all_to_all(pack([res_tiles[:, half:]], n), 'tm', 0, 0, tiled=True)  11 us
    all_to_all x1, starting transfers between devices, on_device_body(): back_b = lax.all_to_all(out, 'tm', 0, 0, tiled=True)  9.62 us
    all_to_all x1, starting transfers between devices, on_device_body(): lax.all_to_all(error_a.reshape(n, half, h, w), 'tm', 0, 0, tiled=True)  6.23 us
  transfers between devices with their start and end apart: 6, of which 4 were waited for; matrix products, arithmetic and copies ran while one was open for 15% of the time, Pallas kernels for 0%

profile of v3, /device:TPU:8, one launch (start us, length us, event | category | flops | bytes accessed | tf_op | source)
XLA Modules:
  0.0 166.4 jit_solution(14588889942545995409)
XLA Ops:
  0.6 0.9 fusion.7
  1.6 1.9 %collective-permute-start = (f32[4,6,512]{2,1,0:T(8,128)S(1)}, f32[4,6,512]{2,1,0:T(8,128)S(1)}, u32[]{:S(2)}, u32[]{:S(2)}) collective-permute-start(f32[4,6,512]{2,1,0:T(8,128)S(1)} %get-tuple-element.201), channel_id=1, source_target_pairs={{0,16},{16,32},{32,48},{48,64},{64,80},{80,96},{96,112},{112,128},... | collective-permute-start | bytes 147464 | tf_op jit(solution)/shard_map/ppermute | solution.py:19
  3.5 3.6 %collective-permute-start.1 = (f32[4,6,512]{2,1,0:T(8,128)S(1)}, f32[4,6,512]{2,1,0:T(8,128)S(1)}, u32[]{:S(2)}, u32[]{:S(2)}) collective-permute-start(f32[4,6,512]{2,1,0:T(8,128)S(1)} %get-tuple-element.202), channel_id=1, source_target_pairs={{16,0},{32,16},{48,32},{64,48},{80,64},{96,80},{112,96},{128,112},... | collective-permute-start | bytes 147464 | tf_op jit(solution)/shard_map/ppermute | solution.py:21
  7.2 1.1 constant_dynamic-update-slice_fusion.1
  8.3 0.8 collective-permute-done.1
  9.0 1.4 select_maximum_fusion
  12.1 0.9 copy.18
  13.0 11.0 %all-to-all-start.1 = ((f32[16,64,128]{2,1,0:T(8,128)}), f32[16,64,128]{2,1,0:T(8,128)S(1)}, u32[]{:S(2)}, u32[]{:S(2)}) async-start(f32[16,64,128]{2,1,0:T(8,128)} %bitcast.229), calls=%async_computation.1 | async-start | bytes 1048576 | tf_op jit(solution)/shard_map/all_to_all | solution.py:113
  25.1 1.2 copy.16
  26.3 16.4 %all-to-all-done.1 = f32[16,64,128]{2,1,0:T(8,128)S(1)} async-done(((f32[16,64,128]{2,1,0:T(8,128)}), f32[16,64,128]{2,1,0:T(8,128)S(1)}, u32[]{:S(2)}, u32[]{:S(2)}) %all-to-all-start.1) | async-done | bytes 524320 | tf_op jit(solution)/shard_map/all_to_all | solution.py:113
  42.8 4.0 %all-to-all-start = ((f32[16,128,128]{2,1,0:T(8,128)}), f32[16,128,128]{2,1,0:T(8,128)S(1)}, u32[]{:S(2)}, u32[]{:S(2)}) async-start(f32[16,128,128]{2,1,0:T(8,128)} %bitcast.225), calls=%async_computation | async-start | bytes 2097152 | tf_op jit(solution)/shard_map/all_to_all | solution.py:109
  48.5 0.8 reshape.84
  49.2 23.5 %all-to-all-done = f32[16,128,128]{2,1,0:T(8,128)S(1)} async-done(((f32[16,128,128]{2,1,0:T(8,128)}), f32[16,128,128]{2,1,0:T(8,128)S(1)}, u32[]{:S(2)}, u32[]{:S(2)}) %all-to-all-start) | async-done | bytes 1048608 | tf_op jit(solution)/shard_map/all_to_all | solution.py:109
  75.4 6.6 %multiply_reduce_fusion.2 = (f32[16,128]{1,0:T(8,128)}, f32[16,128]{1,0:T(8,128)}, f32[16,128]{1,0:T(8,128)}, f32[16,128]{1,0:T(8,128)}, f32[16,128]{1,0:T(8,128...) fusion(f32[32,28,140]{2,1,0:T(8,128)S(1)} %reshape.84, ...), kind=kLoop, calls=%fused_computation.166 | loop fusion | flops 10711040 | bytes 17973248 | tf_op jit(solution)/shard_map/reduce_sum | solution.py:63
  82.4 2.0 %multiply_reduce_fusion.38 = (f32[16,128]{1,0:T(8,128)}, f32[16,128]{1,0:T(8,128)}, f32[16,128]{1,0:T(8,128)}, f32[16,128]{1,0:T(8,128)}, f32[16,128]{1,0:T(8,12...) fusion(f32[32,16,128]{2,1,0:T(8,128)S(1)} %get-tuple-element.13, ...), kind=kLoop, calls=%fused_computation.202 | loop fusion | flops 2322432 | bytes 5128192 | tf_op jit(solution)/shard_map/reduce_sum | solution.py:63
  84.3 1.4 multiply_reduce_fusion.56
  85.7 1.8 %multiply_reduce_fusion.20 = (f32[16,128]{1,0:T(8,128)}, f32[16,128]{1,0:T(8,128)}, f32[16,128]{1,0:T(8,128)}, f32[16,128]{1,0:T(8,128)}, f32[16,128]{1,0:T(8,12...) fusion(f32[32,16,128]{2,1,0:T(8,128)S(1)} %get-tuple-element.13, ...), kind=kLoop, calls=%fused_computation.184 | loop fusion | flops 2322432 | bytes 5128192 | tf_op jit(solution)/shard_map/reduce_sum | solution.py:63
  87.5 0.8 reshape.80
  89.5 6.8 %multiply_reduce_fusion.66 = (f32[16,128]{1,0:T(8,128)S(1)}, f32[16,128]{1,0:T(8,128)S(1)}, f32[16,128]{1,0:T(8,128)S(1)}, f32[16,128]{1,0:T(8,128)S(1)}, f32[16...) fusion(f32[32,28,140]{2,1,0:T(8,128)S(1)} %reshape.80, ...), kind=kLoop, calls=%fused_computation.230 | loop fusion | flops 10711040 | bytes 17973248 | tf_op jit(solution)/shard_map/reduce_sum | solution.py:63
  96.3 2.2 %multiply_reduce_fusion.84 = (f32[16,128]{1,0:T(8,128)S(1)}, f32[16,128]{1,0:T(8,128)S(1)}, f32[16,128]{1,0:T(8,128)S(1)}, f32[16,128]{1,0:T(8,128)S(1)}, f32[16...) fusion(f32[32,16,128]{2,1,0:T(8,128)} %get-tuple-element.134, ...), kind=kLoop, calls=%fused_computation.248 | loop fusion | flops 2322432 | bytes 5128192 | tf_op jit(solution)/shard_map/reduce_sum | solution.py:63
  98.4 2.2 %multiply_reduce_fusion.102 = (f32[16,128]{1,0:T(8,128)S(1)}, f32[16,128]{1,0:T(8,128)S(1)}, f32[16,128]{1,0:T(8,128)S(1)}, f32[16,128]{1,0:T(8,128)S(1)}, f32[1...) fusion(f32[32,16,128]{2,1,0:T(8,128)} %get-tuple-element.134, ...), kind=kLoop, calls=%fused_computation.266 | loop fusion | flops 2322432 | bytes 5128192 | tf_op jit(solution)/shard_map/reduce_sum | solution.py:63
  101.1 1.7 %multiply_reduce_fusion.120 = (f32[16,128]{1,0:T(8,128)S(1)}, f32[16,128]{1,0:T(8,128)S(1)}, f32[16,128]{1,0:T(8,128)S(1)}, f32[16,128]{1,0:T(8,128)S(1)}, f32[1...) fusion(f32[32,16,128]{2,1,0:T(8,128)} %get-tuple-element.134, ...), kind=kLoop, calls=%fused_computation.284 | loop fusion | flops 1290240 | bytes 2965504 | tf_op jit(solution)/shard_map/reduce_sum | solution.py:63
  103.1 0.7 constant_dynamic-update-slice_fusion.145
  103.8 6.2 %all-to-all-start.3 = ((f32[16,2,16,128]{3,2,1,0:T(8,128)}), f32[16,2,16,128]{3,2,1,0:T(8,128)S(1)}, u32[]{:S(2)}, u32[]{:S(2)}) async-start(f32[16,2,16,128]{3,2,1,0:T(8,128)} %bitcast.215), calls=%async_computation.3 | async-start | bytes 524288 | tf_op jit(solution)/shard_map/all_to_all | solution.py:118
  110.0 0.7 constant_dynamic-update-slice_fusion.144
  125.4 0.7 constant_dynamic-update-slice_fusion.117
  127.6 0.8 gather_fusion.1
  128.6 0.9 pad_maximum_fusion
  129.5 9.6 %all-to-all-start.2 = ((f32[16,6,16,128]{3,2,1,0:T(8,128)}), f32[16,6,16,128]{3,2,1,0:T(8,128)S(1)}, u32[]{:S(2)}, u32[]{:S(2)}) async-start(f32[16,6,16,128]{3,2,1,0:T(8,128)} %pad_maximum_fusion), calls=%async_computation.2 | async-start | bytes 1572864 | tf_op jit(solution)/shard_map/all_to_all | solution.py:132
  139.4 24.5 %all-to-all-done.2 = f32[16,6,16,128]{3,2,1,0:T(8,128)S(1)} async-done(((f32[16,6,16,128]{3,2,1,0:T(8,128)}), f32[16,6,16,128]{3,2,1,0:T(8,128)S(1)}, u32[]{:S(2)}, u32[]{:S(2)}) %all-to-all-start.2) | async-done | bytes 786464 | tf_op jit(solution)/shard_map/all_to_all | solution.py:132
  164.6 1.0 reshape.88
  165.6 0.8 pad_maximum_fusion.1
  (431 shorter events, 23.8 us)
Async XLA Ops:
  1.6 6.7 %collective-permute-start = (f32[4,6,512]{2,1,0:T(8,128)S(1)}, f32[4,6,512]{2,1,0:T(8,128)S(1)}, u32[]{:S(2)}, u32[]{:S(2)}) collective-permute-start(f32[4,6,512]{2,1,0:T(8,128)S(1)} %get-tuple-element.201), channel_id=1, source_target_pairs={{0,16},{16,32},{32,48},{48,64},{64,80},{80,96},{96,112},{112,128},... | collective-permute-start | bytes 147464 | tf_op jit(solution)/shard_map/ppermute | solution.py:19
  3.5 5.5 %collective-permute-start.1 = (f32[4,6,512]{2,1,0:T(8,128)S(1)}, f32[4,6,512]{2,1,0:T(8,128)S(1)}, u32[]{:S(2)}, u32[]{:S(2)}) collective-permute-start(f32[4,6,512]{2,1,0:T(8,128)S(1)} %get-tuple-element.202), channel_id=1, source_target_pairs={{16,0},{32,16},{48,32},{64,48},{80,64},{96,80},{112,96},{128,112},... | collective-permute-start | bytes 147464 | tf_op jit(solution)/shard_map/ppermute | solution.py:21
  13.0 29.7 %all-to-all-start.1 = ((f32[16,64,128]{2,1,0:T(8,128)}), f32[16,64,128]{2,1,0:T(8,128)S(1)}, u32[]{:S(2)}, u32[]{:S(2)}) async-start(f32[16,64,128]{2,1,0:T(8,128)} %bitcast.229), calls=%async_computation.1 | async-start | bytes 1048576 | tf_op jit(solution)/shard_map/all_to_all | solution.py:113
  42.8 30.0 %all-to-all-start = ((f32[16,128,128]{2,1,0:T(8,128)}), f32[16,128,128]{2,1,0:T(8,128)S(1)}, u32[]{:S(2)}, u32[]{:S(2)}) async-start(f32[16,128,128]{2,1,0:T(8,128)} %bitcast.225), calls=%async_computation | async-start | bytes 2097152 | tf_op jit(solution)/shard_map/all_to_all | solution.py:109
  100.8 25.5 %copy-start.105 = (f32[16,128]{1,0:T(8,128)S(1)}, f32[16,128]{1,0:T(8,128)}, u32[]{:S(2)}) copy-start(f32[16,128]{1,0:T(8,128)} %get-tuple-element.28) | copy-start | bytes 24580
  100.8 25.5 %copy-start.104 = (f32[16,128]{1,0:T(8,128)S(1)}, f32[16,128]{1,0:T(8,128)}, u32[]{:S(2)}) copy-start(f32[16,128]{1,0:T(8,128)} %get-tuple-element.27) | copy-start | bytes 24580
  100.8 25.5 %copy-start.103 = (f32[16,128]{1,0:T(8,128)S(1)}, f32[16,128]{1,0:T(8,128)}, u32[]{:S(2)}) copy-start(f32[16,128]{1,0:T(8,128)} %get-tuple-element.26) | copy-start | bytes 24580
  100.9 25.5 %copy-start.102 = (f32[16,128]{1,0:T(8,128)S(1)}, f32[16,128]{1,0:T(8,128)}, u32[]{:S(2)}) copy-start(f32[16,128]{1,0:T(8,128)} %get-tuple-element.25) | copy-start | bytes 24580
  100.9 25.5 %copy-start.101 = (f32[16,128]{1,0:T(8,128)S(1)}, f32[16,128]{1,0:T(8,128)}, u32[]{:S(2)}) copy-start(f32[16,128]{1,0:T(8,128)} %get-tuple-element.24) | copy-start | bytes 24580
  100.9 25.5 %copy-start.100 = (f32[16,128]{1,0:T(8,128)S(1)}, f32[16,128]{1,0:T(8,128)}, u32[]{:S(2)}) copy-start(f32[16,128]{1,0:T(8,128)} %get-tuple-element.23) | copy-start | bytes 24580
  100.9 25.6 %copy-start.99 = (f32[16,128]{1,0:T(8,128)S(1)}, f32[16,128]{1,0:T(8,128)}, u32[]{:S(2)}) copy-start(f32[16,128]{1,0:T(8,128)} %get-tuple-element.22) | copy-start | bytes 24580
  100.9 25.6 %copy-start.98 = (f32[16,128]{1,0:T(8,128)S(1)}, f32[16,128]{1,0:T(8,128)}, u32[]{:S(2)}) copy-start(f32[16,128]{1,0:T(8,128)} %get-tuple-element.21) | copy-start | bytes 24580
  100.9 25.6 %copy-start.97 = (f32[16,128]{1,0:T(8,128)S(1)}, f32[16,128]{1,0:T(8,128)}, u32[]{:S(2)}) copy-start(f32[16,128]{1,0:T(8,128)} %get-tuple-element.20) | copy-start | bytes 24580
  100.9 25.6 %copy-start.96 = (f32[16,128]{1,0:T(8,128)S(1)}, f32[16,128]{1,0:T(8,128)}, u32[]{:S(2)}) copy-start(f32[16,128]{1,0:T(8,128)} %get-tuple-element.19) | copy-start | bytes 24580
  100.9 25.6 %copy-start.95 = (f32[16,128]{1,0:T(8,128)S(1)}, f32[16,128]{1,0:T(8,128)}, u32[]{:S(2)}) copy-start(f32[16,128]{1,0:T(8,128)} %get-tuple-element.18) | copy-start | bytes 24580
  100.9 25.6 %copy-start.94 = (f32[16,128]{1,0:T(8,128)S(1)}, f32[16,128]{1,0:T(8,128)}, u32[]{:S(2)}) copy-start(f32[16,128]{1,0:T(8,128)} %get-tuple-element.17) | copy-start | bytes 24580
  100.9 25.6 %copy-start.93 = (f32[16,128]{1,0:T(8,128)S(1)}, f32[16,128]{1,0:T(8,128)}, u32[]{:S(2)}) copy-start(f32[16,128]{1,0:T(8,128)} %get-tuple-element.16) | copy-start | bytes 24580
  101.0 25.6 %copy-start.92 = (f32[16,128]{1,0:T(8,128)S(1)}, f32[16,128]{1,0:T(8,128)}, u32[]{:S(2)}) copy-start(f32[16,128]{1,0:T(8,128)} %get-tuple-element.15) | copy-start | bytes 24580
  101.0 25.6 %copy-start.91 = (f32[16,128]{1,0:T(8,128)S(1)}, f32[16,128]{1,0:T(8,128)}, u32[]{:S(2)}) copy-start(f32[16,128]{1,0:T(8,128)} %get-tuple-element.14) | copy-start | bytes 24580
  101.0 25.7 %copy-start.90 = (f32[16,128]{1,0:T(8,128)S(1)}, f32[16,128]{1,0:T(8,128)}, u32[]{:S(2)}) copy-start(f32[16,128]{1,0:T(8,128)} %get-tuple-element.13) | copy-start | bytes 24580
  101.0 25.7 %copy-start.89 = (f32[16,128]{1,0:T(8,128)S(1)}, f32[16,128]{1,0:T(8,128)}, u32[]{:S(2)}) copy-start(f32[16,128]{1,0:T(8,128)} %get-tuple-element.12) | copy-start | bytes 24580
  101.0 25.7 %copy-start.88 = (f32[16,128]{1,0:T(8,128)S(1)}, f32[16,128]{1,0:T(8,128)}, u32[]{:S(2)}) copy-start(f32[16,128]{1,0:T(8,128)} %get-tuple-element.11) | copy-start | bytes 24580
  101.0 25.7 %copy-start.87 = (f32[16,128]{1,0:T(8,128)S(1)}, f32[16,128]{1,0:T(8,128)}, u32[]{:S(2)}) copy-start(f32[16,128]{1,0:T(8,128)} %get-tuple-element.10) | copy-start | bytes 24580
  101.0 25.7 %copy-start.86 = (f32[16,128]{1,0:T(8,128)S(1)}, f32[16,128]{1,0:T(8,128)}, u32[]{:S(2)}) copy-start(f32[16,128]{1,0:T(8,128)} %get-tuple-element.9) | copy-start | bytes 24580
  101.0 25.7 %copy-start.85 = (f32[16,128]{1,0:T(8,128)S(1)}, f32[16,128]{1,0:T(8,128)}, u32[]{:S(2)}) copy-start(f32[16,128]{1,0:T(8,128)} %get-tuple-element.8) | copy-start | bytes 24580
  101.0 25.7 %copy-start.84 = (f32[16,128]{1,0:T(8,128)S(1)}, f32[16,128]{1,0:T(8,128)}, u32[]{:S(2)}) copy-start(f32[16,128]{1,0:T(8,128)} %get-tuple-element.7) | copy-start | bytes 24580
  101.0 25.7 %copy-start.83 = (f32[16,128]{1,0:T(8,128)S(1)}, f32[16,128]{1,0:T(8,128)}, u32[]{:S(2)}) copy-start(f32[16,128]{1,0:T(8,128)} %get-tuple-element.6) | copy-start | bytes 24580
  101.1 25.7 %copy-start.82 = (f32[16,128]{1,0:T(8,128)S(1)}, f32[16,128]{1,0:T(8,128)}, u32[]{:S(2)}) copy-start(f32[16,128]{1,0:T(8,128)} %get-tuple-element.5) | copy-start | bytes 24580
  101.1 25.8 %copy-start.81 = (f32[16,128]{1,0:T(8,128)S(1)}, f32[16,128]{1,0:T(8,128)}, u32[]{:S(2)}) copy-start(f32[16,128]{1,0:T(8,128)} %get-tuple-element.4) | copy-start | bytes 24580
  101.1 25.8 %copy-start.80 = (f32[16,128]{1,0:T(8,128)S(1)}, f32[16,128]{1,0:T(8,128)}, u32[]{:S(2)}) copy-start(f32[16,128]{1,0:T(8,128)} %get-tuple-element.3) | copy-start | bytes 24580
  103.8 25.7 %all-to-all-start.3 = ((f32[16,2,16,128]{3,2,1,0:T(8,128)}), f32[16,2,16,128]{3,2,1,0:T(8,128)S(1)}, u32[]{:S(2)}, u32[]{:S(2)}) async-start(f32[16,2,16,128]{3,2,1,0:T(8,128)} %bitcast.215), calls=%async_computation.3 | async-start | bytes 524288 | tf_op jit(solution)/shard_map/all_to_all | solution.py:118
  129.5 34.4 %all-to-all-start.2 = ((f32[16,6,16,128]{3,2,1,0:T(8,128)}), f32[16,6,16,128]{3,2,1,0:T(8,128)S(1)}, u32[]{:S(2)}, u32[]{:S(2)}) async-start(f32[16,6,16,128]{3,2,1,0:T(8,128)} %pad_maximum_fusion), calls=%async_computation.2 | async-start | bytes 1572864 | tf_op jit(solution)/shard_map/all_to_all | solution.py:132
  (98 other events, 761.4 us)

commit v4 on v2

--- a/solution.py
+++ b/solution.py
@@ -1,7 +1,11 @@
+import functools
+
 import jax
 import jax.numpy as jnp
 import numpy as np
 from jax import lax
+from jax.experimental import pallas as pl
+from jax.experimental.pallas import tpu as pltpu
 from jax.sharding import PartitionSpec as P
 
 HALO = 6
@@ -51,19 +55,53 @@
     return a, b
 
 
+GROUP = 8
+
+
+def tile_kernel(points, h, w, rt_ref, w_ref, err_ref, grad_ref):
+    frames = rt_ref.shape[0]
+    grad_ref[...] = jnp.zeros(grad_ref.shape, jnp.float32)
+
+    def group(gi, carry):
+        f0 = pl.multiple_of(gi * GROUP, GROUP)
+        frames_here = pl.ds(f0, GROUP)
+        background = jnp.zeros((GROUP, h, w), jnp.float32)
+        for index, (dy, dx) in enumerate(points):
+            window = rt_ref[frames_here, pl.ds(HALO + dy, h), pl.ds(HALO + dx, w)]
+            background = background + w_ref[index][None] * window
+        error = rt_ref[frames_here, pl.ds(HALO, h), pl.ds(HALO, w)] - background
+        err_ref[frames_here] = error
+        for index, (dy, dx) in enumerate(points):
+            window = rt_ref[frames_here, pl.ds(HALO + dy, h), pl.ds(HALO + dx, w)]
+            grad_ref[index] = grad_ref[index] + jnp.sum(error * window, axis=0)
+        return carry
+
+    lax.fori_loop(0, frames // GROUP, group, 0)
+
+
+def tile_terms(rt, ordered_weight, points, h, w):
+    frames = rt.shape[0]
+    cycle = ordered_weight.shape[0]
+    vmem = pl.BlockSpec(memory_space=pltpu.VMEM)
+    return pl.pallas_call(
+        functools.partial(tile_kernel, points, h, w),
+        out_shape=(
+            jax.ShapeDtypeStruct((frames, h, w), jnp.float32),
+            jax.ShapeDtypeStruct((cycle, h, w), jnp.float32),
+        ),
+        in_specs=[vmem, vmem],
+        out_specs=(vmem, vmem),
+        cost_estimate=pl.CostEstimate(
+            flops=4 * frames * cycle * h * w,
+            bytes_accessed=4 * (rt.size + ordered_weight.size + (frames + cycle) * h * w),
+            transcendentals=0,
+        ),
+    )(rt, ordered_weight)
+
+
 def tile_compute(rt, wt, order, place, points, h, w, frames_all, cycle):
     ordered_weight = jnp.take(wt, order, axis=0)
-    background = jnp.zeros((rt.shape[0], h, w), jnp.float32)
-    for index, (dy, dx) in enumerate(points):
-        window = rt[:, HALO + dy : HALO + dy + h, HALO + dx : HALO + dx + w]
-        background = background + ordered_weight[index][None] * window
-    error = rt[:, HALO : HALO + h, HALO : HALO + w] - background
-    grads = jnp.stack(
-        [
-            jnp.sum(error * rt[:, HALO + dy : HALO + dy + h, HALO + dx : HALO + dx + w], axis=0)
-            for dy, dx in points
-        ]
-    )
+    error, grads = tile_terms(rt, ordered_weight, points, h, w)
     squares = jnp.sum(rt * rt, axis=0)
     energy_sum = jnp.zeros((h, w), jnp.float32)
     for dy, dx in points:

time: 135 us -> 200 us (1.48)
  the two profiles are of different devices: /device:TPU:40 before, /device:TPU:8 now
where the time goes in v4:
time: 200 us; the launch traced here: 199 us
  Pallas kernels  79.7 us (40%)
  waiting for transfers between devices  40.1 us (20%)
  blocking collectives  36.8 us (18%)
  local copies, waits for them, and re-layouts  22.6 us (11%)
  starting transfers between devices  16.7 us (8%)
  other arithmetic  2.41 us (1%)
    pallas_call x1, Pallas kernels, tile_terms(): pl.pallas_call(functools.partial(tile_kernel, points, h, w), out_shape=(j...  79.7 us
    all_to_all x1, waiting for transfers between devices, on_device(): got = lax.all_to_all(send, 'tm', 0, 0, tiled=True).reshape(n, chunk)  39.7 us
    all_to_all x1, blocking collectives, on_device(): out = lax.all_to_all(out, 'tm', 0, 0, tiled=True)  36.8 us
    all_to_all x1, starting transfers between devices, on_device(): got = lax.all_to_all(send, 'tm', 0, 0, tiled=True).reshape(n, chunk)  11.2 us
    another operation x17, local copies, waits for them, and re-layouts, on_device(): jnp.stack([padded[:, i * h:i * h + hh, j * w:j * w + ww] for i in range(a...  7.68 us
  transfers between devices with their start and end apart: 3, of which 2 were waited for; matrix products, arithmetic and copies ran while one was open for 1% of the time, Pallas kernels for 0%

profile of v4, /device:TPU:8, one launch (start us, length us, event | category | flops | bytes accessed | tf_op | source)
XLA Modules:
  0.0 199.3 jit_solution(5005323039407123859)
XLA Ops:
  0.6 0.9 fusion.9
  1.6 1.9 collective-permute-start
  3.5 3.6 %collective-permute-start.1 = (f32[4,6,512]{2,1,0:T(8,128)S(1)}, f32[4,6,512]{2,1,0:T(8,128)S(1)}, u32[]{:S(2)}, u32[]{:S(2)}) collective-permute-start(f32[4,6,512]{2,1,0:T(8,128)S(1)} %get-tuple-element.30), channel_id=1, source_target_pairs={{16,0},{32,16},{48,32},{64,48},{80,64},{96,80},{112,96},{128,112},... | collective-permute-start | bytes 147464 | tf_op jit(solution)/shard_map/ppermute | solution.py:24
  7.2 1.1 constant_dynamic-update-slice_fusion.1
  8.3 0.2 reshape.77
  8.6 0.4 collective-permute-done.1
  9.2 0.2 stack.65
  9.6 0.3 select_maximum_fusion
  10.1 0.2 stack.66
  11.5 0.3 fusion.8
  11.8 0.2 stack.61
  12.9 4.9 %stack.67 = f32[16,15680]{1,0:T(8,128)S(1)} concatenate(f32[1,15680]{1,0:T(1,128)S(1)} %stack.51, f32[1,15680]{1,0:T(1,128)S(1)} %stack.52, f32[1,15680]{1,0:T(1,128)S(1)} %stack.53, f32[1,15680]{1,0:T(1,128)S(1)} %stack.54, f32[1,15680]{1,0:T(1,128)S(1)} %stack.55, f32[1,15680]{1,0:T(1,128)S(1)} %stack.56, f32[1,15680]{1,0:T(1,128)S(1)} %stack.57, f32[1,15680]{1,0:T(1,128)S(1)} %stack.58, ...), dimensions={0} | concatenate | bytes 2007040 | tf_op jit(solution)/shard_map/stack | solution.py:133
  17.8 0.6 concatenate.21
  18.4 1.5 copy.12
  19.8 11.2 %all-to-all-start = ((f32[16,192,128]{2,1,0:T(8,128)}), f32[16,192,128]{2,1,0:T(8,128)S(1)}, u32[]{:S(2)}, u32[]{:S(2)}) async-start(f32[16,192,128]{2,1,0:T(8,128)} %bitcast.9), calls=%async_computation | async-start | bytes 3145728 | tf_op jit(solution)/shard_map/all_to_all | solution.py:152
  31.1 0.2 select_reduce_fusion
  31.3 39.7 %all-to-all-done = f32[16,192,128]{2,1,0:T(8,128)S(1)} async-done(((f32[16,192,128]{2,1,0:T(8,128)}), f32[16,192,128]{2,1,0:T(8,128)S(1)}, u32[]{:S(2)}, u32[]{:S(2)}) %all-to-all-start) | async-done | bytes 1572896 | tf_op jit(solution)/shard_map/all_to_all | solution.py:152
  71.0 0.9 copy.17
  71.9 0.2 slice.390
  72.1 1.0 slice.391
  73.2 2.5 %reshape.82.rt_ref = f32[64,28,140]{2,1,0:T(8,128)S(1)} reshape(f32[16,15680]{1,0:T(8,128)} %slice.391) | data formatting | bytes 2007040 | tf_op jit(solution)/shard_map/reshape | solution.py:153
  75.7 0.2 multiply_reduce_fusion
  76.0 0.6 gather_fusion
  76.6 0.5 copy-done
  77.1 0.9 broadcast_select_fusion.w_ref
  78.0 79.7 %shard_map.68 = (f32[64,16,128]{2,1,0:T(8,128)}, f32[64,16,128]{2,1,0:T(8,128)}) custom-call(f32[64,28,140]{2,1,0:T(8,128)} %copy-done, f32[64,16,128]{2,1,0:T(8,128)} %broadcast_select_fusion.w_ref), custom_call_target="tpu_custom_call" | custom-call | flops 33554432 | bytes 2576384 | tf_op jit(solution)/shard_map/pallas_call | solution.py:86
  157.6 0.2 fusion.4
  157.9 1.6 gather_fusion.1
  159.8 36.8 %all_to_all.10 = f32[16,8,16,128]{3,2,1,0:T(8,128)S(1)} all-to-all(f32[16,8,16,128]{3,2,1,0:T(8,128)S(1)} %pad_maximum_fusion), channel_id=1, replica_groups=mesh['rows'=16,'tm'=16] {'tm'}, dimensions={0} | all-to-all | bytes 2097152 | tf_op jit(solution)/shard_map/all_to_all | solution.py:161
  196.5 0.7 copy.18
  197.3 1.0 slice.375
  198.3 1.0 slice.373
  (42 shorter events, 3.2 us)
Async XLA Ops:
  0.6 7.6 %copy-start.2 = (f32[4,64,512]{2,1,0:T(8,128)S(1)}, f32[4,64,512]{2,1,0:T(8,128)}, u32[]{:S(2)}) copy-start(f32[4,64,512]{2,1,0:T(8,128)} %param.8) | copy-start | bytes 1572868
  1.6 8.0 %collective-permute-start = (f32[4,6,512]{2,1,0:T(8,128)S(1)}, f32[4,6,512]{2,1,0:T(8,128)S(1)}, u32[]{:S(2)}, u32[]{:S(2)}) collective-permute-start(f32[4,6,512]{2,1,0:T(8,128)S(1)} %get-tuple-element.29), channel_id=1, source_target_pairs={{0,16},{16,32},{32,48},{48,64},{64,80},{80,96},{96,112},{112,128},... | collective-permute-start | bytes 147464 | tf_op jit(solution)/shard_map/ppermute | solution.py:22
  3.5 5.5 %collective-permute-start.1 = (f32[4,6,512]{2,1,0:T(8,128)S(1)}, f32[4,6,512]{2,1,0:T(8,128)S(1)}, u32[]{:S(2)}, u32[]{:S(2)}) collective-permute-start(f32[4,6,512]{2,1,0:T(8,128)S(1)} %get-tuple-element.30), channel_id=1, source_target_pairs={{16,0},{32,16},{48,32},{64,48},{80,64},{96,80},{112,96},{128,112},... | collective-permute-start | bytes 147464 | tf_op jit(solution)/shard_map/ppermute | solution.py:24
  8.5 1.1 copy-start.1
  19.8 11.2 %copy-start.4 = (s32[64,2]{0,1:T(2,128)S(1)}, s32[64,2]{0,1:T(2,128)}, u32[]{:S(2)}) copy-start(s32[64,2]{0,1:T(2,128)} %param.9) | copy-start | bytes 1540
  19.8 11.2 %copy-start.5 = (s32[64]{0:T(128)S(1)}, s32[64]{0:T(128)}, u32[]{:S(2)}) copy-start(s32[64]{0:T(128)} %constant.30.clone) | copy-start | bytes 772
  19.8 11.2 %copy-start.6 = (s32[64]{0:T(128)S(1)}, s32[64]{0:T(128)}, u32[]{:S(2)}) copy-start(s32[64]{0:T(128)} %constant.29.clone) | copy-start | bytes 772
  19.8 51.2 %all-to-all-start = ((f32[16,192,128]{2,1,0:T(8,128)}), f32[16,192,128]{2,1,0:T(8,128)S(1)}, u32[]{:S(2)}, u32[]{:S(2)}) async-start(f32[16,192,128]{2,1,0:T(8,128)} %bitcast.9), calls=%async_computation | async-start | bytes 3145728 | tf_op jit(solution)/shard_map/all_to_all | solution.py:152
  75.7 1.3 copy-start
  157.6 2.0 %copy-start.3 = (f32[64,16,128]{2,1,0:T(8,128)S(1)}, f32[64,16,128]{2,1,0:T(8,128)}, u32[]{:S(2)}) copy-start(f32[64,16,128]{2,1,0:T(8,128)} %get-tuple-element.6) | copy-start | bytes 1572868

commit v5 on v2

--- a/solution.py
+++ b/solution.py
@@ -92,28 +92,36 @@
     extended = with_halo(residual, (("rows", 1),), HALO)
     padded = jnp.pad(extended, ((0, 0), (0, 0), (HALO, HALO)))
     hh, ww = h + 2 * HALO, w + 2 * HALO
-    res_tiles = jnp.stack(
-        [
-            padded[:, i * h : i * h + hh, j * w : j * w + ww]
-            for i in range(a)
-            for j in range(b)
-        ]
+    lanes = 128
+    spare = ww - lanes
+    tiles = [(i, j) for i in range(a) for j in range(b)]
+    main = jnp.stack([padded[:, i * h : i * h + hh, j * w : j * w + lanes] for i, j in tiles])
+    rest = jnp.stack(
+        [padded[:, i * h : i * h + hh, j * w + lanes : j * w + ww] for i, j in tiles]
     )
     w_tiles = cycle_weight.reshape(k_dev, a, h, b, w).transpose(1, 3, 0, 2, 4)
-    res_len = frames_dev * hh * ww
-    w_len = k_dev * h * w
-    chunk = -(-(res_len + w_len) // 1024) * 1024
+    main_rows = frames_dev * hh
+    w_rows = k_dev * h
+    rest_len = frames_dev * hh * spare
+    rest_rows = -(-rest_len // lanes)
+    used = main_rows + w_rows + rest_rows
+    total = -(-used // 8) * 8
     send = jnp.concatenate(
         [
-            res_tiles.reshape(n, res_len),
-            w_tiles.reshape(n, w_len),
-            jnp.zeros((n, chunk - res_len - w_len), jnp.float32),
+            main.reshape(n, main_rows, lanes),
+            w_tiles.reshape(n, w_rows, lanes),
+            jnp.pad(rest.reshape(n, rest_len), ((0, 0), (0, rest_rows * lanes - rest_len))).reshape(
+                n, rest_rows, lanes
+            ),
+            jnp.zeros((n, total - used, lanes), jnp.float32),
         ],
         axis=1,
-    ).reshape(n, chunk // 128, 128)
-    got = lax.all_to_all(send, "tm", 0, 0, tiled=True).reshape(n, chunk)
-    rt = got[:, :res_len].reshape(frames_all, hh, ww)
-    wt = got[:, res_len : res_len + w_len].reshape(cycle, h, w)
+    )
+    got = lax.all_to_all(send, "tm", 0, 0, tiled=True)
+    rt_main = got[:, :main_rows].reshape(frames_all, hh, lanes)
+    wt = got[:, main_rows : main_rows + w_rows].reshape(cycle, h, w)
+    rt_rest = got[:, main_rows + w_rows : used].reshape(n, rest_rows * lanes)[:, :rest_len]
+    rt = jnp.concatenate([rt_main, rt_rest.reshape(frames_all, hh, spare)], axis=2)
 
     error_t, new_t = tile_compute(rt, wt, order, place, points, h, w, frames_all, cycle)
 
@@ -121,9 +129,12 @@
         [new_t.reshape(n, k_dev, h, w), error_t.reshape(n, frames_dev, h, w)], axis=1
     )
     out = lax.all_to_all(out, "tm", 0, 0, tiled=True)
-    out = out.reshape(a, b, k_dev + frames_dev, h, w).transpose(2, 0, 3, 1, 4)
-    out = out.reshape(k_dev + frames_dev, rows_dev, cols)
-    return out[:k_dev], out[k_dev:]
+
+    def untile(x, lead):
+        x = x.reshape(a, b, lead, h, w).transpose(2, 0, 3, 1, 4)
+        return x.reshape(lead, rows_dev, cols)
+
+    return untile(out[:, :k_dev], k_dev), untile(out[:, k_dev:], frames_dev)
 
 
 def solution(mesh):

time: 135 us -> 127 us (0.941)
  the two profiles are of different devices: /device:TPU:40 before, /device:TPU:1 now
where the time goes in v5:
time: 127 us; the launch traced here: 126 us
  waiting for transfers between devices  37.9 us (30%)
  blocking collectives  33.9 us (27%)
  other arithmetic  19.9 us (16%)
  starting transfers between devices  17.5 us (14%)
  local copies, waits for them, and re-layouts  15 us (12%)
  between operations  1.85 us (1%)
    all_to_all x1, waiting for transfers between devices, on_device(): got = lax.all_to_all(send, 'tm', 0, 0, tiled=True)  37.9 us
    all_to_all x1, blocking collectives, on_device(): out = lax.all_to_all(out, 'tm', 0, 0, tiled=True)  33.9 us
    reduce_sum x4, other arithmetic, tile_compute(): jnp.sum(error * rt[:, HALO + dy:HALO + dy + h, HALO + dx:HALO + dx + w],...  16.7 us
    all_to_all x1, starting transfers between devices, on_device(): got = lax.all_to_all(send, 'tm', 0, 0, tiled=True)  10.4 us
    ppermute x1, starting transfers between devices, with_halo(): lax.ppermute(head, axis, [((i + 1) % count, i) for i in range(ends)])  5.24 us
    unnamed x91, local copies, waits for them, and re-layouts  2.65 us
  transfers between devices with their start and end apart: 3, of which 1 were waited for; matrix products, arithmetic and copies ran while one was open for 2% of the time, Pallas kernels for 0%

profile of v5, /device:TPU:1, one launch (start us, length us, event | category | flops | bytes accessed | tf_op | source)
XLA Modules:
  0.0 126.1 jit_solution(2281401258469447983)
XLA Ops:
  0.6 0.9 fusion.11
  1.5 5.2 %collective-permute-start.1 = (f32[4,6,512]{2,1,0:T(8,128)S(1)}, f32[4,6,512]{2,1,0:T(8,128)S(1)}, u32[]{:S(2)}, u32[]{:S(2)}) collective-permute-start(f32[4,6,512]{2,1,0:T(8,128)S(1)} %get-tuple-element.171), channel_id=1, source_target_pairs={{16,0},{32,16},{48,32},{64,48},{80,64},{96,80},{112,96},{128,112},... | collective-permute-start | bytes 147464 | tf_op jit(solution)/shard_map/ppermute | solution.py:20
  6.8 1.9 %collective-permute-start = (f32[4,6,512]{2,1,0:T(8,128)S(1)}, f32[4,6,512]{2,1,0:T(8,128)S(1)}, u32[]{:S(2)}, u32[]{:S(2)}) collective-permute-start(f32[4,6,512]{2,1,0:T(8,128)S(1)} %get-tuple-element.172), channel_id=1, source_target_pairs={{0,16},{16,32},{32,48},{48,64},{64,80},{80,96},{96,112},{112,128},... | collective-permute-start | bytes 147464 | tf_op jit(solution)/shard_map/ppermute | solution.py:18
  8.7 1.1 constant_dynamic-update-slice_fusion.1
  9.8 1.2 reshape.119
  11.4 0.3 select_maximum_fusion
  12.2 0.2 pad_maximum_fusion.4
  12.6 0.2 fusion.10
  14.3 0.2 stack.330
  14.8 1.4 %maximum_maximum_fusion = f32[16,192,128]{2,1,0:T(8,128)} fusion(f32[16,11,128]{2,1,0:T(8,128)S(1)} %reshape.121, f32[16,64,128]{2,1,0:T(8,128)S(1)} %bitcast.280, f32[16,112,128]{2,1,0:T(8,128)S(1)} %constant_dynamic-update-slice_fusion.2, f32[192]{0:T(256)S(1)} %pad.15.clone), kind=kLoop, calls=%fused_computation.3 | loop fusion | flops 1179648 | bytes 3105536 | tf_op jit(solution)/shard_map/concatenate | solution.py:109
  16.2 10.4 %all-to-all-start = ((f32[16,192,128]{2,1,0:T(8,128)}), f32[16,192,128]{2,1,0:T(8,128)S(1)}, u32[]{:S(2)}, u32[]{:S(2)}) async-start(f32[16,192,128]{2,1,0:T(8,128)} %maximum_maximum_fusion), calls=%async_computation | async-start | bytes 3145728 | tf_op jit(solution)/shard_map/all_to_all | solution.py:120
  26.6 0.2 select_reduce_fusion
  26.8 37.9 %all-to-all-done = f32[16,192,128]{2,1,0:T(8,128)S(1)} async-done(((f32[16,192,128]{2,1,0:T(8,128)}), f32[16,192,128]{2,1,0:T(8,128)S(1)}, u32[]{:S(2)}, u32[]{:S(2)}) %all-to-all-start) | async-done | bytes 1572896 | tf_op jit(solution)/shard_map/all_to_all | solution.py:120
  64.8 0.6 gather_fusion
  65.4 0.1 broadcast_select_fusion
  65.7 1.0 slice.1071
  66.7 1.2 reshape.123
  68.0 1.4 %reshape.125 = f32[64,28,12]{2,1,0:T(8,128)} reshape(f32[16,1344]{1,0:T(8,128)S(1)} %bitcast.285) | data formatting | bytes 172032 | tf_op jit(solution)/shard_map/reshape | solution.py:124
  69.5 1.1 copy-done.1
  70.7 0.2 multiply_reduce_fusion
  70.9 10.2 %multiply_reduce_fusion.1 = (f32[16,128]{1,0:T(8,128)S(1)}, f32[16,128]{1,0:T(8,128)S(1)}, f32[16,128]{1,0:T(8,128)S(1)}, f32[16,128]{1,0:T(8,128)S(1)}, f32[16,...) fusion(f32[64,28,140]{2,1,0:T(8,128)S(1)} %constant_dynamic-upd, ...), kind=kLoop, calls=%fused_computation.13 | loop fusion | flops 21458944 | bytes 35274752 | tf_op jit(solution)/shard_map/reduce_sum | solution.py:63
  81.1 1.3 %multiply_reduce_fusion.56 = (f32[16,128]{1,0:T(8,128)S(1)}, f32[16,128]{1,0:T(8,128)S(1)}, f32[16,128]{1,0:T(8,128)S(1)}, f32[16,128]{1,0:T(8,128)S(1)}, f32[16...) fusion(f32[64,16,128]{2,1,0:T(8,128)S(1)} %get-tuple-element.69, ...), kind=kLoop, calls=%fused_computation.68 | loop fusion | flops 2600960 | bytes 5849088 | tf_op jit(solution)/shard_map/reduce_sum | solution.py:63
  82.4 2.6 %multiply_reduce_fusion.19 = (f32[16,128]{1,0:T(8,128)S(1)}, f32[16,128]{1,0:T(8,128)S(1)}, f32[16,128]{1,0:T(8,128)S(1)}, f32[16,128]{1,0:T(8,128)S(1)}, f32[16...) fusion(f32[64,16,128]{2,1,0:T(8,128)S(1)} %get-tuple-element.69, ...), kind=kLoop, calls=%fused_computation.31 | loop fusion | flops 4681728 | bytes 10108928 | tf_op jit(solution)/shard_map/reduce_sum | solution.py:63
  85.0 2.6 %multiply_reduce_fusion.38 = (f32[16,128]{1,0:T(8,128)S(1)}, f32[16,128]{1,0:T(8,128)S(1)}, f32[16,128]{1,0:T(8,128)S(1)}, f32[16,128]{1,0:T(8,128)S(1)}, f32[16...) fusion(f32[64,16,128]{2,1,0:T(8,128)S(1)} %get-tuple-element.69, ...), kind=kLoop, calls=%fused_computation.50 | loop fusion | flops 4681728 | bytes 10108928 | tf_op jit(solution)/shard_map/reduce_sum | solution.py:63
  87.7 0.2 fusion.4
  88.6 0.6 gather_fusion.1
  89.2 0.1 fusion.1
  89.4 33.9 %all_to_all.10 = f32[16,8,16,128]{3,2,1,0:T(8,128)S(1)} all-to-all(f32[16,8,16,128]{3,2,1,0:T(8,128)S(1)} %pad_maximum_fusion), channel_id=1, replica_groups=mesh['rows'=16,'tm'=16] {'tm'}, dimensions={0} | all-to-all | bytes 2097152 | tf_op jit(solution)/shard_map/all_to_all | solution.py:131
  123.4 0.3 copy.12
  123.8 1.0 reshape.131
  124.8 0.3 copy.11
  125.1 1.0 reshape.129
  (150 shorter events, 3.1 us)
Async XLA Ops:
  1.5 9.9 %copy-start = (f32[4,64,512]{2,1,0:T(8,128)S(1)}, f32[4,64,512]{2,1,0:T(8,128)}, u32[]{:S(2)}) copy-start(f32[4,64,512]{2,1,0:T(8,128)} %param.7) | copy-start | bytes 1572868
  1.5 9.6 %collective-permute-start.1 = (f32[4,6,512]{2,1,0:T(8,128)S(1)}, f32[4,6,512]{2,1,0:T(8,128)S(1)}, u32[]{:S(2)}, u32[]{:S(2)}) collective-permute-start(f32[4,6,512]{2,1,0:T(8,128)S(1)} %get-tuple-element.171), channel_id=1, source_target_pairs={{16,0},{32,16},{48,32},{64,48},{80,64},{96,80},{112,96},{128,112},... | collective-permute-start | bytes 147464 | tf_op jit(solution)/shard_map/ppermute | solution.py:20
  6.8 4.6 %collective-permute-start = (f32[4,6,512]{2,1,0:T(8,128)S(1)}, f32[4,6,512]{2,1,0:T(8,128)S(1)}, u32[]{:S(2)}, u32[]{:S(2)}) collective-permute-start(f32[4,6,512]{2,1,0:T(8,128)S(1)} %get-tuple-element.172), channel_id=1, source_target_pairs={{0,16},{16,32},{32,48},{48,64},{64,80},{80,96},{96,112},{112,128},... | collective-permute-start | bytes 147464 | tf_op jit(solution)/shard_map/ppermute | solution.py:18
  16.2 10.4 %copy-start.2 = (s32[64,2]{0,1:T(2,128)S(1)}, s32[64,2]{0,1:T(2,128)}, u32[]{:S(2)}) copy-start(s32[64,2]{0,1:T(2,128)} %param.9) | copy-start | bytes 1540
  16.2 10.4 %copy-start.3 = (s32[64]{0:T(128)S(1)}, s32[64]{0:T(128)}, u32[]{:S(2)}) copy-start(s32[64]{0:T(128)} %constant.30.clone) | copy-start | bytes 772
  16.2 10.4 %copy-start.4 = (s32[64]{0:T(128)S(1)}, s32[64]{0:T(128)}, u32[]{:S(2)}) copy-start(s32[64]{0:T(128)} %constant.29.clone) | copy-start | bytes 772
  16.2 48.6 %all-to-all-start = ((f32[16,192,128]{2,1,0:T(8,128)}), f32[16,192,128]{2,1,0:T(8,128)S(1)}, u32[]{:S(2)}, u32[]{:S(2)}) async-start(f32[16,192,128]{2,1,0:T(8,128)} %maximum_maximum_fusion), calls=%async_computation | async-start | bytes 3145728 | tf_op jit(solution)/shard_map/all_to_all | solution.py:120
  69.4 1.2 copy-start.1

commit v6 on v5

--- a/solution.py
+++ b/solution.py
@@ -1,7 +1,11 @@
+import functools
+
 import jax
 import jax.numpy as jnp
 import numpy as np
 from jax import lax
+from jax.experimental import pallas as pl
+from jax.experimental.pallas import tpu as pltpu
 from jax.sharding import PartitionSpec as P
 
 HALO = 6
@@ -74,6 +78,52 @@
     return error, new_weight
 
 
+def exchange_kernel(n, x_ref, o_ref, send_sem, recv_sem, local_sem):
+    me = lax.axis_index("tm")
+    row = lax.axis_index("rows")
+    mesh_id = pl.DeviceIdType.MESH
+    barrier = pltpu.get_barrier_semaphore()
+    for step in range(1, n):
+        peer = lax.rem(me + step, n)
+        pl.semaphore_signal(barrier, inc=1, device_id=(row, peer), device_id_type=mesh_id)
+    pl.semaphore_wait(barrier, n - 1)
+    local = pltpu.make_async_copy(x_ref.at[me], o_ref.at[me], local_sem)
+    local.start()
+    copies = []
+    for step in range(1, n):
+        peer = lax.rem(me + step, n)
+        copy = pltpu.make_async_remote_copy(
+            src_ref=x_ref.at[peer],
+            dst_ref=o_ref.at[me],
+            send_sem=send_sem.at[step],
+            recv_sem=recv_sem.at[step],
+            device_id=(row, peer),
+            device_id_type=mesh_id,
+        )
+        copy.start()
+        copies.append(copy)
+    for copy in copies:
+        copy.wait()
+    local.wait()
+
+
+def exchange(x, n, tag):
+    anywhere = pl.BlockSpec(memory_space=pl.ANY)
+    return pl.pallas_call(
+        functools.partial(exchange_kernel, n),
+        out_shape=jax.ShapeDtypeStruct(x.shape, x.dtype),
+        in_specs=[anywhere],
+        out_specs=anywhere,
+        scratch_shapes=[
+            pltpu.SemaphoreType.DMA((n,)),
+            pltpu.SemaphoreType.DMA((n,)),
+            pltpu.SemaphoreType.DMA,
+        ],
+        compiler_params=pltpu.CompilerParams(collective_id=tag, has_side_effects=True),
+        name=f"exchange_{tag}",
+    )(x)
+
+
 def on_device(residual, cycle_weight, cycle_offsets):
     frames_dev, rows_dev, cols = residual.shape
     k_dev = cycle_weight.shape[0]
@@ -128,7 +178,8 @@
     out = jnp.concatenate(
         [new_t.reshape(n, k_dev, h, w), error_t.reshape(n, frames_dev, h, w)], axis=1
     )
-    out = lax.all_to_all(out, "tm", 0, 0, tiled=True)
+    out = exchange(out.reshape(n, (k_dev + frames_dev) * h, w), n, 1)
+    out = out.reshape(n, k_dev + frames_dev, h, w)
 
     def untile(x, lead):
         x = x.reshape(a, b, lead, h, w).transpose(2, 0, 3, 1, 4)

time: 127 us -> 127 us (level)
  blocking collectives: 33.9 us -> 0 us
  Pallas kernels: 0 us -> 32.2 us
    all_to_all x1 -> x0, blocking collectives: 33.9 us -> none  [on_device(): out = lax.all_to_all(out, 'tm', 0, 0, tiled=True)]
    pallas_call x0 -> x1, Pallas kernels: none -> 32.2 us  [exchange(): pl.pallas_call(functools.partial(exchange_kernel, n), out_shape=jax.Shape...]
where the time goes in v6:
time: 127 us
  waiting for transfers between devices  37.9 us (30%)
  Pallas kernels  32.2 us (25%)
  other arithmetic  20.9 us (16%)
  starting transfers between devices  17.5 us (14%)
  local copies, waits for them, and re-layouts  16.2 us (13%)
  between operations  1.85 us (1%)
    all_to_all x1, waiting for transfers between devices, on_device(): got = lax.all_to_all(send, 'tm', 0, 0, tiled=True)  37.9 us
    pallas_call x1, Pallas kernels, exchange(): pl.pallas_call(functools.partial(exchange_kernel, n), out_shape=jax.Shape...  32.2 us
    reduce_sum x4, other arithmetic, tile_compute(): jnp.sum(error * rt[:, HALO + dy:HALO + dy + h, HALO + dx:HALO + dx + w],...  16.7 us
    all_to_all x1, starting transfers between devices, on_device(): got = lax.all_to_all(send, 'tm', 0, 0, tiled=True)  10.4 us
    ppermute x1, starting transfers between devices, with_halo(): lax.ppermute(head, axis, [((i + 1) % count, i) for i in range(ends)])  5.24 us
    unnamed x91, local copies, waits for them, and re-layouts  2.65 us
  transfers between devices with their start and end apart: 3, of which 1 were waited for; matrix products, arithmetic and copies ran while one was open for 2% of the time, Pallas kernels for 0%

profile of v6, /device:TPU:1, one launch (start us, length us, event | category | flops | bytes accessed | tf_op | source)
XLA Modules:
  0.0 126.6 jit_solution(3980059104835933122)
XLA Ops:
  0.6 0.9 fusion.11
  1.5 5.2 %collective-permute-start.1 = (f32[4,6,512]{2,1,0:T(8,128)S(1)}, f32[4,6,512]{2,1,0:T(8,128)S(1)}, u32[]{:S(2)}, u32[]{:S(2)}) collective-permute-start(f32[4,6,512]{2,1,0:T(8,128)S(1)} %get-tuple-element.171), channel_id=1, source_target_pairs={{16,0},{32,16},{48,32},{64,48},{80,64},{96,80},{112,96},{128,112},... | collective-permute-start | bytes 147464 | tf_op jit(solution)/shard_map/ppermute | solution.py:24
  6.8 1.9 %collective-permute-start = (f32[4,6,512]{2,1,0:T(8,128)S(1)}, f32[4,6,512]{2,1,0:T(8,128)S(1)}, u32[]{:S(2)}, u32[]{:S(2)}) collective-permute-start(f32[4,6,512]{2,1,0:T(8,128)S(1)} %get-tuple-element.172), channel_id=1, source_target_pairs={{0,16},{16,32},{32,48},{48,64},{64,80},{80,96},{96,112},{112,128},... | collective-permute-start | bytes 147464 | tf_op jit(solution)/shard_map/ppermute | solution.py:22
  8.7 1.1 constant_dynamic-update-slice_fusion.1
  9.8 1.2 reshape.125
  11.4 0.3 select_maximum_fusion
  12.2 0.2 pad_maximum_fusion.4
  12.6 0.2 fusion.10
  14.3 0.2 stack.330
  14.8 1.4 %maximum_maximum_fusion = f32[16,192,128]{2,1,0:T(8,128)} fusion(f32[16,11,128]{2,1,0:T(8,128)S(1)} %reshape.127, f32[16,64,128]{2,1,0:T(8,128)S(1)} %bitcast.288, f32[16,112,128]{2,1,0:T(8,128)S(1)} %constant_dynamic-update-slice_fusion.2, f32[192]{0:T(256)S(1)} %pad.15.clone), kind=kLoop, calls=%fused_computation.3 | loop fusion | flops 1179648 | bytes 3105536 | tf_op jit(solution)/shard_map/concatenate | solution.py:159
  16.2 10.4 %all-to-all-start = ((f32[16,192,128]{2,1,0:T(8,128)}), f32[16,192,128]{2,1,0:T(8,128)S(1)}, u32[]{:S(2)}, u32[]{:S(2)}) async-start(f32[16,192,128]{2,1,0:T(8,128)} %maximum_maximum_fusion), calls=%async_computation | async-start | bytes 3145728 | tf_op jit(solution)/shard_map/all_to_all | solution.py:170
  26.6 0.2 select_reduce_fusion
  26.8 37.9 %all-to-all-done = f32[16,192,128]{2,1,0:T(8,128)S(1)} async-done(((f32[16,192,128]{2,1,0:T(8,128)}), f32[16,192,128]{2,1,0:T(8,128)S(1)}, u32[]{:S(2)}, u32[]{:S(2)}) %all-to-all-start) | async-done | bytes 1572896 | tf_op jit(solution)/shard_map/all_to_all | solution.py:170
  64.8 0.6 gather_fusion
  65.7 1.0 slice.1071
  66.7 1.2 reshape.129
  68.0 1.4 %reshape.131 = f32[64,28,12]{2,1,0:T(8,128)} reshape(f32[16,1344]{1,0:T(8,128)S(1)} %bitcast.293) | data formatting | bytes 172032 | tf_op jit(solution)/shard_map/reshape | solution.py:174
  69.5 1.1 copy-done.1
  70.7 0.2 multiply_reduce_fusion
  70.9 10.2 %multiply_reduce_fusion.1 = (f32[16,128]{1,0:T(8,128)S(1)}, f32[16,128]{1,0:T(8,128)S(1)}, f32[16,128]{1,0:T(8,128)S(1)}, f32[16,128]{1,0:T(8,128)S(1)}, f32[16,...) fusion(f32[64,28,140]{2,1,0:T(8,128)S(1)} %constant_dynamic-upd, ...), kind=kLoop, calls=%fused_computation.15 | loop fusion | flops 21458944 | bytes 35274752 | tf_op jit(solution)/shard_map/reduce_sum | solution.py:67
  81.1 1.3 %multiply_reduce_fusion.56 = (f32[16,128]{1,0:T(8,128)S(1)}, f32[16,128]{1,0:T(8,128)S(1)}, f32[16,128]{1,0:T(8,128)S(1)}, f32[16,128]{1,0:T(8,128)S(1)}, f32[16...) fusion(f32[64,16,128]{2,1,0:T(8,128)S(1)} %get-tuple-element.69, ...), kind=kLoop, calls=%fused_computation.70 | loop fusion | flops 2600960 | bytes 5849088 | tf_op jit(solution)/shard_map/reduce_sum | solution.py:67
  82.4 2.6 %multiply_reduce_fusion.19 = (f32[16,128]{1,0:T(8,128)S(1)}, f32[16,128]{1,0:T(8,128)S(1)}, f32[16,128]{1,0:T(8,128)S(1)}, f32[16,128]{1,0:T(8,128)S(1)}, f32[16...) fusion(f32[64,16,128]{2,1,0:T(8,128)S(1)} %get-tuple-element.69, ...), kind=kLoop, calls=%fused_computation.33 | loop fusion | flops 4681728 | bytes 10108928 | tf_op jit(solution)/shard_map/reduce_sum | solution.py:67
  85.0 2.6 %multiply_reduce_fusion.38 = (f32[16,128]{1,0:T(8,128)S(1)}, f32[16,128]{1,0:T(8,128)S(1)}, f32[16,128]{1,0:T(8,128)S(1)}, f32[16,128]{1,0:T(8,128)S(1)}, f32[16...) fusion(f32[64,16,128]{2,1,0:T(8,128)S(1)} %get-tuple-element.69, ...), kind=kLoop, calls=%fused_computation.52 | loop fusion | flops 4681728 | bytes 10108928 | tf_op jit(solution)/shard_map/reduce_sum | solution.py:67
  87.7 0.2 fusion.4
  88.6 0.6 gather_fusion.1
  89.4 1.1 pad_maximum_fusion
  90.4 32.2 %exchange_1.1 = f32[16,128,128]{2,1,0:T(8,128)} custom-call(f32[16,128,128]{2,1,0:T(8,128)} %bitcast.284), custom_call_target="tpu_custom_call" | custom-call | tf_op jit(solution)/shard_map/exchange_1/pallas_call | solution.py:112
  122.6 1.3 %fusion.5 = (f32[16,4,16,128]{3,2,1,0:T(8,128)S(1)}, f32[16,4,16,128]{3,2,1,0:T(8,128)S(1)}) fusion(f32[16,8,16,128]{3,2,1,0:T(8,128)} %bitcast.283), kind=kLoop, calls=%fused_computation.312 | loop fusion | bytes 2097152 | tf_op jit(solution)/shard_map/slice | solution.py:188
  123.9 0.3 copy.21
  124.3 1.0 reshape.139
  125.3 0.3 copy.22
  125.6 1.0 reshape.137
  (150 shorter events, 3.2 us)
Async XLA Ops:
  1.5 9.9 %copy-start = (f32[4,64,512]{2,1,0:T(8,128)S(1)}, f32[4,64,512]{2,1,0:T(8,128)}, u32[]{:S(2)}) copy-start(f32[4,64,512]{2,1,0:T(8,128)} %param.7) | copy-start | bytes 1572868
  1.5 9.6 %collective-permute-start.1 = (f32[4,6,512]{2,1,0:T(8,128)S(1)}, f32[4,6,512]{2,1,0:T(8,128)S(1)}, u32[]{:S(2)}, u32[]{:S(2)}) collective-permute-start(f32[4,6,512]{2,1,0:T(8,128)S(1)} %get-tuple-element.171), channel_id=1, source_target_pairs={{16,0},{32,16},{48,32},{64,48},{80,64},{96,80},{112,96},{128,112},... | collective-permute-start | bytes 147464 | tf_op jit(solution)/shard_map/ppermute | solution.py:24
  6.8 4.6 %collective-permute-start = (f32[4,6,512]{2,1,0:T(8,128)S(1)}, f32[4,6,512]{2,1,0:T(8,128)S(1)}, u32[]{:S(2)}, u32[]{:S(2)}) collective-permute-start(f32[4,6,512]{2,1,0:T(8,128)S(1)} %get-tuple-element.172), channel_id=1, source_target_pairs={{0,16},{16,32},{32,48},{48,64},{64,80},{80,96},{96,112},{112,128},... | collective-permute-start | bytes 147464 | tf_op jit(solution)/shard_map/ppermute | solution.py:22
  16.2 10.4 %copy-start.2 = (s32[64,2]{0,1:T(2,128)S(1)}, s32[64,2]{0,1:T(2,128)}, u32[]{:S(2)}) copy-start(s32[64,2]{0,1:T(2,128)} %param.9) | copy-start | bytes 1540
  16.2 10.4 %copy-start.3 = (s32[64]{0:T(128)S(1)}, s32[64]{0:T(128)}, u32[]{:S(2)}) copy-start(s32[64]{0:T(128)} %constant.30.clone) | copy-start | bytes 772
  16.2 10.4 %copy-start.4 = (s32[64]{0:T(128)S(1)}, s32[64]{0:T(128)}, u32[]{:S(2)}) copy-start(s32[64]{0:T(128)} %constant.29.clone) | copy-start | bytes 772
  16.2 48.6 %all-to-all-start = ((f32[16,192,128]{2,1,0:T(8,128)}), f32[16,192,128]{2,1,0:T(8,128)S(1)}, u32[]{:S(2)}, u32[]{:S(2)}) async-start(f32[16,192,128]{2,1,0:T(8,128)} %maximum_maximum_fusion), calls=%async_computation | async-start | bytes 3145728 | tf_op jit(solution)/shard_map/all_to_all | solution.py:170
  69.4 1.2 copy-start.1

commit v7 on v6

--- a/solution.py
+++ b/solution.py
@@ -167,7 +167,7 @@
         ],
         axis=1,
     )
-    got = lax.all_to_all(send, "tm", 0, 0, tiled=True)
+    got = exchange(send, n, 0)
     rt_main = got[:, :main_rows].reshape(frames_all, hh, lanes)
     wt = got[:, main_rows : main_rows + w_rows].reshape(cycle, h, w)
     rt_rest = got[:, main_rows + w_rows : used].reshape(n, rest_rows * lanes)[:, :rest_len]

time: 127 us -> 123 us (0.969); the launches traced: 127 us -> 121 us
  Pallas kernels: 32.2 us -> 74 us
  waiting for transfers between devices: 37.9 us -> 0.01 us
  starting transfers between devices: 17.5 us -> 7.16 us
    pallas_call x1 -> x2, Pallas kernels: 32.2 us -> 74 us  [exchange(): pl.pallas_call(functools.partial(exchange_kernel, n), out_shape=jax.Shape...]
    all_to_all x1 -> x0, waiting for transfers between devices: 37.9 us -> none  [on_device(): got = lax.all_to_all(send, 'tm', 0, 0, tiled=True)]
    all_to_all x1 -> x0, starting transfers between devices: 10.4 us -> none  [on_device(): got = lax.all_to_all(send, 'tm', 0, 0, tiled=True)]
    unnamed x91 -> x85, local copies, waits for them, and re-layouts: 2.65 us -> 2.63 us
  transfers between devices with their start and end apart: 3 -> 2, of which waited for: 1 -> 0; matrix products, arithmetic and copies ran while one was open for 2% -> 4% of each run, Pallas kernels for 0% -> 0%
where the time goes in v7:
time: 123 us; the launch traced here: 121 us
  Pallas kernels  74 us (60%)
  other arithmetic  21.8 us (18%)
  local copies, waits for them, and re-layouts  16.2 us (13%)
  starting transfers between devices  7.16 us (6%)
  between operations  1.82 us (1%)
    pallas_call x2, Pallas kernels, exchange(): pl.pallas_call(functools.partial(exchange_kernel, n), out_shape=jax.Shape...  74 us
    reduce_sum x4, other arithmetic, tile_compute(): jnp.sum(error * rt[:, HALO + dy:HALO + dy + h, HALO + dx:HALO + dx + w],...  16.9 us
    ppermute x1, starting transfers between devices, with_halo(): lax.ppermute(head, axis, [((i + 1) % count, i) for i in range(ends)])  5.24 us
    unnamed x85, local copies, waits for them, and re-layouts  2.63 us
  transfers between devices with their start and end apart: 2, of which 0 were waited for; matrix products, arithmetic and copies ran while one was open for 4% of the time, Pallas kernels for 0%

profile of v7, /device:TPU:1, one launch (start us, length us, event | category | flops | bytes accessed | tf_op | source)
XLA Modules:
  0.0 121.0 jit_solution(2252708960961685662)
XLA Ops:
  0.6 0.9 fusion.11
  1.5 5.2 %collective-permute-start.1 = (f32[4,6,512]{2,1,0:T(8,128)S(1)}, f32[4,6,512]{2,1,0:T(8,128)S(1)}, u32[]{:S(2)}, u32[]{:S(2)}) collective-permute-start(f32[4,6,512]{2,1,0:T(8,128)S(1)} %get-tuple-element.171), channel_id=1, source_target_pairs={{16,0},{32,16},{48,32},{64,48},{80,64},{96,80},{112,96},{128,112},... | collective-permute-start | bytes 147464 | tf_op jit(solution)/shard_map/ppermute | solution.py:24
  6.8 1.9 %collective-permute-start = (f32[4,6,512]{2,1,0:T(8,128)S(1)}, f32[4,6,512]{2,1,0:T(8,128)S(1)}, u32[]{:S(2)}, u32[]{:S(2)}) collective-permute-start(f32[4,6,512]{2,1,0:T(8,128)S(1)} %get-tuple-element.172), channel_id=1, source_target_pairs={{0,16},{16,32},{32,48},{48,64},{64,80},{80,96},{96,112},{112,128},... | collective-permute-start | bytes 147464 | tf_op jit(solution)/shard_map/ppermute | solution.py:22
  8.7 0.8 slice_bitcast_fusion.65
  9.5 0.9 select_reduce_fusion
  10.4 1.1 constant_dynamic-update-slice_fusion.1
  11.5 1.2 %reshape.125 = f32[4,4,16,4,128]{4,3,2,1,0:T(4,128)S(1)} reshape(f32[4,64,512]{2,1,0:T(8,128)} %param.8) | data formatting | bytes 1048576 | tf_op jit(solution)/shard_map/reshape | solution.py:152
  13.1 0.3 select_maximum_fusion
  13.9 0.2 pad_maximum_fusion.4
  14.3 0.2 fusion.10
  16.0 0.2 stack.330
  16.4 1.4 %maximum_maximum_fusion.x_ref = f32[16,192,128]{2,1,0:T(8,128)} fusion(f32[16,11,128]{2,1,0:T(8,128)S(1)} %reshape.127, f32[16,64,128]{2,1,0:T(8,128)S(1)} %bitcast.289, f32[16,112,128]{2,1,0:T(8,128)S(1)} %constant_dynamic-update-slice_fusion.2, f32[192]{0:T(256)S(1)} %pad.15.clone), kind=kLoop, calls=%fused_computation.3 | loop fusion | flops 1179648 | bytes 3105536 | tf_op jit(solution)/shard_map/concatenate | solution.py:159
  17.9 38.5 %exchange_0.1 = f32[16,192,128]{2,1,0:T(8,128)} custom-call(f32[16,192,128]{2,1,0:T(8,128)} %maximum_maximum_fusion.x_ref), custom_call_target="tpu_custom_call" | custom-call | tf_op jit(solution)/shard_map/exchange_0/pallas_call | solution.py:112
  56.3 1.1 slice.851
  57.4 0.6 gather_fusion
  58.4 0.3 slice-done.1
  58.8 1.4 %reshape.131 = f32[64,28,12]{2,1,0:T(8,128)} reshape(f32[16,1344]{1,0:T(8,128)S(1)} %bitcast.293) | data formatting | bytes 172032 | tf_op jit(solution)/shard_map/reshape | solution.py:174
  60.2 1.1 copy-done.1
  61.5 0.2 multiply_reduce_fusion
  61.7 10.4 %multiply_reduce_fusion.1 = (f32[16,128]{1,0:T(8,128)S(1)}, f32[16,128]{1,0:T(8,128)S(1)}, f32[16,128]{1,0:T(8,128)S(1)}, f32[16,128]{1,0:T(8,128)S(1)}, f32[16,...) fusion(f32[64,28,140]{2,1,0:T(8,128)S(1)} %constant_dynamic-upd, ...), kind=kLoop, calls=%fused_computation.15 | loop fusion | flops 21458944 | bytes 35274752 | tf_op jit(solution)/shard_map/reduce_sum | solution.py:67
  72.1 1.3 %multiply_reduce_fusion.56 = (f32[16,128]{1,0:T(8,128)S(1)}, f32[16,128]{1,0:T(8,128)S(1)}, f32[16,128]{1,0:T(8,128)S(1)}, f32[16,128]{1,0:T(8,128)S(1)}, f32[16...) fusion(f32[64,16,128]{2,1,0:T(8,128)S(1)} %get-tuple-element.69, ...), kind=kLoop, calls=%fused_computation.70 | loop fusion | flops 2600960 | bytes 5849088 | tf_op jit(solution)/shard_map/reduce_sum | solution.py:67
  73.4 2.6 %multiply_reduce_fusion.19 = (f32[16,128]{1,0:T(8,128)S(1)}, f32[16,128]{1,0:T(8,128)S(1)}, f32[16,128]{1,0:T(8,128)S(1)}, f32[16,128]{1,0:T(8,128)S(1)}, f32[16...) fusion(f32[64,16,128]{2,1,0:T(8,128)S(1)} %get-tuple-element.69, ...), kind=kLoop, calls=%fused_computation.33 | loop fusion | flops 4681728 | bytes 10108928 | tf_op jit(solution)/shard_map/reduce_sum | solution.py:67
  76.0 2.6 %multiply_reduce_fusion.38 = (f32[16,128]{1,0:T(8,128)S(1)}, f32[16,128]{1,0:T(8,128)S(1)}, f32[16,128]{1,0:T(8,128)S(1)}, f32[16,128]{1,0:T(8,128)S(1)}, f32[16...) fusion(f32[64,16,128]{2,1,0:T(8,128)S(1)} %get-tuple-element.69, ...), kind=kLoop, calls=%fused_computation.52 | loop fusion | flops 4681728 | bytes 10108928 | tf_op jit(solution)/shard_map/reduce_sum | solution.py:67
  78.6 0.2 fusion.4
  79.5 0.6 gather_fusion.1
  80.3 1.1 pad_maximum_fusion
  81.4 35.6 %exchange_1.1 = f32[16,128,128]{2,1,0:T(8,128)} custom-call(f32[16,128,128]{2,1,0:T(8,128)} %bitcast.286), custom_call_target="tpu_custom_call" | custom-call | tf_op jit(solution)/shard_map/exchange_1/pallas_call | solution.py:112
  117.0 1.3 %fusion.5 = (f32[16,4,16,128]{3,2,1,0:T(8,128)S(1)}, f32[16,4,16,128]{3,2,1,0:T(8,128)S(1)}) fusion(f32[16,8,16,128]{3,2,1,0:T(8,128)} %bitcast.285), kind=kLoop, calls=%fused_computation.312 | loop fusion | bytes 2097152 | tf_op jit(solution)/shard_map/slice | solution.py:188
  118.3 0.3 copy.20
  118.6 1.0 reshape.139
  119.6 0.3 copy.21
  120.0 1.0 reshape.137
  (144 shorter events, 3.2 us)
Async XLA Ops:
  1.5 11.6 %copy-start = (f32[4,64,512]{2,1,0:T(8,128)S(1)}, f32[4,64,512]{2,1,0:T(8,128)}, u32[]{:S(2)}) copy-start(f32[4,64,512]{2,1,0:T(8,128)} %param.7) | copy-start | bytes 1572868
  1.5 11.3 %collective-permute-start.1 = (f32[4,6,512]{2,1,0:T(8,128)S(1)}, f32[4,6,512]{2,1,0:T(8,128)S(1)}, u32[]{:S(2)}, u32[]{:S(2)}) collective-permute-start(f32[4,6,512]{2,1,0:T(8,128)S(1)} %get-tuple-element.171), channel_id=1, source_target_pairs={{16,0},{32,16},{48,32},{64,48},{80,64},{96,80},{112,96},{128,112},... | collective-permute-start | bytes 147464 | tf_op jit(solution)/shard_map/ppermute | solution.py:24
  6.8 6.3 %collective-permute-start = (f32[4,6,512]{2,1,0:T(8,128)S(1)}, f32[4,6,512]{2,1,0:T(8,128)S(1)}, u32[]{:S(2)}, u32[]{:S(2)}) collective-permute-start(f32[4,6,512]{2,1,0:T(8,128)S(1)} %get-tuple-element.172), channel_id=1, source_target_pairs={{0,16},{16,32},{32,48},{48,64},{64,80},{80,96},{96,112},{112,128},... | collective-permute-start | bytes 147464 | tf_op jit(solution)/shard_map/ppermute | solution.py:22
  57.4 0.9 slice-start
  57.4 1.2 %slice-start.1 = ((f32[16,192,128]{2,1,0:T(8,128)}), f32[16,112,128]{2,1,0:T(8,128)S(1)}, s32[]{:S(2)}) async-start(f32[16,192,128]{2,1,0:T(8,128)} %exchange_0.1), calls=%async_computation.1 | async-start | bytes 1835008 | tf_op jit(solution)/shard_map/slice | solution.py:171
  60.2 1.2 %copy-start.1 = (f32[64,28,12]{2,1,0:T(8,128)S(1)}, f32[64,28,12]{2,1,0:T(8,128)}, u32[]{:S(2)}) copy-start(f32[64,28,12]{2,1,0:T(8,128)} %reshape.131) | copy-start | bytes 258052

commit v8 on v7

--- a/solution.py
+++ b/solution.py
@@ -78,45 +78,101 @@
     return error, new_weight
 
 
-def exchange_kernel(n, x_ref, o_ref, send_sem, recv_sem, local_sem):
+def exchange_kernel(
+    n, nz, x_ref, o_ref, relay, send_sem, recv_sem, hop_send, hop_recv, on_send, on_recv, local_sem
+):
+    nx = n // nz
     me = lax.axis_index("tm")
     row = lax.axis_index("rows")
+    xi, zi = me // nz, me % nz
     mesh_id = pl.DeviceIdType.MESH
+    rows = x_ref.shape[1]
+    half = rows // 2
+    far = nz // 2 if nz % 2 == 0 and nz > 2 else -1
+
+    def peer(dx, dz):
+        return lax.rem(xi + dx, nx) * nz + lax.rem(zi + dz, nz)
+
     barrier = pltpu.get_barrier_semaphore()
     for step in range(1, n):
-        peer = lax.rem(me + step, n)
-        pl.semaphore_signal(barrier, inc=1, device_id=(row, peer), device_id_type=mesh_id)
+        pl.semaphore_signal(
+            barrier, inc=1, device_id=(row, lax.rem(me + step, n)), device_id_type=mesh_id
+        )
     pl.semaphore_wait(barrier, n - 1)
+
     local = pltpu.make_async_copy(x_ref.at[me], o_ref.at[me], local_sem)
     local.start()
-    copies = []
-    for step in range(1, n):
-        peer = lax.rem(me + step, n)
-        copy = pltpu.make_async_remote_copy(
-            src_ref=x_ref.at[peer],
-            dst_ref=o_ref.at[me],
-            send_sem=send_sem.at[step],
-            recv_sem=recv_sem.at[step],
-            device_id=(row, peer),
+    direct = []
+    for dx in range(nx):
+        for dz in range(nz):
+            if (dx, dz) == (0, 0) or dz == far:
+                continue
+            slot = dx * nz + dz
+            copy = pltpu.make_async_remote_copy(
+                src_ref=x_ref.at[peer(dx, dz)],
+                dst_ref=o_ref.at[me],
+                send_sem=send_sem.at[slot],
+                recv_sem=recv_sem.at[slot],
+                device_id=(row, peer(dx, dz)),
+                device_id_type=mesh_id,
+            )
+            copy.start()
+            direct.append(copy)
+    hops = []
+    if far > 0:
+        for side, dz in enumerate((1, nz - 1)):
+            for dx in range(nx):
+                slot = side * nx + dx
+                copy = pltpu.make_async_remote_copy(
+                    src_ref=x_ref.at[peer(dx, far), pl.ds(side * half, half)],
+                    dst_ref=relay.at[side, dx],
+                    send_sem=hop_send.at[slot],
+                    recv_sem=hop_recv.at[slot],
+                    device_id=(row, peer(dx, dz)),
+                    device_id_type=mesh_id,
+                )
+                copy.start()
+                hops.append((side, dz, dx, slot, copy))
+    onward = []
+    for side, dz, dx, slot, copy in hops:
+        copy.wait_recv()
+        source = peer(-dx + nx, -dz + nz)
+        nxt = pltpu.make_async_remote_copy(
+            src_ref=relay.at[side, dx],
+            dst_ref=o_ref.at[source, pl.ds(side * half, half)],
+            send_sem=on_send.at[slot],
+            recv_sem=on_recv.at[slot],
+            device_id=(row, peer(0, dz)),
             device_id_type=mesh_id,
         )
-        copy.start()
-        copies.append(copy)
-    for copy in copies:
+        nxt.start()
+        onward.append(nxt)
+    for copy in direct:
+        copy.wait()
+    for side, dz, dx, slot, copy in hops:
+        copy.wait_send()
+    for copy in onward:
         copy.wait()
     local.wait()
 
 
 def exchange(x, n, tag):
+    nz = 4 if n % 4 == 0 else 1
+    nx = n // nz
     anywhere = pl.BlockSpec(memory_space=pl.ANY)
     return pl.pallas_call(
-        functools.partial(exchange_kernel, n),
+        functools.partial(exchange_kernel, n, nz),
         out_shape=jax.ShapeDtypeStruct(x.shape, x.dtype),
         in_specs=[anywhere],
         out_specs=anywhere,
         scratch_shapes=[
+            pltpu.VMEM((2, nx, x.shape[1] // 2, x.shape[2]), x.dtype),
             pltpu.SemaphoreType.DMA((n,)),
             pltpu.SemaphoreType.DMA((n,)),
+            pltpu.SemaphoreType.DMA((2 * nx,)),
+            pltpu.SemaphoreType.DMA((2 * nx,)),
+            pltpu.SemaphoreType.DMA((2 * nx,)),
+            pltpu.SemaphoreType.DMA((2 * nx,)),
             pltpu.SemaphoreType.DMA,
         ],
         compiler_params=pltpu.CompilerParams(collective_id=tag, has_side_effects=True),

time: 123 us -> 125 us (1.016)
  the two profiles are of different devices: /device:TPU:1 before, /device:TPU:32 now
where the time goes in v8:
time: 125 us; the launch traced here: 124 us
  Pallas kernels  77.3 us (62%)
  other arithmetic  21.8 us (17%)
  local copies, waits for them, and re-layouts  16.2 us (13%)
  starting transfers between devices  5.96 us (5%)
  between operations  1.81 us (1%)
  waiting for transfers between devices  1.37 us (1%)
    pallas_call x2, Pallas kernels, exchange(): pl.pallas_call(functools.partial(exchange_kernel, n, nz), out_shape=jax.S...  77.3 us
    reduce_sum x4, other arithmetic, tile_compute(): jnp.sum(error * rt[:, HALO + dy:HALO + dy + h, HALO + dx:HALO + dx + w],...  16.9 us
    ppermute x1, starting transfers between devices, with_halo(): lax.ppermute(head, axis, [((i + 1) % count, i) for i in range(ends)])  4.04 us
    unnamed x85, local copies, waits for them, and re-layouts  2.63 us
  transfers between devices with their start and end apart: 2, of which 1 were waited for; matrix products, arithmetic and copies ran while one was open for 3% of the time, Pallas kernels for 0%

profile of v8, /device:TPU:32, one launch (start us, length us, event | category | flops | bytes accessed | tf_op | source)
XLA Modules:
  0.0 124.4 jit_solution(865187239624695925)
XLA Ops:
  0.6 0.9 fusion.11
  1.5 4.0 %collective-permute-start.1 = (f32[4,6,512]{2,1,0:T(8,128)S(1)}, f32[4,6,512]{2,1,0:T(8,128)S(1)}, u32[]{:S(2)}, u32[]{:S(2)}) collective-permute-start(f32[4,6,512]{2,1,0:T(8,128)S(1)} %get-tuple-element.171), channel_id=1, source_target_pairs={{16,0},{32,16},{48,32},{64,48},{80,64},{96,80},{112,96},{128,112},... | collective-permute-start | bytes 147464 | tf_op jit(solution)/shard_map/ppermute | solution.py:24
  5.6 1.9 %collective-permute-start = (f32[4,6,512]{2,1,0:T(8,128)S(1)}, f32[4,6,512]{2,1,0:T(8,128)S(1)}, u32[]{:S(2)}, u32[]{:S(2)}) collective-permute-start(f32[4,6,512]{2,1,0:T(8,128)S(1)} %get-tuple-element.172), channel_id=1, source_target_pairs={{0,16},{16,32},{32,48},{48,64},{64,80},{80,96},{96,112},{112,128},... | collective-permute-start | bytes 147464 | tf_op jit(solution)/shard_map/ppermute | solution.py:22
  7.5 0.8 slice_bitcast_fusion.65
  8.3 0.9 select_reduce_fusion
  9.2 1.1 constant_dynamic-update-slice_fusion.1
  10.3 1.2 reshape.125
  11.9 1.4 %collective-permute-done = f32[4,6,512]{2,1,0:T(8,128)S(1)} collective-permute-done((f32[4,6,512]{2,1,0:T(8,128)S(1)}, f32[4,6,512]{2,1,0:T(8,128)S(1)}, u32[]{:S(2)}, u32[]{:S(2)}) %collective-permute-start) | collective-permute-done | bytes 49184 | tf_op jit(solution)/shard_map/ppermute | solution.py:22
  13.3 0.3 select_maximum_fusion
  14.0 0.2 pad_maximum_fusion.4
  14.4 0.2 fusion.10
  16.6 1.4 %maximum_maximum_fusion.x_ref = f32[16,192,128]{2,1,0:T(8,128)} fusion(f32[16,11,128]{2,1,0:T(8,128)S(1)} %reshape.127, f32[16,64,128]{2,1,0:T(8,128)S(1)} %bitcast.289, f32[16,112,128]{2,1,0:T(8,128)S(1)} %constant_dynamic-update-slice_fusion.2, f32[192]{0:T(256)S(1)} %pad.15.clone), kind=kLoop, calls=%fused_computation.3 | loop fusion | flops 1179648 | bytes 3105536 | tf_op jit(solution)/shard_map/concatenate | solution.py:215
  18.0 45.5 %exchange_0.1 = f32[16,192,128]{2,1,0:T(8,128)} custom-call(f32[16,192,128]{2,1,0:T(8,128)} %maximum_maximum_fusion.x_ref), custom_call_target="tpu_custom_call" | custom-call | tf_op jit(solution)/shard_map/exchange_0/pallas_call | solution.py:163
  63.5 1.1 slice.851
  64.7 0.6 gather_fusion
  65.6 0.3 slice-done.1
  66.0 1.4 %reshape.131 = f32[64,28,12]{2,1,0:T(8,128)} reshape(f32[16,1344]{1,0:T(8,128)S(1)} %bitcast.293) | data formatting | bytes 172032 | tf_op jit(solution)/shard_map/reshape | solution.py:230
  67.5 1.1 copy-done.1
  68.7 0.2 multiply_reduce_fusion
  68.9 10.4 %multiply_reduce_fusion.1 = (f32[16,128]{1,0:T(8,128)S(1)}, f32[16,128]{1,0:T(8,128)S(1)}, f32[16,128]{1,0:T(8,128)S(1)}, f32[16,128]{1,0:T(8,128)S(1)}, f32[16,...) fusion(f32[64,28,140]{2,1,0:T(8,128)S(1)} %constant_dynamic-upd, ...), kind=kLoop, calls=%fused_computation.15 | loop fusion | flops 21458944 | bytes 35274752 | tf_op jit(solution)/shard_map/reduce_sum | solution.py:67
  79.3 1.3 %multiply_reduce_fusion.56 = (f32[16,128]{1,0:T(8,128)S(1)}, f32[16,128]{1,0:T(8,128)S(1)}, f32[16,128]{1,0:T(8,128)S(1)}, f32[16,128]{1,0:T(8,128)S(1)}, f32[16...) fusion(f32[64,16,128]{2,1,0:T(8,128)S(1)} %get-tuple-element.69, ...), kind=kLoop, calls=%fused_computation.70 | loop fusion | flops 2600960 | bytes 5849088 | tf_op jit(solution)/shard_map/reduce_sum | solution.py:67
  80.6 2.6 %multiply_reduce_fusion.19 = (f32[16,128]{1,0:T(8,128)S(1)}, f32[16,128]{1,0:T(8,128)S(1)}, f32[16,128]{1,0:T(8,128)S(1)}, f32[16,128]{1,0:T(8,128)S(1)}, f32[16...) fusion(f32[64,16,128]{2,1,0:T(8,128)S(1)} %get-tuple-element.69, ...), kind=kLoop, calls=%fused_computation.33 | loop fusion | flops 4681728 | bytes 10108928 | tf_op jit(solution)/shard_map/reduce_sum | solution.py:67
  83.2 2.6 %multiply_reduce_fusion.38 = (f32[16,128]{1,0:T(8,128)S(1)}, f32[16,128]{1,0:T(8,128)S(1)}, f32[16,128]{1,0:T(8,128)S(1)}, f32[16,128]{1,0:T(8,128)S(1)}, f32[16...) fusion(f32[64,16,128]{2,1,0:T(8,128)S(1)} %get-tuple-element.69, ...), kind=kLoop, calls=%fused_computation.52 | loop fusion | flops 4681728 | bytes 10108928 | tf_op jit(solution)/shard_map/reduce_sum | solution.py:67
  85.8 0.2 fusion.4
  86.8 0.6 gather_fusion.1
  87.5 1.1 pad_maximum_fusion
  88.6 31.8 %exchange_1.1 = f32[16,128,128]{2,1,0:T(8,128)} custom-call(f32[16,128,128]{2,1,0:T(8,128)} %bitcast.286), custom_call_target="tpu_custom_call" | custom-call | tf_op jit(solution)/shard_map/exchange_1/pallas_call | solution.py:163
  120.4 1.3 %fusion.5 = (f32[16,4,16,128]{3,2,1,0:T(8,128)S(1)}, f32[16,4,16,128]{3,2,1,0:T(8,128)S(1)}) fusion(f32[16,8,16,128]{3,2,1,0:T(8,128)} %bitcast.285), kind=kLoop, calls=%fused_computation.312 | loop fusion | bytes 2097152 | tf_op jit(solution)/shard_map/slice | solution.py:244
  121.7 0.3 copy.20
  122.0 1.0 reshape.139
  123.0 0.3 copy.21
  123.4 1.0 reshape.137
  (144 shorter events, 3.4 us)
Async XLA Ops:
  1.5 11.8 %copy-start = (f32[4,64,512]{2,1,0:T(8,128)S(1)}, f32[4,64,512]{2,1,0:T(8,128)}, u32[]{:S(2)}) copy-start(f32[4,64,512]{2,1,0:T(8,128)} %param.7) | copy-start | bytes 1572868
  1.5 10.1 %collective-permute-start.1 = (f32[4,6,512]{2,1,0:T(8,128)S(1)}, f32[4,6,512]{2,1,0:T(8,128)S(1)}, u32[]{:S(2)}, u32[]{:S(2)}) collective-permute-start(f32[4,6,512]{2,1,0:T(8,128)S(1)} %get-tuple-element.171), channel_id=1, source_target_pairs={{16,0},{32,16},{48,32},{64,48},{80,64},{96,80},{112,96},{128,112},... | collective-permute-start | bytes 147464 | tf_op jit(solution)/shard_map/ppermute | solution.py:24
  5.6 7.7 %collective-permute-start = (f32[4,6,512]{2,1,0:T(8,128)S(1)}, f32[4,6,512]{2,1,0:T(8,128)S(1)}, u32[]{:S(2)}, u32[]{:S(2)}) collective-permute-start(f32[4,6,512]{2,1,0:T(8,128)S(1)} %get-tuple-element.172), channel_id=1, source_target_pairs={{0,16},{16,32},{32,48},{48,64},{64,80},{80,96},{96,112},{112,128},... | collective-permute-start | bytes 147464 | tf_op jit(solution)/shard_map/ppermute | solution.py:22
  64.6 0.9 slice-start
  64.6 1.2 %slice-start.1 = ((f32[16,192,128]{2,1,0:T(8,128)}), f32[16,112,128]{2,1,0:T(8,128)S(1)}, s32[]{:S(2)}) async-start(f32[16,192,128]{2,1,0:T(8,128)} %exchange_0.1), calls=%async_computation.1 | async-start | bytes 1835008 | tf_op jit(solution)/shard_map/slice | solution.py:227
  67.4 1.2 copy-start.1

commit v9 on v7

--- a/solution.py
+++ b/solution.py
@@ -139,20 +139,19 @@
     a, b = tile_split(n, rows_dev, cols)
     h, w = rows_dev // a, cols // b
 
-    extended = with_halo(residual, (("rows", 1),), HALO)
-    padded = jnp.pad(extended, ((0, 0), (0, 0), (HALO, HALO)))
-    hh, ww = h + 2 * HALO, w + 2 * HALO
+    padded = jnp.pad(residual, ((0, 0), (0, 0), (HALO, HALO)))
+    ww = w + 2 * HALO
     lanes = 128
     spare = ww - lanes
     tiles = [(i, j) for i in range(a) for j in range(b)]
-    main = jnp.stack([padded[:, i * h : i * h + hh, j * w : j * w + lanes] for i, j in tiles])
+    main = jnp.stack([padded[:, i * h : (i + 1) * h, j * w : j * w + lanes] for i, j in tiles])
     rest = jnp.stack(
-        [padded[:, i * h : i * h + hh, j * w + lanes : j * w + ww] for i, j in tiles]
+        [padded[:, i * h : (i + 1) * h, j * w + lanes : j * w + ww] for i, j in tiles]
     )
     w_tiles = cycle_weight.reshape(k_dev, a, h, b, w).transpose(1, 3, 0, 2, 4)
-    main_rows = frames_dev * hh
+    main_rows = frames_dev * h
     w_rows = k_dev * h
-    rest_len = frames_dev * hh * spare
+    rest_len = frames_dev * h * spare
     rest_rows = -(-rest_len // lanes)
     used = main_rows + w_rows + rest_rows
     total = -(-used // 8) * 8
@@ -168,10 +167,27 @@
         axis=1,
     )
     got = exchange(send, n, 0)
-    rt_main = got[:, :main_rows].reshape(frames_all, hh, lanes)
+    core_main = got[:, :main_rows].reshape(frames_all, h, lanes)
     wt = got[:, main_rows : main_rows + w_rows].reshape(cycle, h, w)
-    rt_rest = got[:, main_rows + w_rows : used].reshape(n, rest_rows * lanes)[:, :rest_len]
-    rt = jnp.concatenate([rt_main, rt_rest.reshape(frames_all, hh, spare)], axis=2)
+    core_rest = got[:, main_rows + w_rows : used].reshape(n, rest_rows * lanes)[:, :rest_len]
+    core = jnp.concatenate([core_main, core_rest.reshape(frames_all, h, spare)], axis=2)
+
+    bands = lax.axis_size("rows")
+    down, up = [], []
+    for r in range(bands):
+        for m in range(n):
+            i, j = m // b, m % b
+            if i < a - 1:
+                down.append((r * n + m, r * n + m + b))
+            elif r < bands - 1:
+                down.append((r * n + m, (r + 1) * n + j))
+            if i > 0:
+                up.append((r * n + m, r * n + m - b))
+            elif r > 0:
+                up.append((r * n + m, (r - 1) * n + (a - 1) * b + j))
+    above = lax.ppermute(core[:, h - HALO :], ("rows", "tm"), down)
+    below = lax.ppermute(core[:, :HALO], ("rows", "tm"), up)
+    rt = jnp.concatenate([above, core, below], axis=1)
 
     error_t, new_t = tile_compute(rt, wt, order, place, points, h, w, frames_all, cycle)
 

time: 123 us -> 127 us (1.033); the launches traced: 121 us -> 126 us
  other arithmetic: 21.8 us -> 27.3 us
  waiting for transfers between devices: 0.01 us -> 4.47 us
  local copies, waits for them, and re-layouts: 16.2 us -> 12.8 us
  Pallas kernels: 74 us -> 72.6 us
    ppermute x2, waiting for transfers between devices: 0.01 us -> 4.47 us  [the longest x1 4.47 us: on_device(): above = lax.ppermute(core[:, h - HALO:], ('rows', 'tm'), down)]
    concatenate x1 -> x2, other arithmetic: 0.33 us -> 2.33 us  [the longest x1 1.45 us: on_device(): rt = jnp.concatenate([above, core, below], axis=1)]
    reduce_sum x4 -> x5, other arithmetic: 16.9 us -> 18.7 us  [tile_compute(): jnp.sum(error * rt[:, HALO + dy:HALO + dy + h, HALO + dx:HALO + dx + w],...]
    reshape x3 -> x0, local copies, waits for them, and re-layouts: 1.49 us -> none  [the longest x1 1.4 us: on_device(): rt_rest.reshape(frames_all, hh, spare)]
    pallas_call x2, Pallas kernels: 74 us -> 72.6 us  [exchange(): pl.pallas_call(functools.partial(exchange_kernel, n), out_shape=jax.Shape...]
    reduce_sum x1, other arithmetic: 0.22 us -> 1.63 us  [tile_compute(): squares = jnp.sum(rt * rt, axis=0)]
    unnamed x85 -> x155, local copies, waits for them, and re-layouts: 2.63 us -> 1.25 us
  transfers between devices with their start and end apart: 2 -> 2, of which waited for: 0 -> 1; matrix products, arithmetic and copies ran while one was open for 4% -> 3% of each run, Pallas kernels for 0% -> 0%
where the time goes in v9:
time: 127 us; the launch traced here: 126 us
  Pallas kernels  72.6 us (57%)
  other arithmetic  27.3 us (21%)
  local copies, waits for them, and re-layouts  12.8 us (10%)
  starting transfers between devices  7.03 us (6%)
  waiting for transfers between devices  4.47 us (4%)
  between operations  2.16 us (2%)
    pallas_call x2, Pallas kernels, exchange(): pl.pallas_call(functools.partial(exchange_kernel, n), out_shape=jax.Shape...  72.6 us
    reduce_sum x5, other arithmetic, tile_compute(): jnp.sum(error * rt[:, HALO + dy:HALO + dy + h, HALO + dx:HALO + dx + w],...  18.7 us
    ppermute x1, starting transfers between devices, on_device(): below = lax.ppermute(core[:, :HALO], ('rows', 'tm'), up)  4.82 us
    ppermute x1, waiting for transfers between devices, on_device(): above = lax.ppermute(core[:, h - HALO:], ('rows', 'tm'), down)  4.47 us
  transfers between devices with their start and end apart: 2, of which 1 were waited for; matrix products, arithmetic and copies ran while one was open for 3% of the time, Pallas kernels for 0%

profile of v9, /device:TPU:1, one launch (start us, length us, event | category | flops | bytes accessed | tf_op | source)
XLA Modules:
  0.0 126.3 jit_solution(15754835137962522641)
XLA Ops:
  0.6 1.5 %fusion.14 = (f32[4,16,128]{2,1,0:T(8,128)S(1)}, f32[4,16,128]{2,1,0:T(8,128)S(1)}, f32[4,16,128]{2,1,0:T(8,128)S(1)}, f32[4,16,128]{2,1,0:T(8,128)S(1)}, f32[4,...) fusion(f32[4,64,512]{2,1,0:T(8,128)} %param.7), kind=kLoop, calls=%fused_computation.341 | loop fusion | bytes 1441792 | tf_op jit(solution)/shard_map/slice | solution.py:147
  2.2 0.2 pad_slice_fusion.10
  4.7 1.1 maximum_maximum_fusion.1.x_ref
  5.9 33.4 %exchange_0.1 = f32[16,136,128]{2,1,0:T(8,128)} custom-call(f32[16,136,128]{2,1,0:T(8,128)} %maximum_maximum_fusion.1.x_ref), custom_call_target="tpu_custom_call" | custom-call | tf_op jit(solution)/shard_map/exchange_0/pallas_call | solution.py:112
  39.3 1.3 %fusion.12 = (f32[16,64,128]{2,1,0:T(8,128)S(1)}, f32[16,64,128]{2,1,0:T(8,128)S(1)}) fusion(f32[16,136,128]{2,1,0:T(8,128)} %exchange_0.1), kind=kLoop, calls=%fused_computation.339 | loop fusion | bytes 2097152 | tf_op jit(solution)/shard_map/slice | solution.py:171
  40.7 0.5 reshape_reshape.3
  41.2 0.9 fusion.4
  42.1 2.2 %collective-permute-start = (f32[64,6,140]{2,1,0:T(8,128)}, f32[64,6,140]{2,1,0:T(8,128)S(1)}, u32[]{:S(2)}, u32[]{:S(2)}) collective-permute-start(f32[64,6,140]{2,1,0:T(8,128)} %get-tuple-element.76), channel_id=1, source_target_pairs={{0,4},{1,5},{2,6},{3,7},{4,8},{5,9},{6,10},{7,11},{8,12},{9,13},{1... | collective-permute-start | bytes 645128 | tf_op jit(solution)/shard_map/ppermute | solution.py:188
  44.3 4.8 %collective-permute-start.1 = (f32[64,6,140]{2,1,0:T(8,128)S(1)}, f32[64,6,140]{2,1,0:T(8,128)}, u32[]{:S(2)}, u32[]{:S(2)}) collective-permute-start(f32[64,6,140]{2,1,0:T(8,128)S(1)} %get-tuple-element.77), channel_id=1, source_target_pairs={{4,0},{5,1},{6,2},{7,3},{8,4},{9,5},{10,6},{11,7},{12,8},{13,9},{1... | collective-permute-start | bytes 645128 | tf_op jit(solution)/shard_map/ppermute | solution.py:189
  49.4 0.6 compare_select_fusion
  50.0 0.6 gather_fusion
  50.9 0.7 slice_bitcast_fusion.63
  51.5 0.6 pad_clamp_fusion
  52.1 0.6 compare_and_fusion.1
  52.7 4.5 %collective-permute-done = f32[64,6,140]{2,1,0:T(8,128)S(1)} collective-permute-done((f32[64,6,140]{2,1,0:T(8,128)}, f32[64,6,140]{2,1,0:T(8,128)S(1)}, u32[]{:S(2)}, u32[]{:S(2)}) %collective-permute-start) | collective-permute-done | bytes 215072 | tf_op jit(solution)/shard_map/ppermute | solution.py:188
  57.2 0.8 copy-done.3
  58.0 1.5 %maximum_maximum_fusion = (f32[64,22,140]{2,1,0:T(8,128)S(1)}, f32[64,22,140]{2,1,0:T(8,128)S(1)}) fusion(f32[64,16,12]{2,1,0:T(8,128)S(1)} %reshape_reshape.3, f32[64,16,128]{2,1,0:T(8,128)S(1)} %bitcast.326, f32[64,6,140]{2,1,0:T(8,128)} %copy-done.3, f32[64,6,140]{2,1,0:T(8,128)} %collective-permute-done.1), kind=kLoop, calls=%fused_computation.14 | loop fusion | flops 788480 | bytes 2580480 | tf_op jit(solution)/shard_map/concatenate | solution.py:190
  59.5 11.8 %multiply_reduce_fusion = (f32[16,128]{1,0:T(8,128)}, f32[16,128]{1,0:T(8,128)}, f32[16,128]{1,0:T(8,128)}, f32[16,128]{1,0:T(8,128)}, f32[16,128]{1,0:T(8,128)}...) fusion(f32[64,22,140]{2,1,0:T(8,128)S(1)} %get-tuple-element.75, ...), kind=kLoop, calls=%fused_computation.37 | loop fusion | flops 21983232 | bytes 33226752 | tf_op jit(solution)/shard_map/reduce_sum | solution.py:67
  71.3 1.7 %multiply_reduce_fusion.18 = (f32[16,128]{1,0:T(8,128)S(1)}, f32[16,128]{1,0:T(8,128)S(1)}, f32[16,128]{1,0:T(8,128)S(1)}, f32[16,128]{1,0:T(8,128)S(1)}, f32[16...) fusion(f32[64,16,128]{2,1,0:T(8,128)S(1)} %get-tuple-element.69, ...), kind=kLoop, calls=%fused_computation.55 | loop fusion | flops 3121152 | bytes 6914048 | tf_op jit(solution)/shard_map/reduce_sum | solution.py:67
  73.0 0.9 multiply_reduce_fusion.30
  73.9 2.6 %multiply_reduce_fusion.34 = (f32[16,128]{1,0:T(8,128)S(1)}, f32[16,128]{1,0:T(8,128)S(1)}, f32[16,128]{1,0:T(8,128)S(1)}, f32[16,128]{1,0:T(8,128)S(1)}, f32[16...) fusion(f32[64,16,128]{2,1,0:T(8,128)S(1)} %get-tuple-element.69, ...), kind=kLoop, calls=%fused_computation.71 | loop fusion | flops 4681728 | bytes 10108928 | tf_op jit(solution)/shard_map/reduce_sum | solution.py:67
  76.5 1.7 %multiply_reduce_fusion.52 = (f32[16,128]{1,0:T(8,128)S(1)}, f32[16,128]{1,0:T(8,128)S(1)}, f32[16,128]{1,0:T(8,128)S(1)}, f32[16,128]{1,0:T(8,128)S(1)}, f32[16...) fusion(f32[64,16,128]{2,1,0:T(8,128)S(1)} %get-tuple-element.69, ...), kind=kLoop, calls=%fused_computation.89 | loop fusion | flops 3121152 | bytes 6914048 | tf_op jit(solution)/shard_map/reduce_sum | solution.py:67
  78.4 1.6 %fusion = f32[28,140]{1,0:T(8,128)S(1)} fusion(f32[64,6,140]{2,1,0:T(8,128)} %collective-permute-done.1, f32[64,16,12]{2,1,0:T(8,128)S(1)} %reshape_reshape.3, f32[64,16,128]{2,1,0:T(8,128)S(1)} %bitcast.329, f32[64,6,140]{2,1,0:T(8,128)S(1)} %copy-done.4), kind=kLoop, calls=%fused_computation.3 | loop fusion | flops 1250480 | bytes 1019200 | tf_op jit(solution)/shard_map/reduce_sum | solution.py:71
  80.0 0.2 fusion.10
  81.1 0.8 gather_fusion.1
  82.1 1.1 pad_maximum_fusion.1
  83.1 39.2 %exchange_1.1 = f32[16,128,128]{2,1,0:T(8,128)} custom-call(f32[16,128,128]{2,1,0:T(8,128)} %bitcast.334), custom_call_target="tpu_custom_call" | custom-call | tf_op jit(solution)/shard_map/exchange_1/pallas_call | solution.py:112
  122.3 1.3 %fusion.13 = (f32[16,4,16,128]{3,2,1,0:T(8,128)S(1)}, f32[16,4,16,128]{3,2,1,0:T(8,128)S(1)}) fusion(f32[16,8,16,128]{3,2,1,0:T(8,128)} %bitcast.333), kind=kLoop, calls=%fused_computation.340 | loop fusion | bytes 2097152 | tf_op jit(solution)/shard_map/slice | solution.py:204
  123.7 0.3 copy.19
  124.0 1.0 reshape.127
  125.0 0.3 copy.18
  125.3 1.0 reshape.129
  (189 shorter events, 2.9 us)
Async XLA Ops:
  0.6 1.5 %copy-start = (f32[4,64,512]{2,1,0:T(8,128)S(1)}, f32[4,64,512]{2,1,0:T(8,128)}, u32[]{:S(2)}) copy-start(f32[4,64,512]{2,1,0:T(8,128)} %param.7) | copy-start | bytes 1572868
  0.6 3.4 %copy-start.5 = (f32[4,64,512]{2,1,0:T(8,128)S(1)}, f32[4,64,512]{2,1,0:T(8,128)}, u32[]{:S(2)}) copy-start(f32[4,64,512]{2,1,0:T(8,128)} %param.8) | copy-start | bytes 1572868
  39.3 1.4 %slice-start = ((f32[16,136,128]{2,1,0:T(8,128)}), f32[16,6,128]{2,1,0:T(8,128)S(1)}, s32[]{:S(2)}) async-start(f32[16,136,128]{2,1,0:T(8,128)} %exchange_0.1), calls=%async_computation | async-start | bytes 131072 | tf_op jit(solution)/shard_map/slice | solution.py:172
  40.6 10.0 %copy-start.1 = (f32[16,64,128]{2,1,0:T(8,128)}, f32[16,64,128]{2,1,0:T(8,128)S(1)}, u32[]{:S(2)}) copy-start(f32[16,64,128]{2,1,0:T(8,128)S(1)} %get-tuple-element.70) | copy-start | bytes 1572868
  40.6 8.5 %copy-start.27 = (s32[64,2]{0,1:T(2,128)S(1)}, s32[64,2]{0,1:T(2,128)}, u32[]{:S(2)}) copy-start(s32[64,2]{0,1:T(2,128)} %param.9) | copy-start | bytes 1540
  40.6 8.5 %copy-start.29 = (s32[64]{0:T(128)S(1)}, s32[64]{0:T(128)}, u32[]{:S(2)}) copy-start(s32[64]{0:T(128)} %constant.29.clone) | copy-start | bytes 772
  40.7 8.5 %copy-start.30 = (s32[64]{0:T(128)S(1)}, s32[64]{0:T(128)}, u32[]{:S(2)}) copy-start(s32[64]{0:T(128)} %constant.30.clone) | copy-start | bytes 772
  42.1 15.1 %collective-permute-start = (f32[64,6,140]{2,1,0:T(8,128)}, f32[64,6,140]{2,1,0:T(8,128)S(1)}, u32[]{:S(2)}, u32[]{:S(2)}) collective-permute-start(f32[64,6,140]{2,1,0:T(8,128)} %get-tuple-element.76), channel_id=1, source_target_pairs={{0,4},{1,5},{2,6},{3,7},{4,8},{5,9},{6,10},{7,11},{8,12},{9,13},{1... | collective-permute-start | bytes 645128 | tf_op jit(solution)/shard_map/ppermute | solution.py:188
  44.3 13.7 %collective-permute-start.1 = (f32[64,6,140]{2,1,0:T(8,128)S(1)}, f32[64,6,140]{2,1,0:T(8,128)}, u32[]{:S(2)}, u32[]{:S(2)}) collective-permute-start(f32[64,6,140]{2,1,0:T(8,128)S(1)} %get-tuple-element.77), channel_id=1, source_target_pairs={{4,0},{5,1},{6,2},{7,3},{8,4},{9,5},{10,6},{11,7},{12,8},{13,9},{1... | collective-permute-start | bytes 645128 | tf_op jit(solution)/shard_map/ppermute | solution.py:189
  50.6 0.9 copy-start.24
  50.7 1.5 %copy-start.26 = (s32[64]{0:T(128)S(1)}, s32[64]{0:T(128)}, u32[]{:S(2)}) copy-start(s32[64]{0:T(128)} %copy-done.25) | copy-start | bytes 772
  76.5 1.7 %copy-start.4 = (f32[64,6,140]{2,1,0:T(8,128)S(1)}, f32[64,6,140]{2,1,0:T(8,128)}, u32[]{:S(2)}) copy-start(f32[64,6,140]{2,1,0:T(8,128)} %copy-done.3) | copy-start | bytes 645124
  78.2 2.5 %copy-start.23 = (f32[16,128]{1,0:T(8,128)S(1)}, f32[16,128]{1,0:T(8,128)}, u32[]{:S(2)}) copy-start(f32[16,128]{1,0:T(8,128)} %get-tuple-element.20) | copy-start | bytes 24580
  78.2 2.6 %copy-start.22 = (f32[16,128]{1,0:T(8,128)S(1)}, f32[16,128]{1,0:T(8,128)}, u32[]{:S(2)}) copy-start(f32[16,128]{1,0:T(8,128)} %get-tuple-element.19) | copy-start | bytes 24580
  78.2 2.6 %copy-start.21 = (f32[16,128]{1,0:T(8,128)S(1)}, f32[16,128]{1,0:T(8,128)}, u32[]{:S(2)}) copy-start(f32[16,128]{1,0:T(8,128)} %get-tuple-element.18) | copy-start | bytes 24580
  78.2 2.6 %copy-start.20 = (f32[16,128]{1,0:T(8,128)S(1)}, f32[16,128]{1,0:T(8,128)}, u32[]{:S(2)}) copy-start(f32[16,128]{1,0:T(8,128)} %get-tuple-element.17) | copy-start | bytes 24580
  78.2 2.6 %copy-start.19 = (f32[16,128]{1,0:T(8,128)S(1)}, f32[16,128]{1,0:T(8,128)}, u32[]{:S(2)}) copy-start(f32[16,128]{1,0:T(8,128)} %get-tuple-element.16) | copy-start | bytes 24580
  78.3 2.6 %copy-start.18 = (f32[16,128]{1,0:T(8,128)S(1)}, f32[16,128]{1,0:T(8,128)}, u32[]{:S(2)}) copy-start(f32[16,128]{1,0:T(8,128)} %get-tuple-element.15) | copy-start | bytes 24580
  78.3 2.6 %copy-start.17 = (f32[16,128]{1,0:T(8,128)S(1)}, f32[16,128]{1,0:T(8,128)}, u32[]{:S(2)}) copy-start(f32[16,128]{1,0:T(8,128)} %get-tuple-element.14) | copy-start | bytes 24580
  78.3 2.6 %copy-start.16 = (f32[16,128]{1,0:T(8,128)S(1)}, f32[16,128]{1,0:T(8,128)}, u32[]{:S(2)}) copy-start(f32[16,128]{1,0:T(8,128)} %get-tuple-element.13) | copy-start | bytes 24580
  78.3 2.6 %copy-start.15 = (f32[16,128]{1,0:T(8,128)S(1)}, f32[16,128]{1,0:T(8,128)}, u32[]{:S(2)}) copy-start(f32[16,128]{1,0:T(8,128)} %get-tuple-element.12) | copy-start | bytes 24580
  78.3 2.6 %copy-start.14 = (f32[16,128]{1,0:T(8,128)S(1)}, f32[16,128]{1,0:T(8,128)}, u32[]{:S(2)}) copy-start(f32[16,128]{1,0:T(8,128)} %get-tuple-element.11) | copy-start | bytes 24580
  78.3 2.7 %copy-start.13 = (f32[16,128]{1,0:T(8,128)S(1)}, f32[16,128]{1,0:T(8,128)}, u32[]{:S(2)}) copy-start(f32[16,128]{1,0:T(8,128)} %get-tuple-element.10) | copy-start | bytes 24580
  78.3 2.7 %copy-start.12 = (f32[16,128]{1,0:T(8,128)S(1)}, f32[16,128]{1,0:T(8,128)}, u32[]{:S(2)}) copy-start(f32[16,128]{1,0:T(8,128)} %get-tuple-element.9) | copy-start | bytes 24580
  78.3 2.7 %copy-start.11 = (f32[16,128]{1,0:T(8,128)S(1)}, f32[16,128]{1,0:T(8,128)}, u32[]{:S(2)}) copy-start(f32[16,128]{1,0:T(8,128)} %get-tuple-element.8) | copy-start | bytes 24580
  78.3 2.7 %copy-start.10 = (f32[16,128]{1,0:T(8,128)S(1)}, f32[16,128]{1,0:T(8,128)}, u32[]{:S(2)}) copy-start(f32[16,128]{1,0:T(8,128)} %get-tuple-element.7) | copy-start | bytes 24580
  78.3 2.7 %copy-start.9 = (f32[16,128]{1,0:T(8,128)S(1)}, f32[16,128]{1,0:T(8,128)}, u32[]{:S(2)}) copy-start(f32[16,128]{1,0:T(8,128)} %get-tuple-element.6) | copy-start | bytes 24580
  78.4 2.7 %copy-start.8 = (f32[16,128]{1,0:T(8,128)S(1)}, f32[16,128]{1,0:T(8,128)}, u32[]{:S(2)}) copy-start(f32[16,128]{1,0:T(8,128)} %get-tuple-element.5) | copy-start | bytes 24580
  78.4 2.7 %copy-start.7 = (f32[16,128]{1,0:T(8,128)S(1)}, f32[16,128]{1,0:T(8,128)}, u32[]{:S(2)}) copy-start(f32[16,128]{1,0:T(8,128)} %get-tuple-element.4) | copy-start | bytes 24580
  78.4 2.7 %copy-start.6 = (f32[16,128]{1,0:T(8,128)S(1)}, f32[16,128]{1,0:T(8,128)}, u32[]{:S(2)}) copy-start(f32[16,128]{1,0:T(8,128)} %get-tuple-element.3) | copy-start | bytes 24580
  80.0 1.9 %copy-start.2 = (f32[16,64,128]{2,1,0:T(8,128)S(1)}, f32[16,64,128]{2,1,0:T(8,128)}, u32[]{:S(2)}) copy-start(f32[16,64,128]{2,1,0:T(8,128)} %copy-done.1) | copy-start | bytes 1572868
  80.0 1.9 %copy-start.28 = (pred[64]{0:T(512)(128)(4,1)S(1)}, pred[64]{0:T(512)(128)(4,1)}, u32[]{:S(2)}) copy-start(pred[64]{0:T(512)(128)(4,1)} %compare_and_fusion.1) | copy-start | bytes 196
  (2 other events, 1.4 us)

commit v10 on v9

--- a/solution.py
+++ b/solution.py
@@ -185,8 +185,18 @@
                 up.append((r * n + m, r * n + m - b))
             elif r > 0:
                 up.append((r * n + m, (r - 1) * n + (a - 1) * b + j))
-    above = lax.ppermute(core[:, h - HALO :], ("rows", "tm"), down)
-    below = lax.ppermute(core[:, :HALO], ("rows", "tm"), up)
+    edge_len = frames_all * HALO * ww
+    edge_rows = -(-edge_len // 1024) * 8
+
+    def dense(x):
+        x = jnp.pad(x.reshape(edge_len), (0, edge_rows * lanes - edge_len))
+        return x.reshape(edge_rows, lanes)
+
+    def undense(x):
+        return x.reshape(edge_rows * lanes)[:edge_len].reshape(frames_all, HALO, ww)
+
+    above = undense(lax.ppermute(dense(core[:, h - HALO :]), ("rows", "tm"), down))
+    below = undense(lax.ppermute(dense(core[:, :HALO]), ("rows", "tm"), up))
     rt = jnp.concatenate([above, core, below], axis=1)
 
     error_t, new_t = tile_compute(rt, wt, order, place, points, h, w, frames_all, cycle)

time: 127 us -> 122 us (0.961)
  waiting for transfers between devices: 4.47 us -> 0.01 us
  local copies, waits for them, and re-layouts: 12.8 us -> 16 us
  Pallas kernels: 72.6 us -> 70.7 us
  other arithmetic: 27.3 us -> 25.9 us
    ppermute x2, waiting for transfers between devices: 4.47 us -> 0.01 us  [the longest x1 0.01 us: on_device(): lax.ppermute(dense(core[:, h - HALO:]), ('rows', 'tm'), down)]
    reshape x0 -> x6, local copies, waits for them, and re-layouts: none -> 2.63 us  [the longest x2 1.43 us: undense(): return x.reshape(edge_rows * lanes)[:edge_len].reshape(frames_all, HALO, ww)]
    pallas_call x2, Pallas kernels: 72.6 us -> 70.7 us  [exchange(): pl.pallas_call(functools.partial(exchange_kernel, n), out_shape=jax.Shape...]
    mul x4, local copies, waits for them, and re-layouts: 0.71 us -> 2 us  [tile_compute(): background = background + ordered_weight[index][None] * window]
  transfers between devices with their start and end apart: 2 -> 2, of which waited for: 1 -> 0; matrix products, arithmetic and copies ran while one was open for 3% -> 4% of each run, Pallas kernels for 0% -> 0%
where the time goes in v10:
time: 122 us
  Pallas kernels  70.7 us (58%)
  other arithmetic  25.9 us (21%)
  local copies, waits for them, and re-layouts  16 us (13%)
  starting transfers between devices  6.85 us (6%)
  between operations  2.49 us (2%)
    pallas_call x2, Pallas kernels, exchange(): pl.pallas_call(functools.partial(exchange_kernel, n), out_shape=jax.Shape...  70.7 us
    reduce_sum x5, other arithmetic, tile_compute(): jnp.sum(error * rt[:, HALO + dy:HALO + dy + h, HALO + dx:HALO + dx + w],...  18.9 us
    ppermute x1, starting transfers between devices, on_device(): below = undense(lax.ppermute(dense(core[:, :HALO]), ('rows', 'tm'), up))  4.62 us
  transfers between devices with their start and end apart: 2, of which 0 were waited for; matrix products, arithmetic and copies ran while one was open for 4% of the time, Pallas kernels for 0%

profile of v10, /device:TPU:1, one launch (start us, length us, event | category | flops | bytes accessed | tf_op | source)
XLA Modules:
  0.0 121.9 jit_solution(4337822507427911211)
XLA Ops:
  0.6 1.5 %fusion.14 = (f32[4,16,128]{2,1,0:T(8,128)S(1)}, f32[4,16,128]{2,1,0:T(8,128)S(1)}, f32[4,16,128]{2,1,0:T(8,128)S(1)}, f32[4,16,128]{2,1,0:T(8,128)S(1)}, f32[4,...) fusion(f32[4,64,512]{2,1,0:T(8,128)} %param.7), kind=kLoop, calls=%fused_computation.343 | loop fusion | bytes 1441792 | tf_op jit(solution)/shard_map/slice | solution.py:147
  4.7 1.1 maximum_maximum_fusion.1.x_ref
  5.9 33.4 %exchange_0.1 = f32[16,136,128]{2,1,0:T(8,128)} custom-call(f32[16,136,128]{2,1,0:T(8,128)} %maximum_maximum_fusion.1.x_ref), custom_call_target="tpu_custom_call" | custom-call | tf_op jit(solution)/shard_map/exchange_0/pallas_call | solution.py:112
  39.3 1.3 %fusion.12 = (f32[16,64,128]{2,1,0:T(8,128)S(1)}, f32[16,64,128]{2,1,0:T(8,128)S(1)}) fusion(f32[16,136,128]{2,1,0:T(8,128)} %exchange_0.1), kind=kLoop, calls=%fused_computation.341 | loop fusion | bytes 2097152 | tf_op jit(solution)/shard_map/slice | solution.py:171
  40.7 0.5 reshape_reshape.3
  41.4 0.2 reshape.146
  41.6 2.2 %collective-permute-start = (f32[424,128]{1,0:T(8,128)S(1)}, f32[424,128]{1,0:T(8,128)S(1)}, u32[]{:S(2)}, u32[]{:S(2)}) collective-permute-start(f32[424,128]{1,0:T(8,128)S(1)} %pad_bitcast_fusion.1), channel_id=1, source_target_pairs={{0,4},{1,5},{2,6},{3,7},{4,8},{5,9},{6,10},{7,11},{8,12},{9,13},{1... | collective-permute-start | bytes 651272 | tf_op jit(solution)/shard_map/ppermute | solution.py:198
  44.1 0.7 pad_bitcast_fusion
  44.8 4.6 %collective-permute-start.1 = (f32[424,128]{1,0:T(8,128)}, f32[424,128]{1,0:T(8,128)S(1)}, u32[]{:S(2)}, u32[]{:S(2)}) collective-permute-start(f32[424,128]{1,0:T(8,128)} %pad_bitcast_fusion), channel_id=1, source_target_pairs={{4,0},{5,1},{6,2},{7,3},{8,4},{9,5},{10,6},{11,7},{12,8},{13,9},{1... | collective-permute-start | bytes 651272 | tf_op jit(solution)/shard_map/ppermute | solution.py:199
  49.7 0.5 compare_and_fusion.1
  50.2 0.6 gather_fusion
  51.0 0.6 slice_bitcast_fusion.62
  51.6 0.7 slice_bitcast_fusion.61
  52.3 0.7 slice_bitcast_fusion.63
  53.0 0.6 pad_clamp_fusion
  53.6 0.3 reshape.148
  53.9 1.1 reshape.151
  55.1 1.5 %fusion = f32[28,140]{1,0:T(8,128)S(1)} fusion(f32[64,6,140]{2,1,0:T(8,128)} %reshape.151, f32[64,16,12]{2,1,0:T(8,128)S(1)} %reshape_reshape.3, f32[64,16,128]{2,1,0:T(8,128)S(1)} %bitcast.332, f32[64,6,140]{2,1,0:T(8,128)S(1)} %reshape.148), kind=kLoop, calls=%fused_computation.3 | loop fusion | flops 1250480 | bytes 1019200 | tf_op jit(solution)/shard_map/reduce_sum | solution.py:71
  56.8 1.4 %maximum_maximum_fusion = (f32[64,22,140]{2,1,0:T(8,128)S(1)}, f32[64,22,140]{2,1,0:T(8,128)S(1)}) fusion(f32[64,16,12]{2,1,0:T(8,128)S(1)} %reshape_reshape.3, f32[64,16,128]{2,1,0:T(8,128)S(1)} %bitcast.333, f32[64,6,140]{2,1,0:T(8,128)S(1)} %reshape.148, f32[64,6,140]{2,1,0:T(8,128)} %reshape.151), kind=kLoop, calls=%fused_computation.14 | loop fusion | flops 788480 | bytes 2580480 | tf_op jit(solution)/shard_map/concatenate | solution.py:200
  58.4 12.0 %multiply_reduce_fusion = (f32[16,128]{1,0:T(8,128)}, f32[16,128]{1,0:T(8,128)}, f32[16,128]{1,0:T(8,128)}, f32[16,128]{1,0:T(8,128)}, f32[16,128]{1,0:T(8,128)}...) fusion(f32[64,22,140]{2,1,0:T(8,128)S(1)} %get-tuple-element.75, ...), kind=kLoop, calls=%fused_computation.37 | loop fusion | flops 21983232 | bytes 33226752 | tf_op jit(solution)/shard_map/reduce_sum | solution.py:67
  70.4 1.7 %multiply_reduce_fusion.18 = (f32[16,128]{1,0:T(8,128)S(1)}, f32[16,128]{1,0:T(8,128)S(1)}, f32[16,128]{1,0:T(8,128)S(1)}, f32[16,128]{1,0:T(8,128)S(1)}, f32[16...) fusion(f32[64,16,128]{2,1,0:T(8,128)S(1)} %get-tuple-element.69, ...), kind=kLoop, calls=%fused_computation.55 | loop fusion | flops 3121152 | bytes 6914048 | tf_op jit(solution)/shard_map/reduce_sum | solution.py:67
  72.1 0.9 multiply_reduce_fusion.30
  73.0 2.6 %multiply_reduce_fusion.34 = (f32[16,128]{1,0:T(8,128)S(1)}, f32[16,128]{1,0:T(8,128)S(1)}, f32[16,128]{1,0:T(8,128)S(1)}, f32[16,128]{1,0:T(8,128)S(1)}, f32[16...) fusion(f32[64,16,128]{2,1,0:T(8,128)S(1)} %get-tuple-element.69, ...), kind=kLoop, calls=%fused_computation.71 | loop fusion | flops 4681728 | bytes 10108928 | tf_op jit(solution)/shard_map/reduce_sum | solution.py:67
  75.8 1.7 %multiply_reduce_fusion.52 = (f32[16,128]{1,0:T(8,128)S(1)}, f32[16,128]{1,0:T(8,128)S(1)}, f32[16,128]{1,0:T(8,128)S(1)}, f32[16,128]{1,0:T(8,128)S(1)}, f32[16...) fusion(f32[64,16,128]{2,1,0:T(8,128)S(1)} %get-tuple-element.69, ...), kind=kLoop, calls=%fused_computation.89 | loop fusion | flops 3121152 | bytes 6914048 | tf_op jit(solution)/shard_map/reduce_sum | solution.py:67
  78.6 0.8 gather_fusion.1
  79.6 1.1 pad_maximum_fusion.1
  80.6 37.3 %exchange_1.1 = f32[16,128,128]{2,1,0:T(8,128)} custom-call(f32[16,128,128]{2,1,0:T(8,128)} %bitcast.340), custom_call_target="tpu_custom_call" | custom-call | tf_op jit(solution)/shard_map/exchange_1/pallas_call | solution.py:112
  117.9 1.3 %fusion.13 = (f32[16,4,16,128]{3,2,1,0:T(8,128)S(1)}, f32[16,4,16,128]{3,2,1,0:T(8,128)S(1)}) fusion(f32[16,8,16,128]{3,2,1,0:T(8,128)} %bitcast.339), kind=kLoop, calls=%fused_computation.342 | loop fusion | bytes 2097152 | tf_op jit(solution)/shard_map/slice | solution.py:214
  119.2 0.3 copy.19
  119.6 1.0 reshape.157
  120.6 0.3 copy.18
  120.9 1.0 reshape.159
  (228 shorter events, 3.6 us)
Async XLA Ops:
  0.6 3.4 %copy-start.3 = (f32[4,64,512]{2,1,0:T(8,128)S(1)}, f32[4,64,512]{2,1,0:T(8,128)}, u32[]{:S(2)}) copy-start(f32[4,64,512]{2,1,0:T(8,128)} %param.8) | copy-start | bytes 1572868
  40.6 9.6 %copy-start.1 = (f32[16,64,128]{2,1,0:T(8,128)}, f32[16,64,128]{2,1,0:T(8,128)S(1)}, u32[]{:S(2)}) copy-start(f32[16,64,128]{2,1,0:T(8,128)S(1)} %get-tuple-element.70) | copy-start | bytes 1572868
  41.3 8.1 %copy-start.45 = (s32[64,2]{0,1:T(2,128)S(1)}, s32[64,2]{0,1:T(2,128)}, u32[]{:S(2)}) copy-start(s32[64,2]{0,1:T(2,128)} %param.9) | copy-start | bytes 1540
  41.3 8.1 %copy-start.46 = (s32[64]{0:T(128)S(1)}, s32[64]{0:T(128)}, u32[]{:S(2)}) copy-start(s32[64]{0:T(128)} %constant.29.clone) | copy-start | bytes 772
  41.3 8.1 %copy-start.47 = (s32[64]{0:T(128)S(1)}, s32[64]{0:T(128)}, u32[]{:S(2)}) copy-start(s32[64]{0:T(128)} %constant.30.clone) | copy-start | bytes 772
  41.6 12.0 %collective-permute-start = (f32[424,128]{1,0:T(8,128)S(1)}, f32[424,128]{1,0:T(8,128)S(1)}, u32[]{:S(2)}, u32[]{:S(2)}) collective-permute-start(f32[424,128]{1,0:T(8,128)S(1)} %pad_bitcast_fusion.1), channel_id=1, source_target_pairs={{0,4},{1,5},{2,6},{3,7},{4,8},{5,9},{6,10},{7,11},{8,12},{9,13},{1... | collective-permute-start | bytes 651272 | tf_op jit(solution)/shard_map/ppermute | solution.py:198
  44.8 9.1 %collective-permute-start.1 = (f32[424,128]{1,0:T(8,128)}, f32[424,128]{1,0:T(8,128)S(1)}, u32[]{:S(2)}, u32[]{:S(2)}) collective-permute-start(f32[424,128]{1,0:T(8,128)} %pad_bitcast_fusion), channel_id=1, source_target_pairs={{4,0},{5,1},{6,2},{7,3},{8,4},{9,5},{10,6},{11,7},{12,8},{13,9},{1... | collective-permute-start | bytes 651272 | tf_op jit(solution)/shard_map/ppermute | solution.py:199
  56.6 1.6 %copy-start.5 = (f32[16,128]{1,0:T(8,128)S(1)}, f32[16,128]{1,0:T(8,128)}, u32[]{:S(2)}) copy-start(f32[16,128]{1,0:T(8,128)} %get-tuple-element.116) | copy-start | bytes 24580
  56.6 1.6 %copy-start.6 = (f32[16,128]{1,0:T(8,128)S(1)}, f32[16,128]{1,0:T(8,128)}, u32[]{:S(2)}) copy-start(f32[16,128]{1,0:T(8,128)} %get-tuple-element.117) | copy-start | bytes 24580
  56.6 1.6 %copy-start.7 = (f32[16,128]{1,0:T(8,128)S(1)}, f32[16,128]{1,0:T(8,128)}, u32[]{:S(2)}) copy-start(f32[16,128]{1,0:T(8,128)} %get-tuple-element.118) | copy-start | bytes 24580
  56.6 1.6 %copy-start.8 = (f32[16,128]{1,0:T(8,128)S(1)}, f32[16,128]{1,0:T(8,128)}, u32[]{:S(2)}) copy-start(f32[16,128]{1,0:T(8,128)} %get-tuple-element.119) | copy-start | bytes 24580
  56.6 1.6 %copy-start.9 = (f32[16,128]{1,0:T(8,128)S(1)}, f32[16,128]{1,0:T(8,128)}, u32[]{:S(2)}) copy-start(f32[16,128]{1,0:T(8,128)} %get-tuple-element.120) | copy-start | bytes 24580
  56.6 1.6 %copy-start.10 = (f32[16,128]{1,0:T(8,128)S(1)}, f32[16,128]{1,0:T(8,128)}, u32[]{:S(2)}) copy-start(f32[16,128]{1,0:T(8,128)} %get-tuple-element.121) | copy-start | bytes 24580
  56.6 1.6 %copy-start.11 = (f32[16,128]{1,0:T(8,128)S(1)}, f32[16,128]{1,0:T(8,128)}, u32[]{:S(2)}) copy-start(f32[16,128]{1,0:T(8,128)} %get-tuple-element.122) | copy-start | bytes 24580
  56.7 1.6 %copy-start.12 = (f32[16,128]{1,0:T(8,128)S(1)}, f32[16,128]{1,0:T(8,128)}, u32[]{:S(2)}) copy-start(f32[16,128]{1,0:T(8,128)} %get-tuple-element.123) | copy-start | bytes 24580
  56.7 1.6 %copy-start.13 = (f32[16,128]{1,0:T(8,128)S(1)}, f32[16,128]{1,0:T(8,128)}, u32[]{:S(2)}) copy-start(f32[16,128]{1,0:T(8,128)} %get-tuple-element.124) | copy-start | bytes 24580
  56.7 1.6 %copy-start.14 = (f32[16,128]{1,0:T(8,128)S(1)}, f32[16,128]{1,0:T(8,128)}, u32[]{:S(2)}) copy-start(f32[16,128]{1,0:T(8,128)} %get-tuple-element.125) | copy-start | bytes 24580
  56.7 1.6 %copy-start.15 = (f32[16,128]{1,0:T(8,128)S(1)}, f32[16,128]{1,0:T(8,128)}, u32[]{:S(2)}) copy-start(f32[16,128]{1,0:T(8,128)} %get-tuple-element.126) | copy-start | bytes 24580
  56.7 1.6 %copy-start.16 = (f32[16,128]{1,0:T(8,128)S(1)}, f32[16,128]{1,0:T(8,128)}, u32[]{:S(2)}) copy-start(f32[16,128]{1,0:T(8,128)} %get-tuple-element.127) | copy-start | bytes 24580
  75.7 2.6 %copy-start.43 = (f32[16,128]{1,0:T(8,128)S(1)}, f32[16,128]{1,0:T(8,128)}, u32[]{:S(2)}) copy-start(f32[16,128]{1,0:T(8,128)} %get-tuple-element.20) | copy-start | bytes 24580
  75.7 2.6 %copy-start.42 = (f32[16,128]{1,0:T(8,128)S(1)}, f32[16,128]{1,0:T(8,128)}, u32[]{:S(2)}) copy-start(f32[16,128]{1,0:T(8,128)} %get-tuple-element.19) | copy-start | bytes 24580
  75.7 2.6 %copy-start.41 = (f32[16,128]{1,0:T(8,128)S(1)}, f32[16,128]{1,0:T(8,128)}, u32[]{:S(2)}) copy-start(f32[16,128]{1,0:T(8,128)} %get-tuple-element.18) | copy-start | bytes 24580
  75.7 2.6 %copy-start.40 = (f32[16,128]{1,0:T(8,128)S(1)}, f32[16,128]{1,0:T(8,128)}, u32[]{:S(2)}) copy-start(f32[16,128]{1,0:T(8,128)} %get-tuple-element.17) | copy-start | bytes 24580
  75.7 2.7 %copy-start.39 = (f32[16,128]{1,0:T(8,128)S(1)}, f32[16,128]{1,0:T(8,128)}, u32[]{:S(2)}) copy-start(f32[16,128]{1,0:T(8,128)} %get-tuple-element.16) | copy-start | bytes 24580
  75.7 2.7 %copy-start.38 = (f32[16,128]{1,0:T(8,128)S(1)}, f32[16,128]{1,0:T(8,128)}, u32[]{:S(2)}) copy-start(f32[16,128]{1,0:T(8,128)} %get-tuple-element.15) | copy-start | bytes 24580
  75.7 2.7 %copy-start.37 = (f32[16,128]{1,0:T(8,128)S(1)}, f32[16,128]{1,0:T(8,128)}, u32[]{:S(2)}) copy-start(f32[16,128]{1,0:T(8,128)} %get-tuple-element.14) | copy-start | bytes 24580
  75.7 2.7 %copy-start.36 = (f32[16,128]{1,0:T(8,128)S(1)}, f32[16,128]{1,0:T(8,128)}, u32[]{:S(2)}) copy-start(f32[16,128]{1,0:T(8,128)} %get-tuple-element.13) | copy-start | bytes 24580
  75.7 2.7 %copy-start.35 = (f32[16,128]{1,0:T(8,128)S(1)}, f32[16,128]{1,0:T(8,128)}, u32[]{:S(2)}) copy-start(f32[16,128]{1,0:T(8,128)} %get-tuple-element.12) | copy-start | bytes 24580
  75.7 2.7 %copy-start.34 = (f32[16,128]{1,0:T(8,128)S(1)}, f32[16,128]{1,0:T(8,128)}, u32[]{:S(2)}) copy-start(f32[16,128]{1,0:T(8,128)} %get-tuple-element.11) | copy-start | bytes 24580
  75.8 2.7 %copy-start.33 = (f32[16,128]{1,0:T(8,128)S(1)}, f32[16,128]{1,0:T(8,128)}, u32[]{:S(2)}) copy-start(f32[16,128]{1,0:T(8,128)} %get-tuple-element.10) | copy-start | bytes 24580
  77.5 1.9 %copy-start.2 = (f32[16,64,128]{2,1,0:T(8,128)S(1)}, f32[16,64,128]{2,1,0:T(8,128)}, u32[]{:S(2)}) copy-start(f32[16,64,128]{2,1,0:T(8,128)} %copy-done.1) | copy-start | bytes 1572868
  77.5 1.9 %copy-start.44 = (pred[64]{0:T(512)(128)(4,1)S(1)}, pred[64]{0:T(512)(128)(4,1)}, u32[]{:S(2)}) copy-start(pred[64]{0:T(512)(128)(4,1)} %get-tuple-element.178) | copy-start | bytes 196
  (19 other events, 26.7 us)

commit v11 on v10

--- a/solution.py
+++ b/solution.py
@@ -122,6 +122,66 @@
         compiler_params=pltpu.CompilerParams(collective_id=tag, has_side_effects=True),
         name=f"exchange_{tag}",
     )(x)
+
+
+def return_kernel(n, b, nw_ref, er_ref, nw_out, er_out, send_sem, recv_sem, local_sem):
+    me = lax.axis_index("tm")
+    row = lax.axis_index("rows")
+    mesh_id = pl.DeviceIdType.MESH
+    h, w = nw_ref.shape[2], nw_ref.shape[3]
+    rows_at = pl.ds(pl.multiple_of((me // b) * h, h), h)
+    cols_at = pl.ds(pl.multiple_of((me % b) * w, w), w)
+    barrier = pltpu.get_barrier_semaphore()
+    for step in range(1, n):
+        pl.semaphore_signal(
+            barrier, inc=1, device_id=(row, lax.rem(me + step, n)), device_id_type=mesh_id
+        )
+    pl.semaphore_wait(barrier, n - 1)
+    pairs = ((nw_ref, nw_out), (er_ref, er_out))
+    local = []
+    for which, (src, dst) in enumerate(pairs):
+        copy = pltpu.make_async_copy(src.at[me], dst.at[:, rows_at, cols_at], local_sem.at[which])
+        copy.start()
+        local.append(copy)
+    copies = []
+    for step in range(1, n):
+        peer = lax.rem(me + step, n)
+        for which, (src, dst) in enumerate(pairs):
+            copy = pltpu.make_async_remote_copy(
+                src_ref=src.at[peer],
+                dst_ref=dst.at[:, rows_at, cols_at],
+                send_sem=send_sem.at[which, step],
+                recv_sem=recv_sem.at[which, step],
+                device_id=(row, peer),
+                device_id_type=mesh_id,
+            )
+            copy.start()
+            copies.append(copy)
+    for copy in copies:
+        copy.wait()
+    for copy in local:
+        copy.wait()
+
+
+def return_exchange(new_t, error_t, n, b, rows_dev, cols, tag):
+    anywhere = pl.BlockSpec(memory_space=pl.ANY)
+    k_dev, f_dev = new_t.shape[1], error_t.shape[1]
+    return pl.pallas_call(
+        functools.partial(return_kernel, n, b),
+        out_shape=(
+            jax.ShapeDtypeStruct((k_dev, rows_dev, cols), new_t.dtype),
+            jax.ShapeDtypeStruct((f_dev, rows_dev, cols), error_t.dtype),
+        ),
+        in_specs=[anywhere, anywhere],
+        out_specs=(anywhere, anywhere),
+        scratch_shapes=[
+            pltpu.SemaphoreType.DMA((2, n)),
+            pltpu.SemaphoreType.DMA((2, n)),
+            pltpu.SemaphoreType.DMA((2,)),
+        ],
+        compiler_params=pltpu.CompilerParams(collective_id=tag, has_side_effects=True),
+        name=f"exchange_{tag}",
+    )(new_t, error_t)
 
 
 def on_device(residual, cycle_weight, cycle_offsets):
@@ -201,17 +261,9 @@
 
     error_t, new_t = tile_compute(rt, wt, order, place, points, h, w, frames_all, cycle)
 
-    out = jnp.concatenate(
-        [new_t.reshape(n, k_dev, h, w), error_t.reshape(n, frames_dev, h, w)], axis=1
-    )
-    out = exchange(out.reshape(n, (k_dev + frames_dev) * h, w), n, 1)
-    out = out.reshape(n, k_dev + frames_dev, h, w)
-
-    def untile(x, lead):
-        x = x.reshape(a, b, lead, h, w).transpose(2, 0, 3, 1, 4)
-        return x.reshape(lead, rows_dev, cols)
-
-    return untile(out[:, :k_dev], k_dev), untile(out[:, k_dev:], frames_dev)
+    return return_exchange(
+        new_t.reshape(n, k_dev, h, w), error_t.reshape(n, frames_dev, h, w), n, b, rows_dev, cols, 1
+    )
 
 
 def solution(mesh):

time: 122 us -> 122 us (level)
    pallas_call x0 -> x1, Pallas kernels: none -> 37.4 us  [return_exchange(): pl.pallas_call(functools.partial(return_kernel, n, b), out_shape=(jax.Sha...]
    pallas_call x2 -> x1, Pallas kernels: 70.7 us -> 33.4 us  [exchange(): pl.pallas_call(functools.partial(exchange_kernel, n), out_shape=jax.Shape...]
    unnamed x189 -> x193, local copies, waits for them, and re-layouts: 0.54 us -> 4.28 us
    reshape x4 -> x0, local copies, waits for them, and re-layouts: 2.69 us -> none  [the longest x2 2.01 us: untile(): return x.reshape(lead, rows_dev, cols)]
    slice x2 -> x1, local copies, waits for them, and re-layouts: 2.62 us -> 1.32 us  [on_device(): core_main = got[:, :main_rows].reshape(frames_all, h, lanes)]
where the time goes in v11:
time: 122 us; the launch traced here: 121 us
  Pallas kernels  70.8 us (58%)
  other arithmetic  25.5 us (21%)
  local copies, waits for them, and re-layouts  15.7 us (13%)
  starting transfers between devices  7.03 us (6%)
  between operations  2.47 us (2%)
    pallas_call x1, Pallas kernels, return_exchange(): pl.pallas_call(functools.partial(return_kernel, n, b), out_shape=(jax.Sha...  37.4 us
    pallas_call x1, Pallas kernels, exchange(): pl.pallas_call(functools.partial(exchange_kernel, n), out_shape=jax.Shape...  33.4 us
    reduce_sum x5, other arithmetic, tile_compute(): jnp.sum(error * rt[:, HALO + dy:HALO + dy + h, HALO + dx:HALO + dx + w],...  18.7 us
    ppermute x1, starting transfers between devices, on_device(): below = undense(lax.ppermute(dense(core[:, :HALO]), ('rows', 'tm'), up))  4.81 us
    unnamed x193, local copies, waits for them, and re-layouts  4.28 us
  transfers between devices with their start and end apart: 2, of which 0 were waited for; matrix products, arithmetic and copies ran while one was open for 4% of the time, Pallas kernels for 0%

profile of v11, /device:TPU:1, one launch (start us, length us, event | category | flops | bytes accessed | tf_op | source)
XLA Modules:
  0.0 121.5 jit_solution(7302544165195743869)
XLA Ops:
  0.6 1.5 %fusion.13 = (f32[4,16,128]{2,1,0:T(8,128)S(1)}, f32[4,16,128]{2,1,0:T(8,128)S(1)}, f32[4,16,128]{2,1,0:T(8,128)S(1)}, f32[4,16,128]{2,1,0:T(8,128)S(1)}, f32[4,...) fusion(f32[4,64,512]{2,1,0:T(8,128)} %param.7), kind=kLoop, calls=%fused_computation.339 | loop fusion | bytes 1441792 | tf_op jit(solution)/shard_map/slice | solution.py:207
  2.2 0.2 pad_slice_fusion.10
  4.7 1.1 maximum_maximum_fusion.1.x_ref
  5.9 33.4 %exchange_0.1 = f32[16,136,128]{2,1,0:T(8,128)} custom-call(f32[16,136,128]{2,1,0:T(8,128)} %maximum_maximum_fusion.1.x_ref), custom_call_target="tpu_custom_call" | custom-call | tf_op jit(solution)/shard_map/exchange_0/pallas_call | solution.py:112
  39.3 1.3 %fusion.12 = (f32[16,64,128]{2,1,0:T(8,128)S(1)}, f32[16,64,128]{2,1,0:T(8,128)S(1)}) fusion(f32[16,136,128]{2,1,0:T(8,128)} %exchange_0.1), kind=kLoop, calls=%fused_computation.338 | loop fusion | bytes 2097152 | tf_op jit(solution)/shard_map/slice | solution.py:230
  40.7 0.5 reshape_reshape.3
  41.3 0.2 reshape.128
  41.6 2.2 %collective-permute-start = (f32[424,128]{1,0:T(8,128)S(1)}, f32[424,128]{1,0:T(8,128)S(1)}, u32[]{:S(2)}, u32[]{:S(2)}) collective-permute-start(f32[424,128]{1,0:T(8,128)S(1)} %pad_bitcast_fusion.1), channel_id=1, source_target_pairs={{0,4},{1,5},{2,6},{3,7},{4,8},{5,9},{6,10},{7,11},{8,12},{9,13},{1... | collective-permute-start | bytes 651272 | tf_op jit(solution)/shard_map/ppermute | solution.py:258
  43.9 0.2 reshape.131
  44.1 0.7 pad_bitcast_fusion
  44.8 4.8 %collective-permute-start.1 = (f32[424,128]{1,0:T(8,128)}, f32[424,128]{1,0:T(8,128)S(1)}, u32[]{:S(2)}, u32[]{:S(2)}) collective-permute-start(f32[424,128]{1,0:T(8,128)} %pad_bitcast_fusion), channel_id=1, source_target_pairs={{4,0},{5,1},{6,2},{7,3},{8,4},{9,5},{10,6},{11,7},{12,8},{13,9},{1... | collective-permute-start | bytes 651272 | tf_op jit(solution)/shard_map/ppermute | solution.py:259
  49.9 0.5 compare_and_fusion.1
  50.4 0.6 gather_fusion
  51.2 0.6 slice_bitcast_fusion.62
  51.8 0.7 slice_bitcast_fusion.61
  52.5 0.7 slice_bitcast_fusion.63
  53.2 0.6 pad_clamp_fusion
  53.8 0.3 reshape.130
  54.1 1.1 reshape.133
  55.2 1.5 %fusion = f32[28,140]{1,0:T(8,128)S(1)} fusion(f32[64,6,140]{2,1,0:T(8,128)} %reshape.133, f32[64,16,12]{2,1,0:T(8,128)S(1)} %reshape_reshape.3, f32[64,16,128]{2,1,0:T(8,128)S(1)} %bitcast.322, f32[64,6,140]{2,1,0:T(8,128)S(1)} %reshape.130), kind=kLoop, calls=%fused_computation.3 | loop fusion | flops 1250480 | bytes 1019200 | tf_op jit(solution)/shard_map/reduce_sum | solution.py:71
  57.0 1.4 %maximum_maximum_fusion = (f32[64,22,140]{2,1,0:T(8,128)S(1)}, f32[64,22,140]{2,1,0:T(8,128)S(1)}) fusion(f32[64,16,12]{2,1,0:T(8,128)S(1)} %reshape_reshape.3, f32[64,16,128]{2,1,0:T(8,128)S(1)} %bitcast.323, f32[64,6,140]{2,1,0:T(8,128)S(1)} %reshape.130, f32[64,6,140]{2,1,0:T(8,128)} %reshape.133), kind=kLoop, calls=%fused_computation.14 | loop fusion | flops 788480 | bytes 2580480 | tf_op jit(solution)/shard_map/concatenate | solution.py:260
  58.6 11.9 %multiply_reduce_fusion = (f32[16,128]{1,0:T(8,128)}, f32[16,128]{1,0:T(8,128)}, f32[16,128]{1,0:T(8,128)}, f32[16,128]{1,0:T(8,128)}, f32[16,128]{1,0:T(8,128)}...) fusion(f32[64,22,140]{2,1,0:T(8,128)S(1)} %get-tuple-element.73, ...), kind=kLoop, calls=%fused_computation.34 | loop fusion | flops 21983232 | bytes 33226752 | tf_op jit(solution)/shard_map/reduce_sum | solution.py:67
  70.5 1.7 %multiply_reduce_fusion.18 = (f32[16,128]{1,0:T(8,128)S(1)}, f32[16,128]{1,0:T(8,128)S(1)}, f32[16,128]{1,0:T(8,128)S(1)}, f32[16,128]{1,0:T(8,128)S(1)}, f32[16...) fusion(f32[64,16,128]{2,1,0:T(8,128)S(1)} %get-tuple-element.69, ...), kind=kLoop, calls=%fused_computation.52 | loop fusion | flops 3121152 | bytes 6914048 | tf_op jit(solution)/shard_map/reduce_sum | solution.py:67
  72.2 0.9 multiply_reduce_fusion.30
  73.0 2.6 %multiply_reduce_fusion.34 = (f32[16,128]{1,0:T(8,128)S(1)}, f32[16,128]{1,0:T(8,128)S(1)}, f32[16,128]{1,0:T(8,128)S(1)}, f32[16,128]{1,0:T(8,128)S(1)}, f32[16...) fusion(f32[64,16,128]{2,1,0:T(8,128)S(1)} %get-tuple-element.69, ...), kind=kLoop, calls=%fused_computation.68 | loop fusion | flops 4681728 | bytes 10108928 | tf_op jit(solution)/shard_map/reduce_sum | solution.py:67
  75.8 1.7 %multiply_reduce_fusion.52 = (f32[16,128]{1,0:T(8,128)S(1)}, f32[16,128]{1,0:T(8,128)S(1)}, f32[16,128]{1,0:T(8,128)S(1)}, f32[16,128]{1,0:T(8,128)S(1)}, f32[16...) fusion(f32[64,16,128]{2,1,0:T(8,128)S(1)} %get-tuple-element.69, ...), kind=kLoop, calls=%fused_computation.86 | loop fusion | flops 3121152 | bytes 6914048 | tf_op jit(solution)/shard_map/reduce_sum | solution.py:67
  77.6 0.2 fusion.10
  78.7 0.8 gather_fusion.1
  79.4 0.9 fusion.7
  80.4 37.4 %exchange_1.1 = (f32[4,64,512]{2,1,0:T(8,128)}, f32[4,64,512]{2,1,0:T(8,128)}) custom-call(f32[16,4,16,128]{3,2,1,0:T(8,128)} %bitcast.329, f32[16,4,16,128]{3,2,1,0:T(8,128)} %bitcast.326), custom_call_target="tpu_custom_call" | custom-call | tf_op jit(solution)/shard_map/exchange_1/pallas_call | solution.py:169
  117.8 1.9 %copy.105 = f32[4,64,512]{2,1,0:T(8,128)} copy(f32[4,64,512]{2,1,0:T(8,128)} %get-tuple-element.180) | data formatting | bytes 1048576
  119.6 1.9 %copy.106 = f32[4,64,512]{2,1,0:T(8,128)} copy(f32[4,64,512]{2,1,0:T(8,128)} %get-tuple-element.181) | data formatting | bytes 1048576
  (226 shorter events, 2.9 us)
Async XLA Ops:
  0.6 3.4 %copy-start.4 = (f32[4,64,512]{2,1,0:T(8,128)S(1)}, f32[4,64,512]{2,1,0:T(8,128)}, u32[]{:S(2)}) copy-start(f32[4,64,512]{2,1,0:T(8,128)} %param.8) | copy-start | bytes 1572868
  40.6 9.8 %copy-start.2 = (f32[16,64,128]{2,1,0:T(8,128)}, f32[16,64,128]{2,1,0:T(8,128)S(1)}, u32[]{:S(2)}) copy-start(f32[16,64,128]{2,1,0:T(8,128)S(1)} %get-tuple-element.71) | copy-start | bytes 1572868
  41.3 8.3 %copy-start.46 = (s32[64,2]{0,1:T(2,128)S(1)}, s32[64,2]{0,1:T(2,128)}, u32[]{:S(2)}) copy-start(s32[64,2]{0,1:T(2,128)} %param.9) | copy-start | bytes 1540
  41.3 8.3 %copy-start.47 = (s32[64]{0:T(128)S(1)}, s32[64]{0:T(128)}, u32[]{:S(2)}) copy-start(s32[64]{0:T(128)} %constant.29.clone) | copy-start | bytes 772
  41.3 8.3 %copy-start.48 = (s32[64]{0:T(128)S(1)}, s32[64]{0:T(128)}, u32[]{:S(2)}) copy-start(s32[64]{0:T(128)} %constant.30.clone) | copy-start | bytes 772
  41.6 12.2 %collective-permute-start = (f32[424,128]{1,0:T(8,128)S(1)}, f32[424,128]{1,0:T(8,128)S(1)}, u32[]{:S(2)}, u32[]{:S(2)}) collective-permute-start(f32[424,128]{1,0:T(8,128)S(1)} %pad_bitcast_fusion.1), channel_id=1, source_target_pairs={{0,4},{1,5},{2,6},{3,7},{4,8},{5,9},{6,10},{7,11},{8,12},{9,13},{1... | collective-permute-start | bytes 651272 | tf_op jit(solution)/shard_map/ppermute | solution.py:258
  44.8 9.3 %collective-permute-start.1 = (f32[424,128]{1,0:T(8,128)}, f32[424,128]{1,0:T(8,128)S(1)}, u32[]{:S(2)}, u32[]{:S(2)}) collective-permute-start(f32[424,128]{1,0:T(8,128)} %pad_bitcast_fusion), channel_id=1, source_target_pairs={{4,0},{5,1},{6,2},{7,3},{8,4},{9,5},{10,6},{11,7},{12,8},{13,9},{1... | collective-permute-start | bytes 651272 | tf_op jit(solution)/shard_map/ppermute | solution.py:259
  56.8 1.6 %copy-start.6 = (f32[16,128]{1,0:T(8,128)S(1)}, f32[16,128]{1,0:T(8,128)}, u32[]{:S(2)}) copy-start(f32[16,128]{1,0:T(8,128)} %get-tuple-element.114) | copy-start | bytes 24580
  56.8 1.6 %copy-start.7 = (f32[16,128]{1,0:T(8,128)S(1)}, f32[16,128]{1,0:T(8,128)}, u32[]{:S(2)}) copy-start(f32[16,128]{1,0:T(8,128)} %get-tuple-element.115) | copy-start | bytes 24580
  56.8 1.6 %copy-start.8 = (f32[16,128]{1,0:T(8,128)S(1)}, f32[16,128]{1,0:T(8,128)}, u32[]{:S(2)}) copy-start(f32[16,128]{1,0:T(8,128)} %get-tuple-element.116) | copy-start | bytes 24580
  56.8 1.6 %copy-start.9 = (f32[16,128]{1,0:T(8,128)S(1)}, f32[16,128]{1,0:T(8,128)}, u32[]{:S(2)}) copy-start(f32[16,128]{1,0:T(8,128)} %get-tuple-element.117) | copy-start | bytes 24580
  56.8 1.6 %copy-start.10 = (f32[16,128]{1,0:T(8,128)S(1)}, f32[16,128]{1,0:T(8,128)}, u32[]{:S(2)}) copy-start(f32[16,128]{1,0:T(8,128)} %get-tuple-element.118) | copy-start | bytes 24580
  56.8 1.6 %copy-start.11 = (f32[16,128]{1,0:T(8,128)S(1)}, f32[16,128]{1,0:T(8,128)}, u32[]{:S(2)}) copy-start(f32[16,128]{1,0:T(8,128)} %get-tuple-element.119) | copy-start | bytes 24580
  56.8 1.6 %copy-start.12 = (f32[16,128]{1,0:T(8,128)S(1)}, f32[16,128]{1,0:T(8,128)}, u32[]{:S(2)}) copy-start(f32[16,128]{1,0:T(8,128)} %get-tuple-element.120) | copy-start | bytes 24580
  56.8 1.6 %copy-start.13 = (f32[16,128]{1,0:T(8,128)S(1)}, f32[16,128]{1,0:T(8,128)}, u32[]{:S(2)}) copy-start(f32[16,128]{1,0:T(8,128)} %get-tuple-element.121) | copy-start | bytes 24580
  56.8 1.6 %copy-start.14 = (f32[16,128]{1,0:T(8,128)S(1)}, f32[16,128]{1,0:T(8,128)}, u32[]{:S(2)}) copy-start(f32[16,128]{1,0:T(8,128)} %get-tuple-element.122) | copy-start | bytes 24580
  56.9 1.6 %copy-start.15 = (f32[16,128]{1,0:T(8,128)S(1)}, f32[16,128]{1,0:T(8,128)}, u32[]{:S(2)}) copy-start(f32[16,128]{1,0:T(8,128)} %get-tuple-element.123) | copy-start | bytes 24580
  56.9 1.6 %copy-start.16 = (f32[16,128]{1,0:T(8,128)S(1)}, f32[16,128]{1,0:T(8,128)}, u32[]{:S(2)}) copy-start(f32[16,128]{1,0:T(8,128)} %get-tuple-element.124) | copy-start | bytes 24580
  70.5 5.2 %copy-start = (f32[64,16,128]{2,1,0:T(8,128)}, f32[64,16,128]{2,1,0:T(8,128)S(1)}, u32[]{:S(2)}) copy-start(f32[64,16,128]{2,1,0:T(8,128)S(1)} %get-tuple-element.69) | copy-start | bytes 1572868
  75.7 2.6 %copy-start.44 = (f32[16,128]{1,0:T(8,128)S(1)}, f32[16,128]{1,0:T(8,128)}, u32[]{:S(2)}) copy-start(f32[16,128]{1,0:T(8,128)} %get-tuple-element.20) | copy-start | bytes 24580
  75.7 2.6 %copy-start.43 = (f32[16,128]{1,0:T(8,128)S(1)}, f32[16,128]{1,0:T(8,128)}, u32[]{:S(2)}) copy-start(f32[16,128]{1,0:T(8,128)} %get-tuple-element.19) | copy-start | bytes 24580
  75.7 2.6 %copy-start.42 = (f32[16,128]{1,0:T(8,128)S(1)}, f32[16,128]{1,0:T(8,128)}, u32[]{:S(2)}) copy-start(f32[16,128]{1,0:T(8,128)} %get-tuple-element.18) | copy-start | bytes 24580
  75.7 2.6 %copy-start.41 = (f32[16,128]{1,0:T(8,128)S(1)}, f32[16,128]{1,0:T(8,128)}, u32[]{:S(2)}) copy-start(f32[16,128]{1,0:T(8,128)} %get-tuple-element.17) | copy-start | bytes 24580
  75.7 2.7 %copy-start.40 = (f32[16,128]{1,0:T(8,128)S(1)}, f32[16,128]{1,0:T(8,128)}, u32[]{:S(2)}) copy-start(f32[16,128]{1,0:T(8,128)} %get-tuple-element.16) | copy-start | bytes 24580
  75.7 2.7 %copy-start.39 = (f32[16,128]{1,0:T(8,128)S(1)}, f32[16,128]{1,0:T(8,128)}, u32[]{:S(2)}) copy-start(f32[16,128]{1,0:T(8,128)} %get-tuple-element.15) | copy-start | bytes 24580
  75.7 2.7 %copy-start.38 = (f32[16,128]{1,0:T(8,128)S(1)}, f32[16,128]{1,0:T(8,128)}, u32[]{:S(2)}) copy-start(f32[16,128]{1,0:T(8,128)} %get-tuple-element.14) | copy-start | bytes 24580
  75.7 2.7 %copy-start.37 = (f32[16,128]{1,0:T(8,128)S(1)}, f32[16,128]{1,0:T(8,128)}, u32[]{:S(2)}) copy-start(f32[16,128]{1,0:T(8,128)} %get-tuple-element.13) | copy-start | bytes 24580
  75.8 2.7 %copy-start.36 = (f32[16,128]{1,0:T(8,128)S(1)}, f32[16,128]{1,0:T(8,128)}, u32[]{:S(2)}) copy-start(f32[16,128]{1,0:T(8,128)} %get-tuple-element.12) | copy-start | bytes 24580
  75.8 2.7 %copy-start.35 = (f32[16,128]{1,0:T(8,128)S(1)}, f32[16,128]{1,0:T(8,128)}, u32[]{:S(2)}) copy-start(f32[16,128]{1,0:T(8,128)} %get-tuple-element.11) | copy-start | bytes 24580
  75.8 2.7 %copy-start.34 = (f32[16,128]{1,0:T(8,128)S(1)}, f32[16,128]{1,0:T(8,128)}, u32[]{:S(2)}) copy-start(f32[16,128]{1,0:T(8,128)} %get-tuple-element.10) | copy-start | bytes 24580
  77.6 1.9 %copy-start.3 = (f32[16,64,128]{2,1,0:T(8,128)S(1)}, f32[16,64,128]{2,1,0:T(8,128)}, u32[]{:S(2)}) copy-start(f32[16,64,128]{2,1,0:T(8,128)} %copy-done.2) | copy-start | bytes 1572868
  77.6 1.9 %copy-start.45 = (pred[64]{0:T(512)(128)(4,1)S(1)}, pred[64]{0:T(512)(128)(4,1)}, u32[]{:S(2)}) copy-start(pred[64]{0:T(512)(128)(4,1)} %get-tuple-element.176) | copy-start | bytes 196
  (20 other events, 28.3 us)

commit v12 on v11

--- a/solution.py
+++ b/solution.py
@@ -257,7 +257,7 @@
 
     above = undense(lax.ppermute(dense(core[:, h - HALO :]), ("rows", "tm"), down))
     below = undense(lax.ppermute(dense(core[:, :HALO]), ("rows", "tm"), up))
-    rt = jnp.concatenate([above, core, below], axis=1)
+    rt = lax.optimization_barrier(jnp.concatenate([above, core, below], axis=1))
 
     error_t, new_t = tile_compute(rt, wt, order, place, points, h, w, frames_all, cycle)
 

time: 122 us -> 117 us (0.959)
  waiting for transfers between devices: 0.01 us -> 5.61 us
  Pallas kernels: 70.8 us -> 66.4 us
  other arithmetic: 25.5 us -> 21.5 us
  local copies, waits for them, and re-layouts: 15.7 us -> 13.9 us
    ppermute x1, waiting for transfers between devices: 0.01 us -> 5.15 us  [on_device(): lax.ppermute(dense(core[:, h - HALO:]), ('rows', 'tm'), down)]
    pallas_call x1, Pallas kernels: 37.4 us -> 33 us  [return_exchange(): pl.pallas_call(functools.partial(return_kernel, n, b), out_shape=(jax.Sha...]
    mul x4, local copies, waits for them, and re-layouts: 2 us -> 0.7 us  [tile_compute(): background = background + ordered_weight[index][None] * window]
    reduce_sum x1, other arithmetic: 1.52 us -> 0.22 us  [tile_compute(): squares = jnp.sum(rt * rt, axis=0)]
    slice x1, local copies, waits for them, and re-layouts: 0.2 us -> 1.48 us  [on_device(): padded[:, i * h:(i + 1) * h, j * w + lanes:j * w + ww]]
    reduce_sum x5 -> x4, other arithmetic: 18.7 us -> 17.7 us  [tile_compute(): jnp.sum(error * rt[:, HALO + dy:HALO + dy + h, HALO + dx:HALO + dx + w],...]
    unnamed x193 -> x107, local copies, waits for them, and re-layouts: 4.28 us -> 4.09 us
  transfers between devices with their start and end apart: 2 -> 2, of which waited for: 0 -> 2; matrix products, arithmetic and copies ran while one was open for 4% -> 2% of each run, Pallas kernels for 0% -> 0%
where the time goes in v12:
time: 117 us; the launch traced here: 116 us
  Pallas kernels  66.4 us (57%)
  other arithmetic  21.5 us (18%)
  local copies, waits for them, and re-layouts  13.9 us (12%)
  starting transfers between devices  7.04 us (6%)
  waiting for transfers between devices  5.61 us (5%)
  between operations  1.84 us (2%)
    pallas_call x1, Pallas kernels, exchange(): pl.pallas_call(functools.partial(exchange_kernel, n), out_shape=jax.Shape...  33.4 us
    pallas_call x1, Pallas kernels, return_exchange(): pl.pallas_call(functools.partial(return_kernel, n, b), out_shape=(jax.Sha...  33 us
    reduce_sum x4, other arithmetic, tile_compute(): jnp.sum(error * rt[:, HALO + dy:HALO + dy + h, HALO + dx:HALO + dx + w],...  17.7 us
    ppermute x1, waiting for transfers between devices, on_device(): lax.ppermute(dense(core[:, h - HALO:]), ('rows', 'tm'), down)  5.15 us
    ppermute x1, starting transfers between devices, on_device(): below = undense(lax.ppermute(dense(core[:, :HALO]), ('rows', 'tm'), up))  4.94 us
    unnamed x107, local copies, waits for them, and re-layouts  4.09 us
  transfers between devices with their start and end apart: 2, of which 2 were waited for; matrix products, arithmetic and copies ran while one was open for 2% of the time, Pallas kernels for 0%

profile of v12, /device:TPU:1, one launch (start us, length us, event | category | flops | bytes accessed | tf_op | source)
XLA Modules:
  0.0 116.2 jit_solution(1213959181032277534)
XLA Ops:
  0.6 1.5 %pad_slice_fusion.2 = (f32[4,16,12]{2,1,0:T(8,128)S(1)}, f32[4,16,12]{2,1,0:T(8,128)S(1)}, f32[4,16,12]{2,1,0:T(8,128)S(1)}, f32[4,16,12]{2,1,0:T(8,128)S(1)}, f...) fusion(f32[4,64,512]{2,1,0:T(8,128)} %param.7), kind=kLoop, calls=%fused_computation.7 | loop fusion | bytes 966656 | tf_op jit(solution)/shard_map/slice | solution.py:209
  2.1 1.4 %fusion.6 = (f32[4,16,128]{2,1,0:T(8,128)S(1)}, f32[4,16,128]{2,1,0:T(8,128)S(1)}, f32[4,16,128]{2,1,0:T(8,128)S(1)}, f32[4,16,128]{2,1,0:T(8,128)S(1)}, f32[4,1...) fusion(f32[4,64,512]{2,1,0:T(8,128)} %param.7), kind=kLoop, calls=%fused_computation.325 | loop fusion | bytes 1441792 | tf_op jit(solution)/shard_map/slice | solution.py:207
  5.2 0.2 reshape.124
  5.9 1.1 maximum_maximum_fusion.x_ref
  7.1 33.4 %exchange_0.1 = f32[16,136,128]{2,1,0:T(8,128)} custom-call(f32[16,136,128]{2,1,0:T(8,128)} %maximum_maximum_fusion.x_ref), custom_call_target="tpu_custom_call" | custom-call | tf_op jit(solution)/shard_map/exchange_0/pallas_call | solution.py:112
  40.5 1.3 %fusion.5 = (f32[16,64,128]{2,1,0:T(8,128)S(1)}, f32[16,64,128]{2,1,0:T(8,128)S(1)}) fusion(f32[16,136,128]{2,1,0:T(8,128)} %exchange_0.1), kind=kLoop, calls=%fused_computation.324 | loop fusion | bytes 2097152 | tf_op jit(solution)/shard_map/slice | solution.py:230
  41.9 0.5 reshape_reshape.3
  42.5 0.2 reshape.131
  42.8 4.9 %collective-permute-start.1 = (f32[424,128]{1,0:T(8,128)S(1)}, f32[424,128]{1,0:T(8,128)S(1)}, u32[]{:S(2)}, u32[]{:S(2)}) collective-permute-start(f32[424,128]{1,0:T(8,128)S(1)} %pad_bitcast_fusion), channel_id=1, source_target_pairs={{4,0},{5,1},{6,2},{7,3},{8,4},{9,5},{10,6},{11,7},{12,8},{13,9},{1... | collective-permute-start | bytes 651272 | tf_op jit(solution)/shard_map/ppermute | solution.py:259
  47.8 0.2 reshape.128
  48.0 2.1 %collective-permute-start = (f32[424,128]{1,0:T(8,128)S(1)}, f32[424,128]{1,0:T(8,128)S(1)}, u32[]{:S(2)}, u32[]{:S(2)}) collective-permute-start(f32[424,128]{1,0:T(8,128)S(1)} %pad_bitcast_fusion.1), channel_id=1, source_target_pairs={{0,4},{1,5},{2,6},{3,7},{4,8},{5,9},{6,10},{7,11},{8,12},{9,13},{1... | collective-permute-start | bytes 651272 | tf_op jit(solution)/shard_map/ppermute | solution.py:258
  50.2 0.2 select_reduce_fusion
  50.4 0.5 compare_and_fusion.1
  50.9 0.6 gather_fusion
  51.6 0.1 broadcast_select_fusion
  51.8 0.7 slice_bitcast_fusion.61
  52.4 0.5 collective-permute-done.1
  52.9 0.3 reshape.133
  53.2 5.2 %collective-permute-done = f32[424,128]{1,0:T(8,128)S(1)} collective-permute-done((f32[424,128]{1,0:T(8,128)S(1)}, f32[424,128]{1,0:T(8,128)S(1)}, u32[]{:S(2)}, u32[]{:S(2)}) %collective-permute-start) | collective-permute-done | bytes 217120 | tf_op jit(solution)/shard_map/ppermute | solution.py:258
  58.4 0.3 reshape.130
  58.7 0.3 pad_maximum_fusion
  59.1 11.1 %multiply_reduce_fusion.1 = (f32[16,128]{1,0:T(8,128)S(1)}, f32[16,128]{1,0:T(8,128)S(1)}, f32[16,128]{1,0:T(8,128)S(1)}, f32[16,128]{1,0:T(8,128)S(1)}, f32[16,...) fusion(f32[64,28,140]{2,1,0:T(8,128)S(1)} %pad_maximum_fusion, ...), kind=kLoop, calls=%fused_computation.20 | loop fusion | flops 21458944 | bytes 35274752 | tf_op jit(solution)/shard_map/reduce_sum | solution.py:67
  70.2 1.4 %multiply_reduce_fusion.55 = (f32[16,128]{1,0:T(8,128)S(1)}, f32[16,128]{1,0:T(8,128)S(1)}, f32[16,128]{1,0:T(8,128)S(1)}, f32[16,128]{1,0:T(8,128)S(1)}, f32[16...) fusion(f32[64,16,128]{2,1,0:T(8,128)S(1)} %get-tuple-element.69, ...), kind=kLoop, calls=%fused_computation.74 | loop fusion | flops 2600960 | bytes 5849088 | tf_op jit(solution)/shard_map/reduce_sum | solution.py:67
  71.6 2.6 %multiply_reduce_fusion.37 = (f32[16,128]{1,0:T(8,128)S(1)}, f32[16,128]{1,0:T(8,128)S(1)}, f32[16,128]{1,0:T(8,128)S(1)}, f32[16,128]{1,0:T(8,128)S(1)}, f32[16...) fusion(f32[64,16,128]{2,1,0:T(8,128)S(1)} %get-tuple-element.69, ...), kind=kLoop, calls=%fused_computation.56 | loop fusion | flops 4681728 | bytes 10108928 | tf_op jit(solution)/shard_map/reduce_sum | solution.py:67
  74.3 2.5 %multiply_reduce_fusion.19 = (f32[16,128]{1,0:T(8,128)S(1)}, f32[16,128]{1,0:T(8,128)S(1)}, f32[16,128]{1,0:T(8,128)S(1)}, f32[16,128]{1,0:T(8,128)S(1)}, f32[16...) fusion(f32[64,16,128]{2,1,0:T(8,128)S(1)} %get-tuple-element.69, ...), kind=kLoop, calls=%fused_computation.38 | loop fusion | flops 4681728 | bytes 10108928 | tf_op jit(solution)/shard_map/reduce_sum | solution.py:67
  76.8 0.2 multiply_reduce_fusion
  77.0 0.2 fusion.4
  77.9 0.6 gather_fusion.1
  78.6 0.9 fusion.1
  79.5 33.0 %exchange_1.1 = (f32[4,64,512]{2,1,0:T(8,128)}, f32[4,64,512]{2,1,0:T(8,128)}) custom-call(f32[16,4,16,128]{3,2,1,0:T(8,128)} %bitcast.326, f32[16,4,16,128]{3,2,1,0:T(8,128)} %bitcast.321), custom_call_target="tpu_custom_call" | custom-call | tf_op jit(solution)/shard_map/exchange_1/pallas_call | solution.py:169
  112.5 1.9 %copy.105 = f32[4,64,512]{2,1,0:T(8,128)} copy(f32[4,64,512]{2,1,0:T(8,128)} %get-tuple-element.178) | data formatting | bytes 1048576
  114.4 1.9 %copy.106 = f32[4,64,512]{2,1,0:T(8,128)} copy(f32[4,64,512]{2,1,0:T(8,128)} %get-tuple-element.179) | data formatting | bytes 1048576
  (139 shorter events, 2.2 us)
Async XLA Ops:
  0.6 4.6 %copy-start.1 = (f32[4,64,512]{2,1,0:T(8,128)S(1)}, f32[4,64,512]{2,1,0:T(8,128)}, u32[]{:S(2)}) copy-start(f32[4,64,512]{2,1,0:T(8,128)} %param.8) | copy-start | bytes 1572868
  40.5 1.4 %slice-start = ((f32[16,136,128]{2,1,0:T(8,128)}), f32[16,6,128]{2,1,0:T(8,128)S(1)}, s32[]{:S(2)}) async-start(f32[16,136,128]{2,1,0:T(8,128)} %exchange_0.1), calls=%async_computation | async-start | bytes 131072 | tf_op jit(solution)/shard_map/slice | solution.py:232
  42.4 7.7 %copy-start.3 = (s32[64,2]{0,1:T(2,128)S(1)}, s32[64,2]{0,1:T(2,128)}, u32[]{:S(2)}) copy-start(s32[64,2]{0,1:T(2,128)} %param.9) | copy-start | bytes 1540
  42.4 7.7 %copy-start.4 = (s32[64]{0:T(128)S(1)}, s32[64]{0:T(128)}, u32[]{:S(2)}) copy-start(s32[64]{0:T(128)} %constant.30.clone) | copy-start | bytes 772
  42.4 7.7 %copy-start.5 = (s32[64]{0:T(128)S(1)}, s32[64]{0:T(128)}, u32[]{:S(2)}) copy-start(s32[64]{0:T(128)} %constant.29.clone) | copy-start | bytes 772
  42.8 10.1 %collective-permute-start.1 = (f32[424,128]{1,0:T(8,128)S(1)}, f32[424,128]{1,0:T(8,128)S(1)}, u32[]{:S(2)}, u32[]{:S(2)}) collective-permute-start(f32[424,128]{1,0:T(8,128)S(1)} %pad_bitcast_fusion), channel_id=1, source_target_pairs={{4,0},{5,1},{6,2},{7,3},{8,4},{9,5},{10,6},{11,7},{12,8},{13,9},{1... | collective-permute-start | bytes 651272 | tf_op jit(solution)/shard_map/ppermute | solution.py:259
  48.0 10.3 %collective-permute-start = (f32[424,128]{1,0:T(8,128)S(1)}, f32[424,128]{1,0:T(8,128)S(1)}, u32[]{:S(2)}, u32[]{:S(2)}) collective-permute-start(f32[424,128]{1,0:T(8,128)S(1)} %pad_bitcast_fusion.1), channel_id=1, source_target_pairs={{0,4},{1,5},{2,6},{3,7},{4,8},{5,9},{6,10},{7,11},{8,12},{9,13},{1... | collective-permute-start | bytes 651272 | tf_op jit(solution)/shard_map/ppermute | solution.py:258
  70.2 4.1 %copy-start = (f32[64,16,128]{2,1,0:T(8,128)}, f32[64,16,128]{2,1,0:T(8,128)S(1)}, u32[]{:S(2)}) copy-start(f32[64,16,128]{2,1,0:T(8,128)S(1)} %get-tuple-element.69) | copy-start | bytes 1572868
  76.8 1.8 %copy-start.2 = (pred[64]{0:T(512)(128)(4,1)S(1)}, pred[64]{0:T(512)(128)(4,1)}, u32[]{:S(2)}) copy-start(pred[64]{0:T(512)(128)(4,1)} %get-tuple-element.174) | copy-start | bytes 196

commit v13 on v12

--- a/solution.py
+++ b/solution.py
@@ -230,7 +230,9 @@
     core_main = got[:, :main_rows].reshape(frames_all, h, lanes)
     wt = got[:, main_rows : main_rows + w_rows].reshape(cycle, h, w)
     core_rest = got[:, main_rows + w_rows : used].reshape(n, rest_rows * lanes)[:, :rest_len]
-    core = jnp.concatenate([core_main, core_rest.reshape(frames_all, h, spare)], axis=2)
+    core = lax.optimization_barrier(
+        jnp.concatenate([core_main, core_rest.reshape(frames_all, h, spare)], axis=2)
+    )
 
     bands = lax.axis_size("rows")
     down, up = [], []

time: 117 us -> 117 us (level)
  no operation moved by 1% of the time
where the time goes in v13:
time: 117 us; the launch traced here: 116 us
  Pallas kernels  66.4 us (57%)
  other arithmetic  21.5 us (18%)
  local copies, waits for them, and re-layouts  14 us (12%)
  starting transfers between devices  7.04 us (6%)
  waiting for transfers between devices  5.61 us (5%)
  between operations  1.85 us (2%)
    pallas_call x1, Pallas kernels, exchange(): pl.pallas_call(functools.partial(exchange_kernel, n), out_shape=jax.Shape...  33.4 us
    pallas_call x1, Pallas kernels, return_exchange(): pl.pallas_call(functools.partial(return_kernel, n, b), out_shape=(jax.Sha...  33 us
    reduce_sum x4, other arithmetic, tile_compute(): jnp.sum(error * rt[:, HALO + dy:HALO + dy + h, HALO + dx:HALO + dx + w],...  17.7 us
    ppermute x1, waiting for transfers between devices, on_device(): lax.ppermute(dense(core[:, h - HALO:]), ('rows', 'tm'), down)  5.15 us
    ppermute x1, starting transfers between devices, on_device(): below = undense(lax.ppermute(dense(core[:, :HALO]), ('rows', 'tm'), up))  4.94 us
    unnamed x107, local copies, waits for them, and re-layouts  4.09 us
  transfers between devices with their start and end apart: 2, of which 2 were waited for; matrix products, arithmetic and copies ran while one was open for 2% of the time, Pallas kernels for 0%

profile of v13, /device:TPU:1, one launch (start us, length us, event | category | flops | bytes accessed | tf_op | source)
XLA Modules:
  0.0 116.4 jit_solution(5100202887903794616)
XLA Ops:
  0.6 1.5 %pad_slice_fusion = (f32[4,16,12]{2,1,0:T(8,128)S(1)}, f32[4,16,12]{2,1,0:T(8,128)S(1)}, f32[4,16,12]{2,1,0:T(8,128)S(1)}, f32[4,16,12]{2,1,0:T(8,128)S(1)}, f32...) fusion(f32[4,64,512]{2,1,0:T(8,128)} %param.7), kind=kLoop, calls=%fused_computation.6 | loop fusion | bytes 966656 | tf_op jit(solution)/shard_map/slice | solution.py:209
  2.1 1.4 %fusion.6 = (f32[4,16,128]{2,1,0:T(8,128)S(1)}, f32[4,16,128]{2,1,0:T(8,128)S(1)}, f32[4,16,128]{2,1,0:T(8,128)S(1)}, f32[4,16,128]{2,1,0:T(8,128)S(1)}, f32[4,1...) fusion(f32[4,64,512]{2,1,0:T(8,128)} %param.7), kind=kLoop, calls=%fused_computation.323 | loop fusion | bytes 1441792 | tf_op jit(solution)/shard_map/slice | solution.py:207
  5.2 0.2 reshape.124
  5.9 1.1 maximum_maximum_fusion.x_ref
  7.1 33.4 %exchange_0.1 = f32[16,136,128]{2,1,0:T(8,128)} custom-call(f32[16,136,128]{2,1,0:T(8,128)} %maximum_maximum_fusion.x_ref), custom_call_target="tpu_custom_call" | custom-call | tf_op jit(solution)/shard_map/exchange_0/pallas_call | solution.py:112
  40.5 1.3 %fusion.4 = (f32[16,64,128]{2,1,0:T(8,128)S(1)}, f32[16,64,128]{2,1,0:T(8,128)S(1)}) fusion(f32[16,136,128]{2,1,0:T(8,128)} %exchange_0.1), kind=kLoop, calls=%fused_computation.321 | loop fusion | bytes 2097152 | tf_op jit(solution)/shard_map/slice | solution.py:230
  41.9 0.5 reshape_reshape.3
  42.6 0.2 reshape.131
  42.9 4.9 %collective-permute-start.1 = (f32[424,128]{1,0:T(8,128)S(1)}, f32[424,128]{1,0:T(8,128)S(1)}, u32[]{:S(2)}, u32[]{:S(2)}) collective-permute-start(f32[424,128]{1,0:T(8,128)S(1)} %pad_bitcast_fusion), channel_id=1, source_target_pairs={{4,0},{5,1},{6,2},{7,3},{8,4},{9,5},{10,6},{11,7},{12,8},{13,9},{1... | collective-permute-start | bytes 651272 | tf_op jit(solution)/shard_map/ppermute | solution.py:261
  47.9 0.2 reshape.128
  48.1 2.1 %collective-permute-start = (f32[424,128]{1,0:T(8,128)S(1)}, f32[424,128]{1,0:T(8,128)S(1)}, u32[]{:S(2)}, u32[]{:S(2)}) collective-permute-start(f32[424,128]{1,0:T(8,128)S(1)} %pad_bitcast_fusion.1), channel_id=1, source_target_pairs={{0,4},{1,5},{2,6},{3,7},{4,8},{5,9},{6,10},{7,11},{8,12},{9,13},{1... | collective-permute-start | bytes 651272 | tf_op jit(solution)/shard_map/ppermute | solution.py:260
  50.3 0.2 select_reduce_fusion
  50.5 0.5 compare_and_fusion.1
  51.0 0.6 gather_fusion
  51.7 0.1 broadcast_select_fusion
  51.9 0.7 slice_bitcast_fusion.61
  52.5 0.5 collective-permute-done.1
  53.0 0.3 reshape.133
  53.3 5.2 %collective-permute-done = f32[424,128]{1,0:T(8,128)S(1)} collective-permute-done((f32[424,128]{1,0:T(8,128)S(1)}, f32[424,128]{1,0:T(8,128)S(1)}, u32[]{:S(2)}, u32[]{:S(2)}) %collective-permute-start) | collective-permute-done | bytes 217120 | tf_op jit(solution)/shard_map/ppermute | solution.py:260
  58.5 0.3 reshape.130
  58.8 0.4 pad_maximum_fusion
  59.2 11.1 %multiply_reduce_fusion.1 = (f32[16,128]{1,0:T(8,128)S(1)}, f32[16,128]{1,0:T(8,128)S(1)}, f32[16,128]{1,0:T(8,128)S(1)}, f32[16,128]{1,0:T(8,128)S(1)}, f32[16,...) fusion(f32[64,28,140]{2,1,0:T(8,128)S(1)} %pad_maximum_fusion, ...), kind=kLoop, calls=%fused_computation.17 | loop fusion | flops 21458944 | bytes 35274752 | tf_op jit(solution)/shard_map/reduce_sum | solution.py:67
  70.3 1.4 %multiply_reduce_fusion.55 = (f32[16,128]{1,0:T(8,128)S(1)}, f32[16,128]{1,0:T(8,128)S(1)}, f32[16,128]{1,0:T(8,128)S(1)}, f32[16,128]{1,0:T(8,128)S(1)}, f32[16...) fusion(f32[64,16,128]{2,1,0:T(8,128)S(1)} %get-tuple-element.69, ...), kind=kLoop, calls=%fused_computation.71 | loop fusion | flops 2600960 | bytes 5849088 | tf_op jit(solution)/shard_map/reduce_sum | solution.py:67
  71.7 2.6 %multiply_reduce_fusion.37 = (f32[16,128]{1,0:T(8,128)S(1)}, f32[16,128]{1,0:T(8,128)S(1)}, f32[16,128]{1,0:T(8,128)S(1)}, f32[16,128]{1,0:T(8,128)S(1)}, f32[16...) fusion(f32[64,16,128]{2,1,0:T(8,128)S(1)} %get-tuple-element.69, ...), kind=kLoop, calls=%fused_computation.53 | loop fusion | flops 4681728 | bytes 10108928 | tf_op jit(solution)/shard_map/reduce_sum | solution.py:67
  74.4 2.5 %multiply_reduce_fusion.19 = (f32[16,128]{1,0:T(8,128)S(1)}, f32[16,128]{1,0:T(8,128)S(1)}, f32[16,128]{1,0:T(8,128)S(1)}, f32[16,128]{1,0:T(8,128)S(1)}, f32[16...) fusion(f32[64,16,128]{2,1,0:T(8,128)S(1)} %get-tuple-element.69, ...), kind=kLoop, calls=%fused_computation.35 | loop fusion | flops 4681728 | bytes 10108928 | tf_op jit(solution)/shard_map/reduce_sum | solution.py:67
  76.9 0.2 multiply_reduce_fusion
  77.2 0.2 fusion.3
  78.1 0.6 gather_fusion.1
  78.7 0.9 fusion
  79.7 33.0 %exchange_1.1 = (f32[4,64,512]{2,1,0:T(8,128)}, f32[4,64,512]{2,1,0:T(8,128)}) custom-call(f32[16,4,16,128]{3,2,1,0:T(8,128)} %bitcast.324, f32[16,4,16,128]{3,2,1,0:T(8,128)} %bitcast.321), custom_call_target="tpu_custom_call" | custom-call | tf_op jit(solution)/shard_map/exchange_1/pallas_call | solution.py:169
  112.6 1.9 %copy.105 = f32[4,64,512]{2,1,0:T(8,128)} copy(f32[4,64,512]{2,1,0:T(8,128)} %get-tuple-element.178) | data formatting | bytes 1048576
  114.5 1.9 %copy.106 = f32[4,64,512]{2,1,0:T(8,128)} copy(f32[4,64,512]{2,1,0:T(8,128)} %get-tuple-element.179) | data formatting | bytes 1048576
  (140 shorter events, 2.3 us)
Async XLA Ops:
  0.6 4.6 %copy-start.1 = (f32[4,64,512]{2,1,0:T(8,128)S(1)}, f32[4,64,512]{2,1,0:T(8,128)}, u32[]{:S(2)}) copy-start(f32[4,64,512]{2,1,0:T(8,128)} %param.8) | copy-start | bytes 1572868
  40.5 1.4 %slice-start = ((f32[16,136,128]{2,1,0:T(8,128)}), f32[16,6,128]{2,1,0:T(8,128)S(1)}, s32[]{:S(2)}) async-start(f32[16,136,128]{2,1,0:T(8,128)} %exchange_0.1), calls=%async_computation | async-start | bytes 131072 | tf_op jit(solution)/shard_map/slice | solution.py:232
  42.5 7.7 %copy-start.3 = (s32[64,2]{0,1:T(2,128)S(1)}, s32[64,2]{0,1:T(2,128)}, u32[]{:S(2)}) copy-start(s32[64,2]{0,1:T(2,128)} %param.9) | copy-start | bytes 1540
  42.5 7.7 %copy-start.4 = (s32[64]{0:T(128)S(1)}, s32[64]{0:T(128)}, u32[]{:S(2)}) copy-start(s32[64]{0:T(128)} %constant.30.clone) | copy-start | bytes 772
  42.5 7.7 %copy-start.5 = (s32[64]{0:T(128)S(1)}, s32[64]{0:T(128)}, u32[]{:S(2)}) copy-start(s32[64]{0:T(128)} %constant.29.clone) | copy-start | bytes 772
  42.9 10.1 %collective-permute-start.1 = (f32[424,128]{1,0:T(8,128)S(1)}, f32[424,128]{1,0:T(8,128)S(1)}, u32[]{:S(2)}, u32[]{:S(2)}) collective-permute-start(f32[424,128]{1,0:T(8,128)S(1)} %pad_bitcast_fusion), channel_id=1, source_target_pairs={{4,0},{5,1},{6,2},{7,3},{8,4},{9,5},{10,6},{11,7},{12,8},{13,9},{1... | collective-permute-start | bytes 651272 | tf_op jit(solution)/shard_map/ppermute | solution.py:261
  48.1 10.3 %collective-permute-start = (f32[424,128]{1,0:T(8,128)S(1)}, f32[424,128]{1,0:T(8,128)S(1)}, u32[]{:S(2)}, u32[]{:S(2)}) collective-permute-start(f32[424,128]{1,0:T(8,128)S(1)} %pad_bitcast_fusion.1), channel_id=1, source_target_pairs={{0,4},{1,5},{2,6},{3,7},{4,8},{5,9},{6,10},{7,11},{8,12},{9,13},{1... | collective-permute-start | bytes 651272 | tf_op jit(solution)/shard_map/ppermute | solution.py:260
  70.3 4.1 %copy-start = (f32[64,16,128]{2,1,0:T(8,128)}, f32[64,16,128]{2,1,0:T(8,128)S(1)}, u32[]{:S(2)}) copy-start(f32[64,16,128]{2,1,0:T(8,128)S(1)} %get-tuple-element.69) | copy-start | bytes 1572868
  76.9 1.8 %copy-start.2 = (pred[64]{0:T(512)(128)(4,1)S(1)}, pred[64]{0:T(512)(128)(4,1)}, u32[]{:S(2)}) copy-start(pred[64]{0:T(512)(128)(4,1)} %get-tuple-element.174) | copy-start | bytes 196

commit v14 on v12

--- a/solution.py
+++ b/solution.py
@@ -61,7 +61,7 @@
     for index, (dy, dx) in enumerate(points):
         window = rt[:, HALO + dy : HALO + dy + h, HALO + dx : HALO + dx + w]
         background = background + ordered_weight[index][None] * window
-    error = rt[:, HALO : HALO + h, HALO : HALO + w] - background
+    error = lax.optimization_barrier(rt[:, HALO : HALO + h, HALO : HALO + w] - background)
     grads = jnp.stack(
         [
             jnp.sum(error * rt[:, HALO + dy : HALO + dy + h, HALO + dx : HALO + dx + w], axis=0)

time: 117 us -> 118 us (level)
  other arithmetic: 21.5 us -> 23.4 us
    sub x0 -> x1, other arithmetic: none -> 10.4 us  [tile_compute(): rt[:, HALO:HALO + h, HALO:HALO + w] - background]
    reduce_sum x4, other arithmetic: 17.7 us -> 9.19 us  [tile_compute(): jnp.sum(error * rt[:, HALO + dy:HALO + dy + h, HALO + dx:HALO + dx + w],...]
where the time goes in v14:
time: 118 us
  Pallas kernels  66.4 us (56%)
  other arithmetic  23.4 us (20%)
  local copies, waits for them, and re-layouts  13.9 us (12%)
  starting transfers between devices  7.04 us (6%)
  waiting for transfers between devices  5.61 us (5%)
  between operations  1.85 us (2%)
    pallas_call x1, Pallas kernels, exchange(): pl.pallas_call(functools.partial(exchange_kernel, n), out_shape=jax.Shape...  33.4 us
    pallas_call x1, Pallas kernels, return_exchange(): pl.pallas_call(functools.partial(return_kernel, n, b), out_shape=(jax.Sha...  33 us
    sub x1, other arithmetic, tile_compute(): rt[:, HALO:HALO + h, HALO:HALO + w] - background  10.4 us
    reduce_sum x4, other arithmetic, tile_compute(): jnp.sum(error * rt[:, HALO + dy:HALO + dy + h, HALO + dx:HALO + dx + w],...  9.19 us
    ppermute x1, waiting for transfers between devices, on_device(): lax.ppermute(dense(core[:, h - HALO:]), ('rows', 'tm'), down)  5.15 us
    ppermute x1, starting transfers between devices, on_device(): below = undense(lax.ppermute(dense(core[:, :HALO]), ('rows', 'tm'), up))  4.94 us
    unnamed x107, local copies, waits for them, and re-layouts  4.09 us
  transfers between devices with their start and end apart: 2, of which 2 were waited for; matrix products, arithmetic and copies ran while one was open for 2% of the time, Pallas kernels for 0%

profile of v14, /device:TPU:1, one launch (start us, length us, event | category | flops | bytes accessed | tf_op | source)
XLA Modules:
  0.0 118.1 jit_solution(5272753142854490637)
XLA Ops:
  0.6 1.5 %pad_slice_fusion.2 = (f32[4,16,12]{2,1,0:T(8,128)S(1)}, f32[4,16,12]{2,1,0:T(8,128)S(1)}, f32[4,16,12]{2,1,0:T(8,128)S(1)}, f32[4,16,12]{2,1,0:T(8,128)S(1)}, f...) fusion(f32[4,64,512]{2,1,0:T(8,128)} %param.7), kind=kLoop, calls=%fused_computation.7 | loop fusion | bytes 966656 | tf_op jit(solution)/shard_map/slice | solution.py:209
  2.1 1.4 %fusion.6 = (f32[4,16,128]{2,1,0:T(8,128)S(1)}, f32[4,16,128]{2,1,0:T(8,128)S(1)}, f32[4,16,128]{2,1,0:T(8,128)S(1)}, f32[4,16,128]{2,1,0:T(8,128)S(1)}, f32[4,1...) fusion(f32[4,64,512]{2,1,0:T(8,128)} %param.7), kind=kLoop, calls=%fused_computation.325 | loop fusion | bytes 1441792 | tf_op jit(solution)/shard_map/slice | solution.py:207
  5.2 0.2 reshape.124
  5.9 1.1 maximum_maximum_fusion.x_ref
  7.1 33.4 %exchange_0.1 = f32[16,136,128]{2,1,0:T(8,128)} custom-call(f32[16,136,128]{2,1,0:T(8,128)} %maximum_maximum_fusion.x_ref), custom_call_target="tpu_custom_call" | custom-call | tf_op jit(solution)/shard_map/exchange_0/pallas_call | solution.py:112
  40.5 1.3 %fusion.5 = (f32[16,64,128]{2,1,0:T(8,128)S(1)}, f32[16,64,128]{2,1,0:T(8,128)S(1)}) fusion(f32[16,136,128]{2,1,0:T(8,128)} %exchange_0.1), kind=kLoop, calls=%fused_computation.324 | loop fusion | bytes 2097152 | tf_op jit(solution)/shard_map/slice | solution.py:230
  41.9 0.5 reshape_reshape.3
  42.5 0.2 reshape.131
  42.8 4.9 %collective-permute-start.1 = (f32[424,128]{1,0:T(8,128)S(1)}, f32[424,128]{1,0:T(8,128)S(1)}, u32[]{:S(2)}, u32[]{:S(2)}) collective-permute-start(f32[424,128]{1,0:T(8,128)S(1)} %pad_bitcast_fusion), channel_id=1, source_target_pairs={{4,0},{5,1},{6,2},{7,3},{8,4},{9,5},{10,6},{11,7},{12,8},{13,9},{1... | collective-permute-start | bytes 651272 | tf_op jit(solution)/shard_map/ppermute | solution.py:259
  47.8 0.2 reshape.128
  48.0 2.1 %collective-permute-start = (f32[424,128]{1,0:T(8,128)S(1)}, f32[424,128]{1,0:T(8,128)S(1)}, u32[]{:S(2)}, u32[]{:S(2)}) collective-permute-start(f32[424,128]{1,0:T(8,128)S(1)} %pad_bitcast_fusion.1), channel_id=1, source_target_pairs={{0,4},{1,5},{2,6},{3,7},{4,8},{5,9},{6,10},{7,11},{8,12},{9,13},{1... | collective-permute-start | bytes 651272 | tf_op jit(solution)/shard_map/ppermute | solution.py:258
  50.2 0.2 select_reduce_fusion
  50.4 0.5 compare_and_fusion.1
  50.9 0.6 gather_fusion
  51.8 0.7 slice_bitcast_fusion.61
  52.4 0.5 collective-permute-done.1
  52.9 0.3 reshape.133
  53.2 5.2 %collective-permute-done = f32[424,128]{1,0:T(8,128)S(1)} collective-permute-done((f32[424,128]{1,0:T(8,128)S(1)}, f32[424,128]{1,0:T(8,128)S(1)}, u32[]{:S(2)}, u32[]{:S(2)}) %collective-permute-start) | collective-permute-done | bytes 217120 | tf_op jit(solution)/shard_map/ppermute | solution.py:258
  58.4 0.3 reshape.130
  58.7 0.3 pad_maximum_fusion
  59.1 10.4 %slice_subtract_fusion = f32[64,16,128]{2,1,0:T(8,128)S(1)} fusion(f32[64,28,140]{2,1,0:T(8,128)S(1)} %pad_maximum_fusion, f32[16,128]{1,0:T(8,128)S(1)} %get-tuple-element.74, f32[16,128]{1,0:T(8,128)S(1)} %get-tuple-element.75, f32[16,128]{1,0:T(8,128)S(1)} %get-tuple-element.76, f32[16,128]{1,0:T(8,128)S(1)} %get-tuple-element.77, ...), kind=kLoop, calls=%fused_computation.16 | loop fusion | flops 16777216 | bytes 35127296 | tf_op jit(solution)/shard_map/sub | solution.py:64
  69.4 1.4 %multiply_reduce_fusion.55 = (f32[16,128]{1,0:T(8,128)S(1)}, f32[16,128]{1,0:T(8,128)S(1)}, f32[16,128]{1,0:T(8,128)S(1)}, f32[16,128]{1,0:T(8,128)S(1)}, f32[16...) fusion(f32[64,16,128]{2,1,0:T(8,128)S(1)} %slice_subtract_fusio, ...), kind=kLoop, calls=%fused_computation.74 | loop fusion | flops 2600960 | bytes 5849088 | tf_op jit(solution)/shard_map/reduce_sum | solution.py:67
  70.9 2.6 %multiply_reduce_fusion.37 = (f32[16,128]{1,0:T(8,128)S(1)}, f32[16,128]{1,0:T(8,128)S(1)}, f32[16,128]{1,0:T(8,128)S(1)}, f32[16,128]{1,0:T(8,128)S(1)}, f32[16...) fusion(f32[64,16,128]{2,1,0:T(8,128)S(1)} %slice_subtract_fusio, ...), kind=kLoop, calls=%fused_computation.56 | loop fusion | flops 4681728 | bytes 10108928 | tf_op jit(solution)/shard_map/reduce_sum | solution.py:67
  73.5 2.5 %multiply_reduce_fusion.19 = (f32[16,128]{1,0:T(8,128)S(1)}, f32[16,128]{1,0:T(8,128)S(1)}, f32[16,128]{1,0:T(8,128)S(1)}, f32[16,128]{1,0:T(8,128)S(1)}, f32[16...) fusion(f32[64,16,128]{2,1,0:T(8,128)S(1)} %slice_subtract_fusio, ...), kind=kLoop, calls=%fused_computation.38 | loop fusion | flops 4681728 | bytes 10108928 | tf_op jit(solution)/shard_map/reduce_sum | solution.py:67
  76.0 2.6 %multiply_reduce_fusion.1 = (f32[16,128]{1,0:T(8,128)S(1)}, f32[16,128]{1,0:T(8,128)S(1)}, f32[16,128]{1,0:T(8,128)S(1)}, f32[16,128]{1,0:T(8,128)S(1)}, f32[16,...) fusion(f32[64,16,128]{2,1,0:T(8,128)S(1)} %slice_subtract_fusio, ...), kind=kLoop, calls=%fused_computation.20 | loop fusion | flops 4681728 | bytes 10108928 | tf_op jit(solution)/shard_map/reduce_sum | solution.py:67
  78.7 0.2 multiply_reduce_fusion
  78.9 0.2 fusion.4
  79.8 0.6 gather_fusion.1
  80.5 0.9 fusion.1
  81.4 33.0 %exchange_1.1 = (f32[4,64,512]{2,1,0:T(8,128)}, f32[4,64,512]{2,1,0:T(8,128)}) custom-call(f32[16,4,16,128]{3,2,1,0:T(8,128)} %bitcast.326, f32[16,4,16,128]{3,2,1,0:T(8,128)} %bitcast.321), custom_call_target="tpu_custom_call" | custom-call | tf_op jit(solution)/shard_map/exchange_1/pallas_call | solution.py:169
  114.4 1.9 %copy.105 = f32[4,64,512]{2,1,0:T(8,128)} copy(f32[4,64,512]{2,1,0:T(8,128)} %get-tuple-element.177) | data formatting | bytes 1048576
  116.2 1.9 %copy.106 = f32[4,64,512]{2,1,0:T(8,128)} copy(f32[4,64,512]{2,1,0:T(8,128)} %get-tuple-element.178) | data formatting | bytes 1048576
  (140 shorter events, 2.4 us)
Async XLA Ops:
  0.6 4.6 %copy-start.1 = (f32[4,64,512]{2,1,0:T(8,128)S(1)}, f32[4,64,512]{2,1,0:T(8,128)}, u32[]{:S(2)}) copy-start(f32[4,64,512]{2,1,0:T(8,128)} %param.8) | copy-start | bytes 1572868
  40.5 1.4 %slice-start = ((f32[16,136,128]{2,1,0:T(8,128)}), f32[16,6,128]{2,1,0:T(8,128)S(1)}, s32[]{:S(2)}) async-start(f32[16,136,128]{2,1,0:T(8,128)} %exchange_0.1), calls=%async_computation | async-start | bytes 131072 | tf_op jit(solution)/shard_map/slice | solution.py:232
  42.4 7.7 %copy-start.3 = (s32[64,2]{0,1:T(2,128)S(1)}, s32[64,2]{0,1:T(2,128)}, u32[]{:S(2)}) copy-start(s32[64,2]{0,1:T(2,128)} %param.9) | copy-start | bytes 1540
  42.4 7.7 %copy-start.4 = (s32[64]{0:T(128)S(1)}, s32[64]{0:T(128)}, u32[]{:S(2)}) copy-start(s32[64]{0:T(128)} %constant.30.clone) | copy-start | bytes 772
  42.4 7.7 %copy-start.5 = (s32[64]{0:T(128)S(1)}, s32[64]{0:T(128)}, u32[]{:S(2)}) copy-start(s32[64]{0:T(128)} %constant.29.clone) | copy-start | bytes 772
  42.8 10.1 %collective-permute-start.1 = (f32[424,128]{1,0:T(8,128)S(1)}, f32[424,128]{1,0:T(8,128)S(1)}, u32[]{:S(2)}, u32[]{:S(2)}) collective-permute-start(f32[424,128]{1,0:T(8,128)S(1)} %pad_bitcast_fusion), channel_id=1, source_target_pairs={{4,0},{5,1},{6,2},{7,3},{8,4},{9,5},{10,6},{11,7},{12,8},{13,9},{1... | collective-permute-start | bytes 651272 | tf_op jit(solution)/shard_map/ppermute | solution.py:259
  48.0 10.3 %collective-permute-start = (f32[424,128]{1,0:T(8,128)S(1)}, f32[424,128]{1,0:T(8,128)S(1)}, u32[]{:S(2)}, u32[]{:S(2)}) collective-permute-start(f32[424,128]{1,0:T(8,128)S(1)} %pad_bitcast_fusion.1), channel_id=1, source_target_pairs={{0,4},{1,5},{2,6},{3,7},{4,8},{5,9},{6,10},{7,11},{8,12},{9,13},{1... | collective-permute-start | bytes 651272 | tf_op jit(solution)/shard_map/ppermute | solution.py:258
  69.4 6.6 %copy-start = (f32[64,16,128]{2,1,0:T(8,128)}, f32[64,16,128]{2,1,0:T(8,128)S(1)}, u32[]{:S(2)}) copy-start(f32[64,16,128]{2,1,0:T(8,128)S(1)} %slice_subtract_fusion) | copy-start | bytes 1572868
  78.7 1.8 %copy-start.2 = (pred[64]{0:T(512)(128)(4,1)S(1)}, pred[64]{0:T(512)(128)(4,1)}, u32[]{:S(2)}) copy-start(pred[64]{0:T(512)(128)(4,1)} %get-tuple-element.173) | copy-start | bytes 196
